TPU v7x, 256 devices: a whole 4x4x8 slice. The times are simulated.
256 devices in a mesh: dp: 8 (over z_hi, core), expert: 32 (over x, z_lo, y).
Axes of the slice: x: 4, y: 4, z: 8 (z_hi: 4, z_lo: 2; z = z_hi * 2 + z_lo), core: 2. Of those that a mesh axis runs over, the one named last changes fastest.
Arguments:
- tokens: bfloat16 [256, 256, 1024], P(('dp', 'expert'))
- router: bfloat16 [1024, 128], replicated
- weight_in: bfloat16 [128, 1024, 2048], P('expert', None, 'dp'), may hold values from -0.1875 to 0.1875
- weight_out: bfloat16 [128, 2048, 1024], P('expert', 'dp'), may hold values from -0.125 to 0.125
- cotangent: bfloat16 [256, 256, 1024], P(('dp', 'expert')), may hold values from -6 to 6
Outputs:
- mixed: bfloat16 [256, 256, 1024], P(('dp', 'expert'))
- grad_tokens: bfloat16 [256, 256, 1024], P(('dp', 'expert'))
- grad_router: float32 [1024, 128], replicated
- grad_weight_in: bfloat16 [128, 1024, 2048], P('expert', None, 'dp')
- grad_weight_out: bfloat16 [128, 2048, 1024], P('expert', 'dp')
All inputs are finite; a program needn't handle non-finite values.
Results may differ from a plain program's by a relative error of at most 0.018.
Values may be sent and summed in bfloat16 or wider, within the bound.
A program may use at most 64 MiB of HBM per device.

v0:
```python
import jax
import jax.numpy as jnp
from jax import lax
from jax.sharding import PartitionSpec as P


def gelu_exact(values):
    return jax.nn.gelu(values, approximate=False)


def local(tokens, router, weight_in, weight_out, cotangent):
    experts_dev = weight_in.shape[0]
    width = tokens.shape[2]
    logits = jnp.einsum("isd,de->ise", tokens, router, preferred_element_type=jnp.float32)
    dispatch_prob = jax.nn.softmax(logits, axis=1)
    combine_prob = jax.nn.softmax(logits, axis=2)
    dispatch = dispatch_prob.astype(jnp.bfloat16)
    combine = combine_prob.astype(jnp.bfloat16)
    slots = jnp.einsum("ise,isd->ied", dispatch, tokens, preferred_element_type=jnp.float32).astype(
        jnp.bfloat16
    )
    grad_slots = jnp.einsum(
        "ise,isd->ied", combine, cotangent, preferred_element_type=jnp.float32
    ).astype(jnp.bfloat16)

    def to_owners(local_rows):
        arrived = lax.all_to_all(local_rows, "expert", split_axis=1, concat_axis=1, tiled=True)
        return lax.all_gather(arrived, "dp", axis=0, tiled=True)

    def from_owners(partial_value):
        summed = lax.psum_scatter(partial_value, "dp", scatter_dimension=0, tiled=True).astype(
            jnp.float32
        )
        return lax.all_to_all(
            summed.astype(jnp.bfloat16), "expert", split_axis=1, concat_axis=1, tiled=True
        )

    slot_rows = to_owners(slots)
    blocks = slot_rows.reshape(-1, experts_dev, width)
    pre_act = jnp.einsum("rkd,kdf->rkf", blocks, weight_in, preferred_element_type=jnp.float32)
    hidden = gelu_exact(pre_act).astype(jnp.bfloat16)
    partial_value = jnp.einsum(
        "rkf,kfd->rkd", hidden, weight_out, preferred_element_type=jnp.float32
    )
    blocks, pre_act, hidden, partial_value = (
        blocks,
        pre_act,
        hidden,
        partial_value.astype(jnp.bfloat16).reshape(slot_rows.shape),
    )
    expert_outs = from_owners(partial_value)
    grad_rows = to_owners(grad_slots)
    grad_blocks = grad_rows.reshape(blocks.shape)
    grad_hidden = jnp.einsum(
        "rkd,kfd->rkf", grad_blocks, weight_out, preferred_element_type=jnp.float32
    )
    _, gelu_back = jax.vjp(gelu_exact, pre_act)
    grad_pre = gelu_back(grad_hidden)[0].astype(jnp.bfloat16)
    grad_second = jnp.einsum(
        "rkf,rkd->kfd", hidden, grad_blocks, preferred_element_type=jnp.float32
    ).astype(jnp.bfloat16)
    grad_first = jnp.einsum(
        "rkd,rkf->kdf", blocks, grad_pre, preferred_element_type=jnp.float32
    ).astype(jnp.bfloat16)
    partial_back = jnp.einsum(
        "rkf,kdf->rkd", grad_pre, weight_in, preferred_element_type=jnp.float32
    )
    grad_first, grad_second, partial_back = (
        grad_first,
        grad_second,
        partial_back.astype(jnp.bfloat16).reshape(grad_rows.shape),
    )
    grad_slot_all = from_owners(partial_back)
    mixed = jnp.einsum(
        "ise,ied->isd", combine, expert_outs, preferred_element_type=jnp.float32
    ).astype(jnp.bfloat16)
    grad_comb = jnp.einsum(
        "isd,ied->ise", cotangent, expert_outs, preferred_element_type=jnp.float32
    )
    grad_disp = jnp.einsum(
        "isd,ied->ise", tokens, grad_slot_all, preferred_element_type=jnp.float32
    )
    part_disp = dispatch_prob * (
        grad_disp - jnp.sum(dispatch_prob * grad_disp, axis=1, keepdims=True)
    )
    part_comb = combine_prob * (
        grad_comb - jnp.sum(combine_prob * grad_comb, axis=2, keepdims=True)
    )
    grad_logits = (part_disp + part_comb).astype(jnp.bfloat16)
    grad_tokens = (
        jnp.einsum("ise,ied->isd", dispatch, grad_slot_all, preferred_element_type=jnp.float32)
        + jnp.einsum("ise,de->isd", grad_logits, router, preferred_element_type=jnp.float32)
    ).astype(jnp.bfloat16)
    router_term = jnp.einsum("isd,ise->de", tokens, grad_logits, preferred_element_type=jnp.float32)
    grad_router = lax.psum(router_term, ("dp", "expert"))
    return (mixed, grad_tokens, grad_router, grad_first, grad_second)


def solution(mesh):
    return jax.shard_map(
        local,
        mesh=mesh,
        in_specs=(
            P(("dp", "expert"), None, None),
            P(),
            P("expert", None, "dp"),
            P("expert", "dp", None),
            P(("dp", "expert"), None, None),
        ),
        out_specs=(
            P(("dp", "expert"), None, None),
            P(("dp", "expert"), None, None),
            P(),
            P("expert", None, "dp"),
            P("expert", "dp", None),
        ),
        check_vma=False,
    )
```

profile of v0, /device:TPU:1, one launch (start us, length us, event | category | flops | bytes accessed | tf_op | source)
XLA Modules:
  0.0 496.4 jit_solution(17294189357701382762)
XLA Ops:
  7.2 0.0 all-gather.3.cloned.1.call-start
  7.2 1.6 fusion.62
  8.8 0.2 fusion.47
  9.0 1.3 fusion.9
  10.4 0.4 copy.95
  10.8 0.5 broadcast.298
  11.3 2.1 reduce.12
  13.4 0.2 reshape.119
  13.6 17.1 %all_to_all.20 = bf16[32,2,2048]{2,1,0:T(2,128)(2,1)S(1)} all-to-all(bf16[32,2,2048]{2,1,0:T(2,128)(2,1)S(1)} %reshape.119), channel_id=1, replica_groups=mesh['dp'=8,'expert'=32] {'expert'}, dimensions={0} | all-to-all | bytes 524288 | tf_op jit(solution)/shard_map/all_to_all | solution.py:27
  30.7 0.3 reshape.120
  31.0 0.8 copy.42
  31.8 0.0 all-gather.3.cloned.1.call-update
  31.8 0.0 all-gather.5.cloned.1.call-start
  31.8 0.4 fusion.10
  32.2 0.4 copy.93
  32.6 2.2 reduce.14
  34.8 0.2 reshape.123
  35.0 11.5 %all_to_all.21 = bf16[32,2,2048]{2,1,0:T(2,128)(2,1)S(1)} all-to-all(bf16[32,2,2048]{2,1,0:T(2,128)(2,1)S(1)} %reshape.123), channel_id=1, replica_groups=mesh['dp'=8,'expert'=32] {'expert'}, dimensions={0} | all-to-all | bytes 524288 | tf_op jit(solution)/shard_map/all_to_all | solution.py:27
  46.5 0.3 reshape.124
  46.8 0.8 copy.47
  47.6 0.0 all-gather.5.cloned.1.call-update
  47.6 0.2 reduce-scatter.5.cloned.1.call-start
  47.8 20.7 %all-gather.3.cloned.1.call-done = bf16[8,128,1024]{2,1,0:T(8,128)(2,1)} async-done(((bf16[1,128,1024]{2,1,0:T(8,128)(2,1)}), bf16[8,128,1024]{2,1,0:T(8,128)(2,1)}) %all-gather.3.cloned.1.call-update) | async-done | bytes 2097168 | tf_op jit(solution)/shard_map/all_gather | solution.py:28
  68.5 4.1 reshape.112
  72.6 4.3 copy.53
  76.9 5.3 %fusion.13 = (bf16[256,4,256]{2,0,1:T(8,128)(2,1)S(1)}, f32[4,256,256]{2,1,0:T(8,128)}) fusion(bf16[256,4,1024]{0,2,1:T(8,128)(2,1)} %copy.53, bf16[4,1024,256]{2,1,0:T(8,128)(2,1)S(1)} %copy-done), kind=kOutput, calls=%fused_computation.29 | convolution fusion | flops 553910272 | bytes 5767168 | tf_op jit(solution)/shard_map/rkd,kdf->rkf/dot_general | solution.py:40
  82.2 22.7 %all-gather.5.cloned.1.call-done = bf16[8,128,1024]{2,1,0:T(8,128)(2,1)} async-done(((bf16[1,128,1024]{2,1,0:T(8,128)(2,1)}), bf16[8,128,1024]{2,1,0:T(8,128)(2,1)}) %all-gather.5.cloned.1.call-update) | async-done | bytes 2097168 | tf_op jit(solution)/shard_map/all_gather | solution.py:28
  104.9 4.1 reshape.116
  109.1 5.7 %fusion.19 = bf16[256,4,256]{2,0,1:T(8,128)(2,1)S(1)} fusion(bf16[4,256,1024]{2,1,0:T(8,128)(2,1)} %param.8, bf16[256,4,1024]{2,1,0:T(4,128)(2,1)} %reshape.116, f32[4,256,256]{2,1,0:T(8,128)} %get-tuple-element.33), kind=kOutput, calls=%fused_computation.35 | convolution fusion | flops 555745280 | bytes 5767168 | tf_op jit(solution)/shard_map/rkd,kfd->rkf/dot_general | solution.py:54
  114.8 0.7 convert_bitcast_fusion
  115.5 2.9 copy.49
  118.5 4.0 reshape.117
  122.5 0.0 reduce-scatter.5.cloned.1.call-update
  122.5 0.3 reduce-scatter.3.cloned.1.call-start
  122.7 2.3 convert_bitcast_fusion.1
  125.1 2.9 copy.44
  128.0 3.9 reshape.113
  132.0 0.0 reduce-scatter.3.cloned.1.call-update
  132.0 30.0 %reduce-scatter.5.cloned.1.call-done = bf16[1,128,1024]{2,1,0:T(8,128)(2,1)} async-done(((bf16[8,128,1024]{2,1,0:T(8,128)(2,1)}), bf16[1,128,1024]{2,1,0:T(8,128)(2,1)}) %reduce-scatter.5.cloned.1.call-update) | async-done | bytes 262160 | tf_op jit(solution)/shard_map/reduce_scatter | solution.py:31
  162.0 2.1 copy.92
  164.2 3.1 reduce.15
  167.3 0.9 reshape.125
  168.2 7.4 %all-to-all-start.3 = ((bf16[32,2,2048]{2,1,0:T(2,128)(2,1)}), bf16[32,2,2048]{2,1,0:T(2,128)(2,1)S(1)}, u32[]{:S(2)}, u32[]{:S(2)}) async-start(bf16[32,2,2048]{2,1,0:T(2,128)(2,1)} %reshape.125), calls=%async_computation.5 | async-start | bytes 524288 | tf_op jit(solution)/shard_map/all_to_all | solution.py:34
  175.6 4.5 convolution_convert_fusion
  180.1 26.2 %reduce-scatter.3.cloned.1.call-done = bf16[1,128,1024]{2,1,0:T(8,128)(2,1)} async-done(((bf16[8,128,1024]{2,1,0:T(8,128)(2,1)}), bf16[1,128,1024]{2,1,0:T(8,128)(2,1)}) %reduce-scatter.3.cloned.1.call-update) | async-done | bytes 262160 | tf_op jit(solution)/shard_map/reduce_scatter | solution.py:31
  206.3 1.4 copy.94
  207.7 2.9 reduce.13
  210.5 1.8 reshape.121
  212.4 10.0 %all-to-all-start.1 = ((bf16[32,2,2048]{2,1,0:T(2,128)(2,1)}), bf16[32,2,2048]{2,1,0:T(2,128)(2,1)}, u32[]{:S(2)}, u32[]{:S(2)}) async-start(bf16[32,2,2048]{2,1,0:T(2,128)(2,1)} %reshape.121), calls=%async_computation.2 | async-start | bytes 524288 | tf_op jit(solution)/shard_map/all_to_all | solution.py:34
  222.3 0.3 all-reduce.2.cloned.1.call-start
  222.7 3.6 convolution_convert_fusion.1
  226.3 1.0 reshape.126
  227.2 1.4 fusion.42
  228.6 1.7 all-to-all-done.1
  230.3 2.8 reshape.122
  233.1 1.6 convolution_bitcast_fusion.1
  234.7 1.6 multiply_reduce_fusion.1
  236.4 0.6 copy-done.5
  237.0 1.2 convolution_bitcast_fusion
  238.2 0.0 all-reduce.2.cloned.1.call-update
  238.2 2.2 fusion.7
  240.4 2.2 fusion.8
  242.6 245.2 %all-reduce.2.cloned.1.call-done = f32[1024,128]{0,1:T(8,128)} async-done(((f32[1024,128]{0,1:T(8,128)}), f32[1024,128]{0,1:T(8,128)}) %all-reduce.2.cloned.1.call-update) | async-done | bytes 524304 | tf_op jit(solution)/shard_map/psum | solution.py:95
  487.8 2.0 copy.56
  (16 shorter events, 0.0 us)
Async XLA Ops:
  7.2 69.7 %copy-start = (bf16[4,1024,256]{2,1,0:T(8,128)(2,1)S(1)}, bf16[4,1024,256]{2,1,0:T(8,128)(2,1)}, u32[]{:S(2)}) copy-start(bf16[4,1024,256]{2,1,0:T(8,128)(2,1)} %param.7) | copy-start | bytes 6291460
  7.2 61.3 %all-gather.3.cloned.1.call-start = ((), (), s32[]{:S(2)}) async-start(), calls=%async_computation.6 | async-start | bytes 2359296 | tf_op jit(solution)/shard_map/all_gather | solution.py:28
  10.3 21.5 %copy-start.1 = (bf16[1,256,1024]{2,1,0:T(8,128)(2,1)S(1)}, bf16[1,256,1024]{2,1,0:T(8,128)(2,1)}, u32[]{:S(2)}) copy-start(bf16[1,256,1024]{2,1,0:T(8,128)(2,1)} %param.9) | copy-start | bytes 1572868
  31.8 73.2 %all-gather.5.cloned.1.call-start = ((), (), s32[]{:S(2)}) async-start(), calls=%async_computation.8 | async-start | bytes 2359296 | tf_op jit(solution)/shard_map/all_gather | solution.py:28
  47.6 114.4 %reduce-scatter.5.cloned.1.call-start = ((), (), s32[]{:S(2)}) async-start(), calls=%async_computation.9 | async-start | bytes 2359296 | tf_op jit(solution)/shard_map/reduce_scatter | solution.py:31
  122.5 83.8 %reduce-scatter.3.cloned.1.call-start = ((), (), s32[]{:S(2)}) async-start(), calls=%async_computation.7 | async-start | bytes 2359296 | tf_op jit(solution)/shard_map/reduce_scatter | solution.py:31
  168.2 44.2 %all-to-all-start.3 = ((bf16[32,2,2048]{2,1,0:T(2,128)(2,1)}), bf16[32,2,2048]{2,1,0:T(2,128)(2,1)S(1)}, u32[]{:S(2)}, u32[]{:S(2)}) async-start(bf16[32,2,2048]{2,1,0:T(2,128)(2,1)} %reshape.125), calls=%async_computation.5 | async-start | bytes 524288 | tf_op jit(solution)/shard_map/all_to_all | solution.py:34
  212.4 18.0 %all-to-all-start.1 = ((bf16[32,2,2048]{2,1,0:T(2,128)(2,1)}), bf16[32,2,2048]{2,1,0:T(2,128)(2,1)}, u32[]{:S(2)}, u32[]{:S(2)}) async-start(bf16[32,2,2048]{2,1,0:T(2,128)(2,1)} %reshape.121), calls=%async_computation.2 | async-start | bytes 524288 | tf_op jit(solution)/shard_map/all_to_all | solution.py:34
  222.3 265.4 %all-reduce.2.cloned.1.call-start = ((), (), s32[]{:S(2)}) async-start(), calls=%async_computation.10 | async-start | bytes 1048576 | tf_op jit(solution)/shard_map/psum | solution.py:95
  233.1 3.9 copy-start.2
  234.7 1.6 copy-start.4
  234.7 5.7 %copy-start.3 = (bf16[1024,128]{1,0:T(8,128)(2,1)S(1)}, bf16[1024,128]{1,0:T(8,128)(2,1)}, u32[]{:S(2)}) copy-start(bf16[1024,128]{1,0:T(8,128)(2,1)} %param.6) | copy-start | bytes 786436
  236.3 0.7 copy-start.5
  236.3 0.7 copy-start.6
  236.3 0.6 copy-start.7
Sparse Core Ops, SparseCore 0:
  31.9 36.5 all-gather.2
  70.9 33.9 all-gather.4
  122.6 39.3 reduce-scatter.4
  165.0 41.2 reduce-scatter.2
  238.4 249.3 all-reduce.1
where the time goes:
time: 498 us; the launch traced here: 496 us
  waiting for transfers between devices  347 us (70%)
  local copies, waits for them, and re-layouts  42.7 us (9%)
  matrix products  35.6 us (7%)
  blocking collectives  28.6 us (6%)
  starting transfers between devices  18.3 us (4%)
  between operations  14 us (3%)
  other arithmetic  10.5 us (2%)
    psum x1, waiting for transfers between devices, local(): grad_router = lax.psum(router_term, ('dp', 'expert'))  245 us
    reduce_scatter x2, waiting for transfers between devices, from_owners(): lax.psum_scatter(partial_value, 'dp', scatter_dimension=0, tiled=True)  56.2 us
    all_gather x2, waiting for transfers between devices, to_owners(): return lax.all_gather(arrived, 'dp', axis=0, tiled=True)  43.4 us
    all_to_all x2, blocking collectives, to_owners(): lax.all_to_all(local_rows, 'expert', split_axis=1, concat_axis=1, tiled=T...  28.6 us
    all_to_all x2, starting transfers between devices, from_owners(): lax.all_to_all(summed.astype(jnp.bfloat16), 'expert', split_axis=1, conca...  17.4 us
    unnamed x26, local copies, waits for them, and re-layouts  10.5 us
    unnamed x4, other arithmetic  10.3 us
  transfers between devices with their start and end apart: 7, of which 6 were waited for; matrix products, arithmetic and copies ran while one was open for 11% of the time, Pallas kernels for 0%

commit v1 on v0

--- a/solution.py
+++ b/solution.py
@@ -1,3 +1,5 @@
+import functools
+
 import jax
 import jax.numpy as jnp
 from jax import lax
@@ -8,7 +10,20 @@
     return jax.nn.gelu(values, approximate=False)
 
 
-def local(tokens, router, weight_in, weight_out, cotangent):
+def all_sum(value, n_dp, n_expert):
+    rows, cols = value.shape
+    part = value.reshape(n_expert, rows // n_expert, cols)
+    part = lax.all_to_all(part, "expert", 0, 0, tiled=True).sum(0)
+    part = part.reshape(n_dp, rows // (n_expert * n_dp), cols)
+    part = lax.all_to_all(part, "dp", 0, 0, tiled=True).sum(0)
+    whole = jnp.broadcast_to(part[None], (n_dp,) + part.shape)
+    whole = lax.all_to_all(whole, "dp", 0, 0, tiled=True).reshape(rows // n_expert, cols)
+    whole = jnp.broadcast_to(whole[None], (n_expert,) + whole.shape)
+    whole = lax.all_to_all(whole, "expert", 0, 0, tiled=True)
+    return whole.reshape(rows, cols)
+
+
+def local(n_dp, n_expert, tokens, router, weight_in, weight_out, cotangent):
     experts_dev = weight_in.shape[0]
     width = tokens.shape[2]
     logits = jnp.einsum("isd,de->ise", tokens, router, preferred_element_type=jnp.float32)
@@ -92,13 +107,13 @@
         + jnp.einsum("ise,de->isd", grad_logits, router, preferred_element_type=jnp.float32)
     ).astype(jnp.bfloat16)
     router_term = jnp.einsum("isd,ise->de", tokens, grad_logits, preferred_element_type=jnp.float32)
-    grad_router = lax.psum(router_term, ("dp", "expert"))
+    grad_router = all_sum(router_term, n_dp, n_expert)
     return (mixed, grad_tokens, grad_router, grad_first, grad_second)
 
 
 def solution(mesh):
     return jax.shard_map(
-        local,
+        functools.partial(local, mesh.shape["dp"], mesh.shape["expert"]),
         mesh=mesh,
         in_specs=(
             P(("dp", "expert"), None, None),

time: 498 us -> 290 us (0.58)
  waiting for transfers between devices: 347 us -> 95.5 us
  blocking collectives: 28.6 us -> 68.6 us
  matrix products: 35.6 us -> 29.8 us
    psum x1 -> x0, waiting for transfers between devices: 245 us -> none  [local(): grad_router = lax.psum(router_term, ('dp', 'expert'))]
    all_to_all x0 -> x3, blocking collectives: none -> 39.9 us  [the longest x1 17 us: all_sum(): part = lax.all_to_all(part, 'dp', 0, 0, tiled=True).sum(0)]
    all_gather x2, waiting for transfers between devices: 43.4 us -> 35.6 us  [to_owners(): return lax.all_gather(arrived, 'dp', axis=0, tiled=True)]
    unnamed x26 -> x55, local copies, waits for them, and re-layouts: 10.5 us -> 10.9 us
  transfers between devices with their start and end apart: 7 -> 7, of which waited for: 6 -> 6; matrix products, arithmetic and copies ran while one was open for 11% -> 24% of each run, Pallas kernels for 0% -> 0%
where the time goes in v1:
time: 290 us; the launch traced here: 288 us
  waiting for transfers between devices  95.5 us (33%)
  blocking collectives  68.6 us (24%)
  local copies, waits for them, and re-layouts  44.7 us (15%)
  matrix products  29.8 us (10%)
  starting transfers between devices  22.3 us (8%)
  between operations  14.2 us (5%)
  other arithmetic  13.5 us (5%)
    reduce_scatter x2, waiting for transfers between devices, from_owners(): lax.psum_scatter(partial_value, 'dp', scatter_dimension=0, tiled=True)  55.2 us
    all_gather x2, waiting for transfers between devices, to_owners(): return lax.all_gather(arrived, 'dp', axis=0, tiled=True)  35.6 us
    all_to_all x2, blocking collectives, to_owners(): lax.all_to_all(local_rows, 'expert', split_axis=1, concat_axis=1, tiled=T...  28.6 us
    all_to_all x2, starting transfers between devices, from_owners(): lax.all_to_all(summed.astype(jnp.bfloat16), 'expert', split_axis=1, conca...  17.2 us
    all_to_all x1, blocking collectives, all_sum(): part = lax.all_to_all(part, 'dp', 0, 0, tiled=True).sum(0)  17 us
    all_to_all x1, blocking collectives, all_sum(): part = lax.all_to_all(part, 'expert', 0, 0, tiled=True).sum(0)  12.8 us
    unnamed x4, other arithmetic  11.5 us
    unnamed x55, local copies, waits for them, and re-layouts  10.9 us
  transfers between devices with their start and end apart: 7, of which 6 were waited for; matrix products, arithmetic and copies ran while one was open for 24% of the time, Pallas kernels for 0%

profile of v1, /device:TPU:1, one launch (start us, length us, event | category | flops | bytes accessed | tf_op | source)
XLA Modules:
  0.0 288.5 jit_solution(6162932482091810062)
XLA Ops:
  7.2 1.6 fusion.62
  8.9 0.2 fusion.46
  9.1 1.3 fusion.9
  10.4 0.4 copy.129
  10.8 0.6 broadcast.299
  11.4 2.2 reduce.12
  13.6 0.2 reshape.132
  13.7 17.1 %all_to_all.40 = bf16[32,2,2048]{2,1,0:T(2,128)(2,1)S(1)} all-to-all(bf16[32,2,2048]{2,1,0:T(2,128)(2,1)S(1)} %reshape.132), channel_id=1, replica_groups=mesh['dp'=8,'expert'=32] {'expert'}, dimensions={0} | all-to-all | bytes 524288 | tf_op jit(solution)/shard_map/all_to_all | solution.py:42
  30.8 0.3 reshape.133
  31.1 0.8 copy.75
  31.9 0.0 all-gather.5.cloned.1.call-start
  32.0 0.4 fusion.10
  32.4 0.4 copy.127
  32.8 2.2 reduce.14
  35.0 0.2 reshape.136
  35.1 11.5 %all_to_all.41 = bf16[32,2,2048]{2,1,0:T(2,128)(2,1)S(1)} all-to-all(bf16[32,2,2048]{2,1,0:T(2,128)(2,1)S(1)} %reshape.136), channel_id=1, replica_groups=mesh['dp'=8,'expert'=32] {'expert'}, dimensions={0} | all-to-all | bytes 524288 | tf_op jit(solution)/shard_map/all_to_all | solution.py:42
  46.7 0.3 reshape.137
  47.0 0.8 copy.80
  47.8 0.2 reduce-scatter.3.cloned.1.call-start
  48.0 20.6 %all-gather.3.cloned.1.call-done = bf16[8,128,1024]{2,1,0:T(8,128)(2,1)} async-done(((bf16[1,128,1024]{2,1,0:T(8,128)(2,1)}), bf16[8,128,1024]{2,1,0:T(8,128)(2,1)}) %all-gather.3.cloned.1.call-update) | async-done | bytes 2097168 | tf_op jit(solution)/shard_map/all_gather | solution.py:43
  68.6 4.1 %reshape.122 = bf16[256,4,1024]{2,1,0:T(4,128)(2,1)} reshape(bf16[8,128,1024]{2,1,0:T(8,128)(2,1)} %all-gather.3.cloned.1.call-done) | data formatting | bytes 4194304 | tf_op jit(solution)/shard_map/reshape | solution.py:54
  72.7 4.3 %copy.87 = bf16[256,4,1024]{0,2,1:T(8,128)(2,1)} copy(bf16[256,4,1024]{2,1,0:T(4,128)(2,1)} %reshape.122) | data formatting | bytes 4194304 | tf_op jit(solution)/shard_map/reshape | solution.py:54
  77.0 5.5 %fusion.13 = (bf16[256,4,256]{2,0,1:T(8,128)(2,1)S(1)}, f32[4,256,256]{2,1,0:T(8,128)}) fusion(bf16[256,4,1024]{0,2,1:T(8,128)(2,1)} %copy.87, bf16[4,1024,256]{2,1,0:T(8,128)(2,1)S(1)} %copy-done), kind=kOutput, calls=%fused_computation.29 | convolution fusion | flops 553910272 | bytes 5767168 | tf_op jit(solution)/shard_map/rkd,kdf->rkf/dot_general | solution.py:55
  82.4 0.7 convert_bitcast_fusion.1
  83.2 2.9 %copy.77 = bf16[256,4,1024]{2,1,0:T(4,128)(2,1)} copy(bf16[256,4,1024]{2,0,1:T(8,128)(2,1)S(1)} %convert_bitcast_fusion.1) | data formatting | bytes 4194304 | tf_op jit(solution)/shard_map/convert_element_type | solution.py:64
  86.1 3.9 %reshape.123 = bf16[8,128,1024]{2,1,0:T(8,128)(2,1)} reshape(bf16[256,4,1024]{2,1,0:T(4,128)(2,1)} %copy.77) | data formatting | bytes 4194304 | tf_op jit(solution)/shard_map/reshape | solution.py:64
  90.1 0.3 reduce-scatter.5.cloned.1.call-start
  90.4 14.9 %all-gather.5.cloned.1.call-done = bf16[8,128,1024]{2,1,0:T(8,128)(2,1)} async-done(((bf16[1,128,1024]{2,1,0:T(8,128)(2,1)}), bf16[8,128,1024]{2,1,0:T(8,128)(2,1)}) %all-gather.5.cloned.1.call-update) | async-done | bytes 2097168 | tf_op jit(solution)/shard_map/all_gather | solution.py:43
  105.3 4.1 %reshape.126 = bf16[256,4,1024]{2,1,0:T(4,128)(2,1)} reshape(bf16[8,128,1024]{2,1,0:T(8,128)(2,1)} %all-gather.5.cloned.1.call-done) | data formatting | bytes 4194304 | tf_op jit(solution)/shard_map/reshape | solution.py:68
  109.4 5.7 %fusion.19 = bf16[256,4,256]{2,0,1:T(8,128)(2,1)S(1)} fusion(bf16[4,256,1024]{2,1,0:T(8,128)(2,1)} %param.8, bf16[256,4,1024]{2,1,0:T(4,128)(2,1)} %reshape.126, f32[4,256,256]{2,1,0:T(8,128)} %get-tuple-element.13), kind=kOutput, calls=%fused_computation.35 | convolution fusion | flops 555745280 | bytes 5767168 | tf_op jit(solution)/shard_map/rkd,kfd->rkf/dot_general | solution.py:69
  115.1 0.7 convert_bitcast_fusion
  115.9 2.9 %copy.82 = bf16[256,4,1024]{2,1,0:T(4,128)(2,1)} copy(bf16[256,4,1024]{2,0,1:T(8,128)(2,1)S(1)} %convert_bitcast_fusion) | data formatting | bytes 4194304 | tf_op jit(solution)/shard_map/convert_element_type | solution.py:86
  118.9 3.9 %reshape.127 = bf16[8,128,1024]{2,1,0:T(8,128)(2,1)} reshape(bf16[256,4,1024]{2,1,0:T(4,128)(2,1)} %copy.82) | data formatting | bytes 4194304 | tf_op jit(solution)/shard_map/reshape | solution.py:86
  122.8 25.3 %reduce-scatter.3.cloned.1.call-done = bf16[1,128,1024]{2,1,0:T(8,128)(2,1)} async-done(((bf16[8,128,1024]{2,1,0:T(8,128)(2,1)}), bf16[1,128,1024]{2,1,0:T(8,128)(2,1)}) %reduce-scatter.3.cloned.1.call-update) | async-done | bytes 262160 | tf_op jit(solution)/shard_map/reduce_scatter | solution.py:46
  148.2 2.1 copy.128
  150.3 3.2 %reduce.13 = bf16[128,1024]{1,0:T(8,128)(2,1)S(1)} reduce(bf16[128,1,1024]{2,1,0:T(2,128)(2,1)} %bitcast.175, bf16[]{:T(256)} %broadcast.299), dimensions={1}, to_apply=%bitcast.166.reduce_sub_computation | reduce | bytes 524290
  153.5 0.9 reshape.134
  154.4 6.8 %all-to-all-start.1 = ((bf16[32,2,2048]{2,1,0:T(2,128)(2,1)}), bf16[32,2,2048]{2,1,0:T(2,128)(2,1)S(1)}, u32[]{:S(2)}, u32[]{:S(2)}) async-start(bf16[32,2,2048]{2,1,0:T(2,128)(2,1)} %reshape.134), calls=%async_computation.2 | async-start | bytes 524288 | tf_op jit(solution)/shard_map/all_to_all | solution.py:49
  161.2 29.9 %reduce-scatter.5.cloned.1.call-done = bf16[1,128,1024]{2,1,0:T(8,128)(2,1)} async-done(((bf16[8,128,1024]{2,1,0:T(8,128)(2,1)}), bf16[1,128,1024]{2,1,0:T(8,128)(2,1)}) %reduce-scatter.5.cloned.1.call-update) | async-done | bytes 262160 | tf_op jit(solution)/shard_map/reduce_scatter | solution.py:46
  191.0 2.1 copy.126
  193.2 3.9 %reduce.15 = bf16[128,1024]{1,0:T(8,128)(2,1)} reduce(bf16[128,1,1024]{2,1,0:T(2,128)(2,1)} %bitcast.173, bf16[]{:T(256)} %broadcast.299), dimensions={1}, to_apply=%bitcast.164.reduce_sub_computation | reduce | bytes 524290
  197.1 1.8 reshape.138
  198.9 10.4 %all-to-all-start.3 = ((bf16[32,2,2048]{2,1,0:T(2,128)(2,1)}), bf16[32,2,2048]{2,1,0:T(2,128)(2,1)}, u32[]{:S(2)}, u32[]{:S(2)}) async-start(bf16[32,2,2048]{2,1,0:T(2,128)(2,1)} %reshape.138), calls=%async_computation.5 | async-start | bytes 524288 | tf_op jit(solution)/shard_map/all_to_all | solution.py:49
  209.3 1.0 copy.73
  210.3 1.0 reshape.135
  211.2 1.5 convolution_bitcast_fusion.1
  212.8 4.2 %all-to-all-done.3 = bf16[32,2,2048]{2,1,0:T(2,128)(2,1)} async-done(((bf16[32,2,2048]{2,1,0:T(2,128)(2,1)}), bf16[32,2,2048]{2,1,0:T(2,128)(2,1)}, u32[]{:S(2)}, u32[]{:S(2)}) %all-to-all-start.3) | async-done | bytes 262176 | tf_op jit(solution)/shard_map/all_to_all | solution.py:49
  217.0 2.8 reshape.139
  219.8 1.4 multiply_reduce_fusion.1
  221.2 1.5 convolution_bitcast_fusion
  222.8 12.8 %all_to_all.42 = f32[32,32,128]{2,1,0:T(8,128)} all-to-all(f32[32,32,128]{2,1,0:T(8,128)S(1)} %convolution_bitcast_fusion), channel_id=1, replica_groups=mesh['dp'=8,'expert'=32] {'expert'}, dimensions={0} | all-to-all | bytes 1048576 | tf_op jit(solution)/shard_map/all_to_all | solution.py:16
  235.6 1.1 reduce_sum.58
  236.6 17.0 %all_to_all.43 = f32[8,4,128]{2,1,0:T(4,128)} all-to-all(f32[8,4,128]{2,1,0:T(4,128)S(1)} %bitcast.179), channel_id=1, replica_groups=mesh['dp'=8,'expert'=32] {'dp'}, dimensions={0} | all-to-all | bytes 32768 | tf_op jit(solution)/shard_map/all_to_all | solution.py:18
  253.6 0.7 reduce_sum.59
  254.4 10.2 %all_to_all.44 = f32[8,4,128]{2,1,0:T(4,128)S(1)} all-to-all(f32[8,4,128]{2,1,0:T(4,128)S(1)} %broadcast_in_dim.6), channel_id=1, replica_groups=mesh['dp'=8,'expert'=32] {'dp'}, dimensions={0} | all-to-all | bytes 32768 | tf_op jit(solution)/shard_map/all_to_all | solution.py:20
  264.5 0.9 broadcast_in_dim.8
  265.4 4.6 %all-to-all-start.7 = ((f32[32,32,128]{2,1,0:T(8,128)}), f32[32,32,128]{2,1,0:T(8,128)}, u32[]{:S(2)}, u32[]{:S(2)}) async-start(f32[32,32,128]{2,1,0:T(8,128)} %broadcast_in_dim.8), calls=%async_computation.9 | async-start | bytes 1048576 | tf_op jit(solution)/shard_map/all_to_all | solution.py:22
  270.1 3.8 %convolution_convert_fusion.1 = bf16[4,1024,256]{2,1,0:T(8,128)(2,1)} fusion(bf16[256,4,1024]{0,2,1:T(8,128)(2,1)} %copy.87, bf16[256,4,256]{2,0,1:T(8,128)(2,1)S(1)} %copy-done.4), kind=kOutput, calls=%fused_computation.3 | convolution fusion | flops 537919488 | bytes 4718592 | tf_op jit(solution)/shard_map/rkd,rkf->kdf/dot_general | solution.py:77
  273.9 2.9 %convolution_convert_fusion = bf16[4,256,1024]{2,1,0:T(8,128)(2,1)} fusion(bf16[256,4,256]{2,0,1:T(8,128)(2,1)S(1)} %get-tuple-element.12, bf16[256,4,1024]{2,1,0:T(4,128)(2,1)S(1)} %copy-done.1), kind=kOutput, calls=%fused_computation.2 | convolution fusion | flops 537919488 | bytes 4718592 | tf_op jit(solution)/shard_map/rkf,rkd->kfd/dot_general | solution.py:74
  276.8 1.2 fusion.7
  278.0 0.3 fusion.41
  278.4 1.2 fusion.8
  279.6 0.5 all-to-all-done.7
  280.1 1.9 copy.131
  (51 shorter events, 0.3 us)
Async XLA Ops:
  7.2 69.8 %copy-start = (bf16[4,1024,256]{2,1,0:T(8,128)(2,1)S(1)}, bf16[4,1024,256]{2,1,0:T(8,128)(2,1)}, u32[]{:S(2)}) copy-start(bf16[4,1024,256]{2,1,0:T(8,128)(2,1)} %param.7) | copy-start | bytes 6291460
  7.2 61.4 %all-gather.3.cloned.1.call-start = ((), (), s32[]{:S(2)}) async-start(), calls=%async_computation.10 | async-start | bytes 2359296 | tf_op jit(solution)/shard_map/all_gather | solution.py:43
  8.8 212.3 %copy-start.10 = (f32[256]{0:T(256)}, f32[256]{0:T(256)S(1)}, u32[]{:S(2)}) copy-start(f32[256]{0:T(256)S(1)} %get-tuple-element.9) | copy-start | bytes 3076
  8.8 212.3 %copy-start.14 = (f32[128]{0:T(128)}, f32[128]{0:T(128)S(1)}, u32[]{:S(2)}) copy-start(f32[128]{0:T(128)S(1)} %get-tuple-element.10) | copy-start | bytes 1540
  9.0 212.1 %copy-start.12 = (f32[256]{0:T(256)}, f32[256]{0:T(256)S(1)}, u32[]{:S(2)}) copy-start(f32[256]{0:T(256)S(1)} %get-tuple-element.7) | copy-start | bytes 3076
  9.1 212.2 %copy-start.16 = (f32[128]{0:T(128)}, f32[128]{0:T(128)S(1)}, u32[]{:S(2)}) copy-start(f32[128]{0:T(128)S(1)} %get-tuple-element.8) | copy-start | bytes 1540
  10.4 21.6 %copy-start.5 = (bf16[1,256,1024]{2,1,0:T(8,128)(2,1)S(1)}, bf16[1,256,1024]{2,1,0:T(8,128)(2,1)}, u32[]{:S(2)}) copy-start(bf16[1,256,1024]{2,1,0:T(8,128)(2,1)} %param.9) | copy-start | bytes 1572868
  31.9 73.4 %all-gather.5.cloned.1.call-start = ((), (), s32[]{:S(2)}) async-start(), calls=%async_computation.12 | async-start | bytes 2359296 | tf_op jit(solution)/shard_map/all_gather | solution.py:43
  47.8 100.4 %reduce-scatter.3.cloned.1.call-start = ((), (), s32[]{:S(2)}) async-start(), calls=%async_computation.11 | async-start | bytes 2359296 | tf_op jit(solution)/shard_map/reduce_scatter | solution.py:46
  77.0 5.5 %copy-start.7 = (bf16[4,256,1024]{2,1,0:T(8,128)(2,1)S(1)}, bf16[4,256,1024]{2,1,0:T(8,128)(2,1)}, u32[]{:S(2)}) copy-start(bf16[4,256,1024]{2,1,0:T(8,128)(2,1)} %param.8) | copy-start | bytes 6291460
  90.1 101.0 %reduce-scatter.5.cloned.1.call-start = ((), (), s32[]{:S(2)}) async-start(), calls=%async_computation.13 | async-start | bytes 2359296 | tf_op jit(solution)/shard_map/reduce_scatter | solution.py:46
  115.1 0.8 copy-start.3
  150.3 59.0 %copy-start.2 = (bf16[1,256,1024]{2,1,0:T(8,128)(2,1)S(1)}, bf16[1,256,1024]{2,1,0:T(8,128)(2,1)}, u32[]{:S(2)}) copy-start(bf16[1,256,1024]{2,1,0:T(8,128)(2,1)} %param.5) | copy-start | bytes 1572868
  154.4 44.5 %all-to-all-start.1 = ((bf16[32,2,2048]{2,1,0:T(2,128)(2,1)}), bf16[32,2,2048]{2,1,0:T(2,128)(2,1)S(1)}, u32[]{:S(2)}, u32[]{:S(2)}) async-start(bf16[32,2,2048]{2,1,0:T(2,128)(2,1)} %reshape.134), calls=%async_computation.2 | async-start | bytes 524288 | tf_op jit(solution)/shard_map/all_to_all | solution.py:49
  198.9 18.1 %all-to-all-start.3 = ((bf16[32,2,2048]{2,1,0:T(2,128)(2,1)}), bf16[32,2,2048]{2,1,0:T(2,128)(2,1)}, u32[]{:S(2)}, u32[]{:S(2)}) async-start(bf16[32,2,2048]{2,1,0:T(2,128)(2,1)} %reshape.138), calls=%async_computation.5 | async-start | bytes 524288 | tf_op jit(solution)/shard_map/all_to_all | solution.py:49
  221.2 1.6 copy-start.18
  221.2 1.6 copy-start.20
  221.2 48.8 %copy-start.4 = (bf16[256,4,256]{2,0,1:T(8,128)(2,1)S(1)}, bf16[256,4,256]{2,0,1:T(8,128)(2,1)}, u32[]{:S(2)}) copy-start(bf16[256,4,256]{2,0,1:T(8,128)(2,1)} %copy-done.3) | copy-start | bytes 1572868
  265.4 14.7 %all-to-all-start.7 = ((f32[32,32,128]{2,1,0:T(8,128)}), f32[32,32,128]{2,1,0:T(8,128)}, u32[]{:S(2)}, u32[]{:S(2)}) async-start(f32[32,32,128]{2,1,0:T(8,128)} %broadcast_in_dim.8), calls=%async_computation.9 | async-start | bytes 1048576 | tf_op jit(solution)/shard_map/all_to_all | solution.py:22
  270.0 3.8 %copy-start.1 = (bf16[256,4,1024]{2,1,0:T(4,128)(2,1)S(1)}, bf16[256,4,1024]{2,1,0:T(4,128)(2,1)}, u32[]{:S(2)}) copy-start(bf16[256,4,1024]{2,1,0:T(4,128)(2,1)} %reshape.126) | copy-start | bytes 6291460
  273.8 3.0 %copy-start.6 = (bf16[128,1,1024]{2,1,0:T(2,128)(2,1)S(1)}, bf16[128,1,1024]{2,1,0:T(2,128)(2,1)}, u32[]{:S(2)}) copy-start(bf16[128,1,1024]{2,1,0:T(2,128)(2,1)} %reshape.135) | copy-start | bytes 786436
  273.8 3.0 %copy-start.11 = (f32[256]{0:T(256)S(1)}, f32[256]{0:T(256)}, u32[]{:S(2)}) copy-start(f32[256]{0:T(256)} %copy-done.10) | copy-start | bytes 3076
  273.8 3.0 %copy-start.13 = (f32[256]{0:T(256)S(1)}, f32[256]{0:T(256)}, u32[]{:S(2)}) copy-start(f32[256]{0:T(256)} %copy-done.12) | copy-start | bytes 3076
  273.8 4.2 %copy-start.8 = (bf16[128,1,1024]{2,1,0:T(2,128)(2,1)S(1)}, bf16[128,1,1024]{2,1,0:T(2,128)(2,1)}, u32[]{:S(2)}) copy-start(bf16[128,1,1024]{2,1,0:T(2,128)(2,1)} %reshape.139) | copy-start | bytes 786436
  273.9 4.1 %copy-start.15 = (f32[128]{0:T(128)S(1)}, f32[128]{0:T(128)}, u32[]{:S(2)}) copy-start(f32[128]{0:T(128)} %copy-done.14) | copy-start | bytes 1540
  273.9 4.1 %copy-start.17 = (f32[128]{0:T(128)S(1)}, f32[128]{0:T(128)}, u32[]{:S(2)}) copy-start(f32[128]{0:T(128)} %copy-done.16) | copy-start | bytes 1540
  276.8 1.5 copy-start.9
  276.8 1.5 copy-start.19
  276.8 1.5 copy-start.21
Sparse Core Ops, SparseCore 0:
  32.0 36.5 all-gather.2
  71.0 34.2 all-gather.4
  108.4 39.6 reduce-scatter.2
  150.6 40.4 reduce-scatter.4

commit v2 on v1

--- a/solution.py
+++ b/solution.py
@@ -3,7 +3,86 @@
 import jax
 import jax.numpy as jnp
 from jax import lax
+from jax.experimental import pallas as pl
+from jax.experimental.pallas import tpu as pltpu
 from jax.sharding import PartitionSpec as P
+
+
+def _exchange_kernel(axis, other, n, gather, x_ref, o_ref, land, send_sem, recv_sem):
+    me = lax.axis_index(axis)
+    fixed = lax.axis_index(other)
+
+    def peer(j):
+        if axis == "dp":
+            return (j, fixed)
+        return (fixed, j)
+
+    barrier = pltpu.get_barrier_semaphore()
+
+    @pl.loop(0, n)
+    def _(j):
+        @pl.when(j != me)
+        def _():
+            pl.semaphore_signal(barrier, inc=1, device_id=peer(j), device_id_type=pl.DeviceIdType.MESH)
+
+    pl.semaphore_wait(barrier, n - 1)
+
+    def copy_to(j):
+        src = x_ref if gather else x_ref.at[j]
+        return pltpu.make_async_remote_copy(
+            src_ref=src,
+            dst_ref=land.at[me],
+            send_sem=send_sem.at[j],
+            recv_sem=recv_sem.at[me],
+            device_id=peer(j),
+            device_id_type=pl.DeviceIdType.MESH,
+        )
+
+    @pl.loop(0, n)
+    def _(j):
+        @pl.when(j != me)
+        def _():
+            copy_to(j).start()
+
+    own = x_ref[...] if gather else x_ref[me]
+    o_ref[me] = own
+
+    def arrived(j):
+        src = x_ref if gather else x_ref.at[j]
+        return pltpu.make_async_remote_copy(
+            src_ref=src,
+            dst_ref=land.at[j],
+            send_sem=send_sem.at[j],
+            recv_sem=recv_sem.at[j],
+            device_id=peer(j),
+            device_id_type=pl.DeviceIdType.MESH,
+        )
+
+    @pl.loop(0, n)
+    def _(j):
+        @pl.when(j != me)
+        def _():
+            arrived(j).wait_recv()
+            o_ref[j] = land[j]
+            copy_to(j).wait_send()
+
+
+def exchange(x, axis, n, collective_id, gather=False):
+    other = "expert" if axis == "dp" else "dp"
+    block = x.shape if gather else x.shape[1:]
+    out_shape = jax.ShapeDtypeStruct((n,) + tuple(block), x.dtype)
+    return pl.pallas_call(
+        functools.partial(_exchange_kernel, axis, other, n, gather),
+        out_shape=out_shape,
+        in_specs=[pl.BlockSpec(memory_space=pltpu.VMEM)],
+        out_specs=pl.BlockSpec(memory_space=pltpu.VMEM),
+        scratch_shapes=[
+            pltpu.VMEM(out_shape.shape, x.dtype),
+            pltpu.SemaphoreType.DMA((n,)),
+            pltpu.SemaphoreType.DMA((n,)),
+        ],
+        compiler_params=pltpu.CompilerParams(collective_id=collective_id, has_side_effects=True),
+    )(x)
 
 
 def gelu_exact(values):
@@ -13,13 +92,11 @@
 def all_sum(value, n_dp, n_expert):
     rows, cols = value.shape
     part = value.reshape(n_expert, rows // n_expert, cols)
-    part = lax.all_to_all(part, "expert", 0, 0, tiled=True).sum(0)
+    part = exchange(part, "expert", n_expert, 4).sum(0)
     part = part.reshape(n_dp, rows // (n_expert * n_dp), cols)
-    part = lax.all_to_all(part, "dp", 0, 0, tiled=True).sum(0)
-    whole = jnp.broadcast_to(part[None], (n_dp,) + part.shape)
-    whole = lax.all_to_all(whole, "dp", 0, 0, tiled=True).reshape(rows // n_expert, cols)
-    whole = jnp.broadcast_to(whole[None], (n_expert,) + whole.shape)
-    whole = lax.all_to_all(whole, "expert", 0, 0, tiled=True)
+    part = exchange(part, "dp", n_dp, 5).sum(0)
+    whole = exchange(part, "dp", n_dp, 6, gather=True).reshape(rows // n_expert, cols)
+    whole = exchange(whole, "expert", n_expert, 7, gather=True)
     return whole.reshape(rows, cols)
 
 
@@ -38,19 +115,17 @@
         "ise,isd->ied", combine, cotangent, preferred_element_type=jnp.float32
     ).astype(jnp.bfloat16)
 
-    def to_owners(local_rows):
-        arrived = lax.all_to_all(local_rows, "expert", split_axis=1, concat_axis=1, tiled=True)
+    def to_owners(local_rows, cid):
+        chunks = local_rows.reshape(n_expert, experts_dev, width)
+        arrived = exchange(chunks, "expert", n_expert, cid).reshape(local_rows.shape)
         return lax.all_gather(arrived, "dp", axis=0, tiled=True)
 
-    def from_owners(partial_value):
-        summed = lax.psum_scatter(partial_value, "dp", scatter_dimension=0, tiled=True).astype(
-            jnp.float32
-        )
-        return lax.all_to_all(
-            summed.astype(jnp.bfloat16), "expert", split_axis=1, concat_axis=1, tiled=True
-        )
-
-    slot_rows = to_owners(slots)
+    def from_owners(partial_value, cid):
+        summed = lax.psum_scatter(partial_value, "dp", scatter_dimension=0, tiled=True)
+        chunks = summed.reshape(n_expert, experts_dev, width)
+        return exchange(chunks, "expert", n_expert, cid).reshape(summed.shape)
+
+    slot_rows = to_owners(slots, 0)
     blocks = slot_rows.reshape(-1, experts_dev, width)
     pre_act = jnp.einsum("rkd,kdf->rkf", blocks, weight_in, preferred_element_type=jnp.float32)
     hidden = gelu_exact(pre_act).astype(jnp.bfloat16)
@@ -63,8 +138,8 @@
         hidden,
         partial_value.astype(jnp.bfloat16).reshape(slot_rows.shape),
     )
-    expert_outs = from_owners(partial_value)
-    grad_rows = to_owners(grad_slots)
+    expert_outs = from_owners(partial_value, 2)
+    grad_rows = to_owners(grad_slots, 1)
     grad_blocks = grad_rows.reshape(blocks.shape)
     grad_hidden = jnp.einsum(
         "rkd,kfd->rkf", grad_blocks, weight_out, preferred_element_type=jnp.float32
@@ -85,7 +160,7 @@
         grad_second,
         partial_back.astype(jnp.bfloat16).reshape(grad_rows.shape),
     )
-    grad_slot_all = from_owners(partial_back)
+    grad_slot_all = from_owners(partial_back, 3)
     mixed = jnp.einsum(
         "ise,ied->isd", combine, expert_outs, preferred_element_type=jnp.float32
     ).astype(jnp.bfloat16)

time: 290 us -> 273 us (0.941)
  Pallas kernels: 0 us -> 97.2 us
  blocking collectives: 68.6 us -> 0 us
  starting transfers between devices: 22.3 us -> 0.34 us
  waiting for transfers between devices: 95.5 us -> 83.5 us
  other arithmetic: 13.5 us -> 3.2 us
  local copies, waits for them, and re-layouts: 44.7 us -> 40.4 us
    pallas_call x0 -> x8, Pallas kernels: none -> 97.2 us  [exchange(): pl.pallas_call(functools.partial(_exchange_kernel, axis, other, n, gather...]
    all_to_all x5 -> x0, blocking collectives: 68.6 us -> none  [the longest x2 28.6 us: to_owners(): lax.all_to_all(local_rows, 'expert', split_axis=1, concat_axis=1, tiled=T...]
    all_to_all x3 -> x0, starting transfers between devices: 21.8 us -> none  [the longest x2 17.2 us: from_owners(): lax.all_to_all(summed.astype(jnp.bfloat16), 'expert', split_axis=1, conca...]
    reduce_scatter x2, waiting for transfers between devices: 55.2 us -> 43.3 us  [from_owners(): lax.psum_scatter(partial_value, 'dp', scatter_dimension=0, tiled=True)]
    unnamed x4 -> x0, other arithmetic: 11.5 us -> none
    reshape x0 -> x6, local copies, waits for them, and re-layouts: none -> 8.56 us  [the longest x2 3.51 us: from_owners(): chunks = summed.reshape(n_expert, experts_dev, width)]
    unnamed x55 -> x32, local copies, waits for them, and re-layouts: 10.9 us -> 3.52 us
    all_to_all x3 -> x0, waiting for transfers between devices: 4.76 us -> none  [the longest x2 4.22 us: from_owners(): lax.all_to_all(summed.astype(jnp.bfloat16), 'expert', split_axis=1, conca...]
  transfers between devices with their start and end apart: 7 -> 4, of which waited for: 6 -> 4; matrix products, arithmetic and copies ran while one was open for 24% -> 20% of each run, Pallas kernels for 0% -> 9%
where the time goes in v2:
time: 273 us; the launch traced here: 269 us
  Pallas kernels  97.2 us (36%)
  waiting for transfers between devices  83.5 us (31%)
  local copies, waits for them, and re-layouts  40.4 us (15%)
  matrix products  30.9 us (11%)
  between operations  14 us (5%)
  other arithmetic  3.2 us (1%)
    pallas_call x8, Pallas kernels, exchange(): pl.pallas_call(functools.partial(_exchange_kernel, axis, other, n, gather...  97.2 us
    reduce_scatter x2, waiting for transfers between devices, from_owners(): lax.psum_scatter(partial_value, 'dp', scatter_dimension=0, tiled=True)  43.3 us
    all_gather x2, waiting for transfers between devices, to_owners(): return lax.all_gather(arrived, 'dp', axis=0, tiled=True)  40.1 us
    reshape x2, local copies, waits for them, and re-layouts, local(): blocks = slot_rows.reshape(-1, experts_dev, width)  8.38 us
    dot_general x1, matrix products, local(): jnp.einsum('rkd,kfd->rkf', grad_blocks, weight_out, preferred_element_typ...  5.73 us
  transfers between devices with their start and end apart: 4, of which 4 were waited for; matrix products, arithmetic and copies ran while one was open for 20% of the time, Pallas kernels for 9%

profile of v2, /device:TPU:1, one launch (start us, length us, event | category | flops | bytes accessed | tf_op | source)
XLA Modules:
  0.0 269.4 jit_solution(13387242706289736616)
XLA Ops:
  7.2 0.0 copy-start
  7.2 0.0 copy-start.5
  7.2 0.0 all-gather.3.cloned.1.call-start
  7.2 1.7 fusion.52
  8.9 0.2 fusion.39
  9.1 1.3 convolution_convert_fusion.4
  10.4 0.8 reshape.149.x_ref
  11.2 13.6 %shard_map.92 = bf16[32,4,1024]{2,1,0:T(4,128)(2,1)} custom-call(bf16[32,4,1024]{2,1,0:T(4,128)(2,1)} %reshape.149.x_ref), custom_call_target="tpu_custom_call" | custom-call | tf_op jit(solution)/shard_map/pallas_call | solution.py:74
  24.8 1.7 reshape.150
  26.6 0.0 all-gather.3.cloned.1.call-update
  26.6 0.0 all-gather.5.cloned.1.call-start
  26.6 0.0 copy-done.5
  26.6 0.4 convolution_convert_fusion.3
  27.0 0.8 reshape.156.x_ref
  27.8 11.4 %shard_map.94 = bf16[32,4,1024]{2,1,0:T(4,128)(2,1)} custom-call(bf16[32,4,1024]{2,1,0:T(4,128)(2,1)} %reshape.156.x_ref), custom_call_target="tpu_custom_call" | custom-call | tf_op jit(solution)/shard_map/pallas_call | solution.py:74
  39.2 1.7 reshape.157
  41.0 0.0 all-gather.5.cloned.1.call-update
  41.0 0.0 reduce-scatter.3.cloned.1.call-start
  41.0 23.9 %all-gather.3.cloned.1.call-done = bf16[8,128,1024]{2,1,0:T(8,128)(2,1)} async-done(((bf16[1,128,1024]{2,1,0:T(8,128)(2,1)}), bf16[8,128,1024]{2,1,0:T(8,128)(2,1)}) %all-gather.3.cloned.1.call-update) | async-done | bytes 2097168 | tf_op jit(solution)/shard_map/all_gather | solution.py:121
  65.0 4.1 %reshape.151 = bf16[256,4,1024]{2,1,0:T(4,128)(2,1)} reshape(bf16[8,128,1024]{2,1,0:T(8,128)(2,1)} %all-gather.3.cloned.1.call-done) | data formatting | bytes 4194304 | tf_op jit(solution)/shard_map/reshape | solution.py:129
  69.1 4.3 %copy.32 = bf16[256,4,1024]{0,2,1:T(8,128)(2,1)} copy(bf16[256,4,1024]{2,1,0:T(4,128)(2,1)} %reshape.151) | data formatting | bytes 4194304 | tf_op jit(solution)/shard_map/reshape | solution.py:129
  73.4 5.4 %fusion.11 = (bf16[256,4,256]{2,0,1:T(8,128)(2,1)S(1)}, f32[4,256,256]{2,1,0:T(8,128)}) fusion(bf16[256,4,1024]{0,2,1:T(8,128)(2,1)} %copy.32, bf16[4,1024,256]{2,1,0:T(8,128)(2,1)S(1)} %copy-done), kind=kOutput, calls=%fused_computation.27 | convolution fusion | flops 553910272 | bytes 5767168 | tf_op jit(solution)/shard_map/rkd,kdf->rkf/dot_general | solution.py:130
  78.8 0.7 convert_bitcast_fusion.1
  79.6 2.9 %copy.27 = bf16[256,4,1024]{2,1,0:T(4,128)(2,1)} copy(bf16[256,4,1024]{2,0,1:T(8,128)(2,1)S(1)} %convert_bitcast_fusion.1) | data formatting | bytes 4194304 | tf_op jit(solution)/shard_map/convert_element_type | solution.py:139
  82.5 4.0 %reshape.152 = bf16[8,128,1024]{2,1,0:T(8,128)(2,1)} reshape(bf16[256,4,1024]{2,1,0:T(4,128)(2,1)} %copy.27) | data formatting | bytes 4194304 | tf_op jit(solution)/shard_map/reshape | solution.py:139
  86.5 0.0 reduce-scatter.3.cloned.1.call-update
  86.5 0.2 reduce-scatter.5.cloned.1.call-start
  86.7 16.1 %all-gather.5.cloned.1.call-done = bf16[8,128,1024]{2,1,0:T(8,128)(2,1)} async-done(((bf16[1,128,1024]{2,1,0:T(8,128)(2,1)}), bf16[8,128,1024]{2,1,0:T(8,128)(2,1)}) %all-gather.5.cloned.1.call-update) | async-done | bytes 2097168 | tf_op jit(solution)/shard_map/all_gather | solution.py:121
  102.8 4.1 %reshape.158 = bf16[256,4,1024]{2,1,0:T(4,128)(2,1)} reshape(bf16[8,128,1024]{2,1,0:T(8,128)(2,1)} %all-gather.5.cloned.1.call-done) | data formatting | bytes 4194304 | tf_op jit(solution)/shard_map/reshape | solution.py:143
  106.9 5.7 %fusion.17 = bf16[256,4,256]{2,0,1:T(8,128)(2,1)S(1)} fusion(bf16[4,256,1024]{2,1,0:T(8,128)(2,1)} %param.8, bf16[256,4,1024]{2,1,0:T(4,128)(2,1)} %reshape.158, f32[4,256,256]{2,1,0:T(8,128)} %get-tuple-element.13), kind=kOutput, calls=%fused_computation.33 | convolution fusion | flops 555745280 | bytes 5767168 | tf_op jit(solution)/shard_map/rkd,kfd->rkf/dot_general | solution.py:144
  112.7 0.0 copy-start.4
  112.7 0.7 convert_bitcast_fusion
  113.4 0.0 copy-done.4
  113.5 2.9 %copy.29 = bf16[256,4,1024]{2,1,0:T(4,128)(2,1)} copy(bf16[256,4,1024]{2,0,1:T(8,128)(2,1)S(1)} %convert_bitcast_fusion) | data formatting | bytes 4194304 | tf_op jit(solution)/shard_map/convert_element_type | solution.py:161
  116.4 4.0 %reshape.159 = bf16[8,128,1024]{2,1,0:T(8,128)(2,1)} reshape(bf16[256,4,1024]{2,1,0:T(4,128)(2,1)} %copy.29) | data formatting | bytes 4194304 | tf_op jit(solution)/shard_map/reshape | solution.py:161
  120.4 0.0 reduce-scatter.5.cloned.1.call-update
  120.4 1.0 copy-done.2
  121.4 1.0 copy.25
  122.4 3.9 %convolution_convert_fusion.1 = bf16[4,1024,256]{2,1,0:T(8,128)(2,1)} fusion(bf16[256,4,1024]{0,2,1:T(8,128)(2,1)} %copy.32, bf16[256,4,256]{2,0,1:T(8,128)(2,1)} %copy-done.4), kind=kOutput, calls=%fused_computation.3 | convolution fusion | flops 537919488 | bytes 4718592 | tf_op jit(solution)/shard_map/rkd,rkf->kdf/dot_general | solution.py:152
  126.3 2.9 %convolution_convert_fusion = bf16[4,256,1024]{2,1,0:T(8,128)(2,1)} fusion(bf16[256,4,256]{2,0,1:T(8,128)(2,1)S(1)} %get-tuple-element.12, bf16[256,4,1024]{2,1,0:T(4,128)(2,1)S(1)} %copy-done.1), kind=kOutput, calls=%fused_computation.2 | convolution fusion | flops 537919488 | bytes 4718592 | tf_op jit(solution)/shard_map/rkf,rkd->kfd/dot_general | solution.py:149
  129.2 15.2 %reduce-scatter.3.cloned.1.call-done = bf16[1,128,1024]{2,1,0:T(8,128)(2,1)} async-done(((bf16[8,128,1024]{2,1,0:T(8,128)(2,1)}), bf16[1,128,1024]{2,1,0:T(8,128)(2,1)}) %reduce-scatter.3.cloned.1.call-update) | async-done | bytes 262160 | tf_op jit(solution)/shard_map/reduce_scatter | solution.py:124
  144.5 1.8 reshape.153.x_ref
  146.2 11.5 %shard_map.93 = bf16[32,4,1024]{2,1,0:T(4,128)(2,1)} custom-call(bf16[32,4,1024]{2,1,0:T(4,128)(2,1)} %reshape.153.x_ref), custom_call_target="tpu_custom_call" | custom-call | tf_op jit(solution)/shard_map/pallas_call | solution.py:74
  157.7 1.0 reshape.154
  158.8 1.2 fusion.7
  159.9 1.0 convolution_bitcast_fusion.1
  160.9 28.1 %reduce-scatter.5.cloned.1.call-done = bf16[1,128,1024]{2,1,0:T(8,128)(2,1)} async-done(((bf16[8,128,1024]{2,1,0:T(8,128)(2,1)}), bf16[1,128,1024]{2,1,0:T(8,128)(2,1)}) %reduce-scatter.5.cloned.1.call-update) | async-done | bytes 262160 | tf_op jit(solution)/shard_map/reduce_scatter | solution.py:124
  189.0 1.8 reshape.160.x_ref
  190.8 11.7 %shard_map.95 = bf16[32,4,1024]{2,1,0:T(4,128)(2,1)} custom-call(bf16[32,4,1024]{2,1,0:T(4,128)(2,1)} %reshape.160.x_ref), custom_call_target="tpu_custom_call" | custom-call | tf_op jit(solution)/shard_map/pallas_call | solution.py:74
  202.5 1.0 reshape.161
  203.5 0.0 copy-start.11
  203.5 1.3 fusion.43
  204.8 0.3 multiply_reduce_fusion.1
  205.1 0.0 copy-start.9
  205.1 0.6 copy-done.12
  205.7 2.1 convolution_bitcast_fusion.x_ref
  207.9 12.3 %shard_map.96 = f32[32,32,128]{2,1,0:T(8,128)} custom-call(f32[32,32,128]{2,1,0:T(8,128)} %convolution_bitcast_fusion.x_ref), custom_call_target="tpu_custom_call" | custom-call | tf_op jit(solution)/shard_map/pallas_call | solution.py:74
  220.2 1.7 reduce_sum.58
  221.9 14.1 %shard_map.97 = f32[8,4,128]{2,1,0:T(4,128)} custom-call(f32[8,4,128]{2,1,0:T(4,128)} %bitcast.142), custom_call_target="tpu_custom_call" | custom-call | tf_op jit(solution)/shard_map/pallas_call | solution.py:74
  236.0 1.3 reduce_sum.59.x_ref
  237.3 9.0 %shard_map.98 = f32[8,4,128]{2,1,0:T(4,128)} custom-call(f32[4,128]{1,0:T(4,128)} %reduce_sum.59.x_ref), custom_call_target="tpu_custom_call" | custom-call | tf_op jit(solution)/shard_map/pallas_call | solution.py:74
  246.3 13.5 %shard_map.99 = f32[32,32,128]{2,1,0:T(8,128)} custom-call(f32[32,128]{1,0:T(8,128)} %bitcast.143), custom_call_target="tpu_custom_call" | custom-call | tf_op jit(solution)/shard_map/pallas_call | solution.py:74
  259.9 2.2 fusion.8
  262.1 0.8 copy.47
  (21 shorter events, 0.0 us)
Async XLA Ops:
  7.2 66.2 %copy-start = (bf16[4,1024,256]{2,1,0:T(8,128)(2,1)S(1)}, bf16[4,1024,256]{2,1,0:T(8,128)(2,1)}, u32[]{:S(2)}) copy-start(bf16[4,1024,256]{2,1,0:T(8,128)(2,1)} %param.7) | copy-start | bytes 6291460
  7.2 19.5 %copy-start.5 = (bf16[1,256,1024]{2,1,0:T(8,128)(2,1)S(1)}, bf16[1,256,1024]{2,1,0:T(8,128)(2,1)}, u32[]{:S(2)}) copy-start(bf16[1,256,1024]{2,1,0:T(8,128)(2,1)} %param.9) | copy-start | bytes 1572868
  7.2 57.8 %all-gather.3.cloned.1.call-start = ((), (), s32[]{:S(2)}) async-start(), calls=%async_computation.2 | async-start | bytes 2359296 | tf_op jit(solution)/shard_map/all_gather | solution.py:121
  26.6 76.3 %all-gather.5.cloned.1.call-start = ((), (), s32[]{:S(2)}) async-start(), calls=%async_computation.4 | async-start | bytes 2359296 | tf_op jit(solution)/shard_map/all_gather | solution.py:121
  41.0 103.5 %reduce-scatter.3.cloned.1.call-start = ((), (), s32[]{:S(2)}) async-start(), calls=%async_computation.3 | async-start | bytes 2359296 | tf_op jit(solution)/shard_map/reduce_scatter | solution.py:124
  73.4 5.5 %copy-start.7 = (bf16[4,256,1024]{2,1,0:T(8,128)(2,1)S(1)}, bf16[4,256,1024]{2,1,0:T(8,128)(2,1)}, u32[]{:S(2)}) copy-start(bf16[4,256,1024]{2,1,0:T(8,128)(2,1)} %param.8) | copy-start | bytes 6291460
  86.5 102.5 %reduce-scatter.5.cloned.1.call-start = ((), (), s32[]{:S(2)}) async-start(), calls=%async_computation.5 | async-start | bytes 2359296 | tf_op jit(solution)/shard_map/reduce_scatter | solution.py:124
  112.7 0.8 copy-start.4
  120.4 1.0 copy-start.2
  122.4 3.9 %copy-start.1 = (bf16[256,4,1024]{2,1,0:T(4,128)(2,1)S(1)}, bf16[256,4,1024]{2,1,0:T(4,128)(2,1)}, u32[]{:S(2)}) copy-start(bf16[256,4,1024]{2,1,0:T(4,128)(2,1)} %reshape.158) | copy-start | bytes 6291460
  129.2 30.7 %copy-start.6 = (bf16[1,256,1024]{2,1,0:T(8,128)(2,1)S(1)}, bf16[1,256,1024]{2,1,0:T(8,128)(2,1)}, u32[]{:S(2)}) copy-start(bf16[1,256,1024]{2,1,0:T(8,128)(2,1)} %param.9) | copy-start | bytes 1572868
  160.9 43.9 %copy-start.10 = (f32[256,128]{1,0:T(8,128)S(1)}, f32[256,128]{1,0:T(8,128)}, u32[]{:S(2)}) copy-start(f32[256,128]{1,0:T(8,128)} %convolution_bitcast_fusion.1) | copy-start | bytes 393220
  203.5 2.3 copy-start.11
  205.1 0.7 copy-start.12
  205.1 0.7 copy-start.13
  205.1 0.6 copy-start.14
  205.1 54.7 %copy-start.3 = (f32[256,1024]{1,0:T(8,128)S(1)}, f32[256,1024]{1,0:T(8,128)}, u32[]{:S(2)}) copy-start(f32[256,1024]{1,0:T(8,128)} %fusion.43) | copy-start | bytes 3145732
  205.1 54.7 %copy-start.9 = (bf16[1024,128]{1,0:T(8,128)(2,1)S(1)}, bf16[1024,128]{1,0:T(8,128)(2,1)}, u32[]{:S(2)}) copy-start(bf16[1024,128]{1,0:T(8,128)(2,1)} %param.6) | copy-start | bytes 786436
  259.8 2.2 copy-start.8
Sparse Core Ops, SparseCore 0:
  26.7 38.2 all-gather.2
  67.4 35.3 all-gather.4
  105.4 39.0 reduce-scatter.2
  146.9 42.0 reduce-scatter.4

commit v3 on v2

--- a/solution.py
+++ b/solution.py
@@ -93,10 +93,8 @@
     rows, cols = value.shape
     part = value.reshape(n_expert, rows // n_expert, cols)
     part = exchange(part, "expert", n_expert, 4).sum(0)
-    part = part.reshape(n_dp, rows // (n_expert * n_dp), cols)
-    part = exchange(part, "dp", n_dp, 5).sum(0)
-    whole = exchange(part, "dp", n_dp, 6, gather=True).reshape(rows // n_expert, cols)
-    whole = exchange(whole, "expert", n_expert, 7, gather=True)
+    part = exchange(part, "dp", n_dp, 5, gather=True).sum(0)
+    whole = exchange(part, "expert", n_expert, 7, gather=True)
     return whole.reshape(rows, cols)
 
 
@@ -121,9 +119,10 @@
         return lax.all_gather(arrived, "dp", axis=0, tiled=True)
 
     def from_owners(partial_value, cid):
-        summed = lax.psum_scatter(partial_value, "dp", scatter_dimension=0, tiled=True)
+        pieces = exchange(partial_value, "dp", n_dp, cid + 8)
+        summed = pieces.astype(jnp.float32).sum(0).astype(jnp.bfloat16)
         chunks = summed.reshape(n_expert, experts_dev, width)
-        return exchange(chunks, "expert", n_expert, cid).reshape(summed.shape)
+        return exchange(chunks, "expert", n_expert, cid).reshape(1, *summed.shape)
 
     slot_rows = to_owners(slots, 0)
     blocks = slot_rows.reshape(-1, experts_dev, width)

time: 273 us -> 338 us (1.24)
  Pallas kernels: 97.2 us -> 198 us
  waiting for transfers between devices: 83.5 us -> 47.2 us
  other arithmetic: 3.2 us -> 7.35 us
    pallas_call x8 -> x9, Pallas kernels: 97.2 us -> 198 us  [exchange(): pl.pallas_call(functools.partial(_exchange_kernel, axis, other, n, gather...]
    reduce_scatter x2 -> x0, waiting for transfers between devices: 43.3 us -> none  [from_owners(): lax.psum_scatter(partial_value, 'dp', scatter_dimension=0, tiled=True)]
    all_gather x2, waiting for transfers between devices: 40.1 us -> 47.2 us  [to_owners(): return lax.all_gather(arrived, 'dp', axis=0, tiled=True)]
    reduce_sum x1 -> x3, other arithmetic: 1.31 us -> 5.46 us  [the longest x2 3.94 us: from_owners(): summed = pieces.astype(jnp.float32).sum(0).astype(jnp.bfloat16)]
  transfers between devices with their start and end apart: 4 -> 2, of which waited for: 4 -> 2; matrix products, arithmetic and copies ran while one was open for 20% -> 5% of each run, Pallas kernels for 9% -> 3%
where the time goes in v3:
time: 338 us; the launch traced here: 337 us
  Pallas kernels  198 us (59%)
  waiting for transfers between devices  47.2 us (14%)
  local copies, waits for them, and re-layouts  37.4 us (11%)
  matrix products  33 us (10%)
  between operations  14.3 us (4%)
  other arithmetic  7.35 us (2%)
    pallas_call x9, Pallas kernels, exchange(): pl.pallas_call(functools.partial(_exchange_kernel, axis, other, n, gather...  198 us
    all_gather x2, waiting for transfers between devices, to_owners(): return lax.all_gather(arrived, 'dp', axis=0, tiled=True)  47.2 us
    reshape x2, local copies, waits for them, and re-layouts, local(): blocks = slot_rows.reshape(-1, experts_dev, width)  8.36 us
  transfers between devices with their start and end apart: 2, of which 2 were waited for; matrix products, arithmetic and copies ran while one was open for 5% of the time, Pallas kernels for 3%

profile of v3, /device:TPU:1, one launch (start us, length us, event | category | flops | bytes accessed | tf_op | source)
XLA Modules:
  0.0 336.8 jit_solution(12040336291613905408)
XLA Ops:
  7.2 0.0 copy-start
  7.2 0.0 copy-start.5
  7.2 0.0 all-gather.3.cloned.1.call-start
  7.2 1.7 fusion.52
  8.9 0.2 fusion.39
  9.1 1.3 convolution_convert_fusion.4
  10.4 0.8 reshape.143.x_ref
  11.2 13.7 %shard_map.92 = bf16[32,4,1024]{2,1,0:T(4,128)(2,1)} custom-call(bf16[32,4,1024]{2,1,0:T(4,128)(2,1)} %reshape.143.x_ref), custom_call_target="tpu_custom_call" | custom-call | tf_op jit(solution)/shard_map/pallas_call | solution.py:74
  24.9 1.7 reshape.144
  26.6 0.0 all-gather.3.cloned.1.call-update
  26.7 0.0 all-gather.5.cloned.1.call-start
  26.7 0.4 convolution_convert_fusion.3
  27.1 0.8 reshape.150.x_ref
  27.9 11.4 %shard_map.95 = bf16[32,4,1024]{2,1,0:T(4,128)(2,1)} custom-call(bf16[32,4,1024]{2,1,0:T(4,128)(2,1)} %reshape.150.x_ref), custom_call_target="tpu_custom_call" | custom-call | tf_op jit(solution)/shard_map/pallas_call | solution.py:74
  39.4 1.7 reshape.151
  41.1 0.0 all-gather.5.cloned.1.call-update
  41.1 1.0 copy.27
  42.1 23.0 %all-gather.3.cloned.1.call-done = bf16[8,128,1024]{2,1,0:T(8,128)(2,1)} async-done(((bf16[1,128,1024]{2,1,0:T(8,128)(2,1)}), bf16[8,128,1024]{2,1,0:T(8,128)(2,1)}) %all-gather.3.cloned.1.call-update) | async-done | bytes 2097168 | tf_op jit(solution)/shard_map/all_gather | solution.py:119
  65.1 4.1 %reshape.145 = bf16[256,4,1024]{2,1,0:T(4,128)(2,1)} reshape(bf16[8,128,1024]{2,1,0:T(8,128)(2,1)} %all-gather.3.cloned.1.call-done) | data formatting | bytes 4194304 | tf_op jit(solution)/shard_map/reshape | solution.py:128
  69.2 4.3 %copy.34 = bf16[256,4,1024]{0,2,1:T(8,128)(2,1)} copy(bf16[256,4,1024]{2,1,0:T(4,128)(2,1)} %reshape.145) | data formatting | bytes 4194304 | tf_op jit(solution)/shard_map/reshape | solution.py:128
  73.4 5.3 %fusion.11 = (bf16[256,4,256]{2,0,1:T(8,128)(2,1)S(1)}, f32[4,256,256]{2,1,0:T(8,128)}) fusion(bf16[256,4,1024]{0,2,1:T(8,128)(2,1)} %copy.34, bf16[4,1024,256]{2,1,0:T(8,128)(2,1)S(1)} %copy-done), kind=kOutput, calls=%fused_computation.27 | convolution fusion | flops 553910272 | bytes 5767168 | tf_op jit(solution)/shard_map/rkd,kdf->rkf/dot_general | solution.py:129
  78.7 24.2 %all-gather.5.cloned.1.call-done = bf16[8,128,1024]{2,1,0:T(8,128)(2,1)} async-done(((bf16[1,128,1024]{2,1,0:T(8,128)(2,1)}), bf16[8,128,1024]{2,1,0:T(8,128)(2,1)}) %all-gather.5.cloned.1.call-update) | async-done | bytes 2097168 | tf_op jit(solution)/shard_map/all_gather | solution.py:119
  102.9 4.1 %reshape.152 = bf16[256,4,1024]{2,1,0:T(4,128)(2,1)} reshape(bf16[8,128,1024]{2,1,0:T(8,128)(2,1)} %all-gather.5.cloned.1.call-done) | data formatting | bytes 4194304 | tf_op jit(solution)/shard_map/reshape | solution.py:142
  107.0 5.8 %fusion.17 = bf16[256,4,256]{2,0,1:T(8,128)(2,1)S(1)} fusion(bf16[4,256,1024]{2,1,0:T(8,128)(2,1)} %param.8, bf16[256,4,1024]{2,1,0:T(4,128)(2,1)} %reshape.152, f32[4,256,256]{2,1,0:T(8,128)} %get-tuple-element.13), kind=kOutput, calls=%fused_computation.33 | convolution fusion | flops 555745280 | bytes 5767168 | tf_op jit(solution)/shard_map/rkd,kfd->rkf/dot_general | solution.py:143
  112.8 0.0 copy-start.2
  112.8 2.0 convert_bitcast_fusion
  114.9 2.0 convolution_convert_fusion.1
  116.9 0.0 copy-done.6
  116.9 0.7 convert_bitcast_fusion.1
  117.6 2.9 copy.29
  120.6 4.0 %reshape.146.x_ref = bf16[8,128,1024]{2,1,0:T(8,128)(2,1)} reshape(bf16[256,4,1024]{2,1,0:T(4,128)(2,1)} %copy.29) | data formatting | bytes 4194304 | tf_op jit(solution)/shard_map/reshape | solution.py:138
  124.6 42.4 %shard_map.93 = bf16[8,128,1024]{2,1,0:T(8,128)(2,1)} custom-call(bf16[8,128,1024]{2,1,0:T(8,128)(2,1)} %reshape.146.x_ref), custom_call_target="tpu_custom_call" | custom-call | tf_op jit(solution)/shard_map/pallas_call | solution.py:74
  166.9 2.0 reduce_sum.80
  168.9 0.8 reshape.147.x_ref
  169.7 13.5 %shard_map.94 = bf16[32,4,1024]{2,1,0:T(4,128)(2,1)} custom-call(bf16[32,4,1024]{2,1,0:T(4,128)(2,1)} %reshape.147.x_ref), custom_call_target="tpu_custom_call" | custom-call | tf_op jit(solution)/shard_map/pallas_call | solution.py:74
  183.2 1.0 reshape.148
  184.2 2.0 convolution_bitcast_fusion.1
  186.2 1.1 fusion.7
  187.4 4.6 %convolution_convert_fusion = bf16[4,256,1024]{2,1,0:T(8,128)(2,1)} fusion(bf16[256,4,256]{2,0,1:T(8,128)(2,1)S(1)} %get-tuple-element.12, bf16[256,4,1024]{2,1,0:T(4,128)(2,1)} %reshape.152), kind=kOutput, calls=%fused_computation.2 | convolution fusion | flops 537919488 | bytes 4718592 | tf_op jit(solution)/shard_map/rkf,rkd->kfd/dot_general | solution.py:148
  192.0 2.9 copy.31
  194.9 4.0 %reshape.153.x_ref = bf16[8,128,1024]{2,1,0:T(8,128)(2,1)} reshape(bf16[256,4,1024]{2,1,0:T(4,128)(2,1)} %copy.31) | data formatting | bytes 4194304 | tf_op jit(solution)/shard_map/reshape | solution.py:160
  198.9 47.3 %shard_map.96 = bf16[8,128,1024]{2,1,0:T(8,128)(2,1)} custom-call(bf16[8,128,1024]{2,1,0:T(8,128)(2,1)} %reshape.153.x_ref), custom_call_target="tpu_custom_call" | custom-call | tf_op jit(solution)/shard_map/pallas_call | solution.py:74
  246.2 2.0 reduce_sum.81
  248.2 0.8 reshape.154.x_ref
  249.0 17.9 %shard_map.97 = bf16[32,4,1024]{2,1,0:T(4,128)(2,1)} custom-call(bf16[32,4,1024]{2,1,0:T(4,128)(2,1)} %reshape.154.x_ref), custom_call_target="tpu_custom_call" | custom-call | tf_op jit(solution)/shard_map/pallas_call | solution.py:74
  267.0 1.0 reshape.155
  268.0 0.0 copy-start.10
  268.0 1.3 fusion.43
  269.3 0.0 copy-done.9
  269.3 0.3 multiply_reduce_fusion.1
  269.6 0.0 copy-start.8
  269.6 0.6 copy-done.11
  270.3 0.0 copy-done.13
  270.3 2.1 convolution_bitcast_fusion.x_ref
  272.4 13.3 %shard_map.98 = f32[32,32,128]{2,1,0:T(8,128)} custom-call(f32[32,32,128]{2,1,0:T(8,128)} %convolution_bitcast_fusion.x_ref), custom_call_target="tpu_custom_call" | custom-call | tf_op jit(solution)/shard_map/pallas_call | solution.py:74
  285.7 1.7 reduce_sum.84.x_ref
  287.4 21.3 %shard_map.99 = f32[8,32,128]{2,1,0:T(8,128)} custom-call(f32[32,128]{1,0:T(8,128)} %reduce_sum.84.x_ref), custom_call_target="tpu_custom_call" | custom-call | tf_op jit(solution)/shard_map/pallas_call | solution.py:74
  308.7 1.5 reduce_sum.85.x_ref
  310.3 16.7 %shard_map.100 = f32[32,32,128]{2,1,0:T(8,128)} custom-call(f32[32,128]{1,0:T(8,128)} %reduce_sum.85.x_ref), custom_call_target="tpu_custom_call" | custom-call | tf_op jit(solution)/shard_map/pallas_call | solution.py:74
  327.0 0.0 copy-start.7
  327.0 0.0 copy-done.4
  327.0 0.0 copy-done.8
  327.0 2.2 fusion.8
  329.2 0.8 copy.49
  (16 shorter events, 0.0 us)
Async XLA Ops:
  7.2 66.3 %copy-start = (bf16[4,1024,256]{2,1,0:T(8,128)(2,1)S(1)}, bf16[4,1024,256]{2,1,0:T(8,128)(2,1)}, u32[]{:S(2)}) copy-start(bf16[4,1024,256]{2,1,0:T(8,128)(2,1)} %param.7) | copy-start | bytes 6291460
  7.2 19.5 %copy-start.5 = (bf16[1,256,1024]{2,1,0:T(8,128)(2,1)S(1)}, bf16[1,256,1024]{2,1,0:T(8,128)(2,1)}, u32[]{:S(2)}) copy-start(bf16[1,256,1024]{2,1,0:T(8,128)(2,1)} %param.9) | copy-start | bytes 1572868
  7.2 57.9 %all-gather.3.cloned.1.call-start = ((), (), s32[]{:S(2)}) async-start(), calls=%async_computation | async-start | bytes 2359296 | tf_op jit(solution)/shard_map/all_gather | solution.py:119
  11.2 29.9 %copy-start.3 = (bf16[1,256,1024]{2,1,0:T(8,128)(2,1)S(1)}, bf16[1,256,1024]{2,1,0:T(8,128)(2,1)}, u32[]{:S(2)}) copy-start(bf16[1,256,1024]{2,1,0:T(8,128)(2,1)} %param.5) | copy-start | bytes 1572868
  26.7 76.3 %all-gather.5.cloned.1.call-start = ((), (), s32[]{:S(2)}) async-start(), calls=%async_computation.1 | async-start | bytes 2359296 | tf_op jit(solution)/shard_map/all_gather | solution.py:119
  112.8 2.1 copy-start.2
  114.9 2.0 copy-start.6
  187.4 4.7 %copy-start.1 = (bf16[256,4,1024]{2,0,1:T(8,128)(2,1)S(1)}, bf16[256,4,1024]{2,0,1:T(8,128)(2,1)}, u32[]{:S(2)}) copy-start(bf16[256,4,1024]{2,0,1:T(8,128)(2,1)} %convert_bitcast_fusion) | copy-start | bytes 6291460
  248.2 21.1 %copy-start.9 = (f32[256,128]{1,0:T(8,128)S(1)}, f32[256,128]{1,0:T(8,128)}, u32[]{:S(2)}) copy-start(f32[256,128]{1,0:T(8,128)} %convolution_bitcast_fusion.1) | copy-start | bytes 393220
  268.0 2.3 copy-start.10
  269.6 0.6 copy-start.11
  269.6 0.6 copy-start.12
  269.6 0.6 copy-start.13
  269.6 57.4 %copy-start.4 = (f32[256,1024]{1,0:T(8,128)S(1)}, f32[256,1024]{1,0:T(8,128)}, u32[]{:S(2)}) copy-start(f32[256,1024]{1,0:T(8,128)} %fusion.43) | copy-start | bytes 3145732
  269.6 57.4 %copy-start.8 = (bf16[1024,128]{1,0:T(8,128)(2,1)S(1)}, bf16[1024,128]{1,0:T(8,128)(2,1)}, u32[]{:S(2)}) copy-start(bf16[1024,128]{1,0:T(8,128)(2,1)} %param.6) | copy-start | bytes 786436
  327.0 2.2 copy-start.7
Sparse Core Ops, SparseCore 0:
  26.8 38.2 all-gather.2
  67.5 35.3 all-gather.4

commit v4 on v2

--- a/solution.py
+++ b/solution.py
@@ -89,15 +89,115 @@
     return jax.nn.gelu(values, approximate=False)
 
 
+def _allsum_kernel(n_dp, n_ex, x_ref, o_ref, land1, land2, land3, red1, red2, s1, r1, s2, r2, s3, r3):
+    me_d = lax.axis_index("dp")
+    me_e = lax.axis_index("expert")
+    mesh_id = pl.DeviceIdType.MESH
+    barrier = pltpu.get_barrier_semaphore()
+
+    @pl.loop(0, n_ex)
+    def _(j):
+        @pl.when(j != me_e)
+        def _():
+            pl.semaphore_signal(barrier, inc=1, device_id=(me_d, j), device_id_type=mesh_id)
+
+    @pl.loop(0, n_dp)
+    def _(k):
+        @pl.when(k != me_d)
+        def _():
+            pl.semaphore_signal(barrier, inc=1, device_id=(k, me_e), device_id_type=mesh_id)
+
+    pl.semaphore_wait(barrier, n_ex - 1 + n_dp - 1)
+
+    def ex_copy(src, land, send, recv, j, slot):
+        return pltpu.make_async_remote_copy(
+            src_ref=src, dst_ref=land.at[slot], send_sem=send.at[j], recv_sem=recv.at[slot],
+            device_id=(me_d, j), device_id_type=mesh_id)
+
+    def dp_copy(src, land, send, recv, k, slot):
+        return pltpu.make_async_remote_copy(
+            src_ref=src, dst_ref=land.at[slot], send_sem=send.at[k], recv_sem=recv.at[slot],
+            device_id=(k, me_e), device_id_type=mesh_id)
+
+    @pl.loop(0, n_ex)
+    def _(j):
+        @pl.when(j != me_e)
+        def _():
+            ex_copy(x_ref.at[j], land1, s1, r1, j, me_e).start()
+
+    land1[me_e] = x_ref[me_e]
+
+    @pl.loop(0, n_ex)
+    def _(j):
+        @pl.when(j != me_e)
+        def _():
+            ex_copy(x_ref.at[j], land1, s1, r1, j, j).wait_recv()
+            ex_copy(x_ref.at[j], land1, s1, r1, j, me_e).wait_send()
+
+    red1[...] = jnp.sum(land1[...], axis=0)
+
+    @pl.loop(0, n_dp)
+    def _(k):
+        @pl.when(k != me_d)
+        def _():
+            dp_copy(red1, land2, s2, r2, k, me_d).start()
+
+    land2[me_d] = red1[...]
+
+    @pl.loop(0, n_dp)
+    def _(k):
+        @pl.when(k != me_d)
+        def _():
+            dp_copy(red1, land2, s2, r2, k, k).wait_recv()
+            dp_copy(red1, land2, s2, r2, k, me_d).wait_send()
+
+    total = land2[0]
+    for k in range(1, n_dp):
+        total = total + land2[k]
+    red2[...] = total
+
+    @pl.loop(0, n_ex)
+    def _(j):
+        @pl.when(j != me_e)
+        def _():
+            ex_copy(red2, land3, s3, r3, j, me_e).start()
+
+    o_ref[me_e] = red2[...]
+
+    @pl.loop(0, n_ex)
+    def _(j):
+        @pl.when(j != me_e)
+        def _():
+            ex_copy(red2, land3, s3, r3, j, j).wait_recv()
+            o_ref[j] = land3[j]
+            ex_copy(red2, land3, s3, r3, j, me_e).wait_send()
+
+
 def all_sum(value, n_dp, n_expert):
     rows, cols = value.shape
-    part = value.reshape(n_expert, rows // n_expert, cols)
-    part = exchange(part, "expert", n_expert, 4).sum(0)
-    part = part.reshape(n_dp, rows // (n_expert * n_dp), cols)
-    part = exchange(part, "dp", n_dp, 5).sum(0)
-    whole = exchange(part, "dp", n_dp, 6, gather=True).reshape(rows // n_expert, cols)
-    whole = exchange(whole, "expert", n_expert, 7, gather=True)
-    return whole.reshape(rows, cols)
+    block = (rows // n_expert, cols)
+    chunks = value.reshape(n_expert, *block)
+    out = pl.pallas_call(
+        functools.partial(_allsum_kernel, n_dp, n_expert),
+        out_shape=jax.ShapeDtypeStruct(chunks.shape, value.dtype),
+        in_specs=[pl.BlockSpec(memory_space=pltpu.VMEM)],
+        out_specs=pl.BlockSpec(memory_space=pltpu.VMEM),
+        scratch_shapes=[
+            pltpu.VMEM(chunks.shape, value.dtype),
+            pltpu.VMEM((n_dp,) + block, value.dtype),
+            pltpu.VMEM(chunks.shape, value.dtype),
+            pltpu.VMEM(block, value.dtype),
+            pltpu.VMEM(block, value.dtype),
+            pltpu.SemaphoreType.DMA((n_expert,)),
+            pltpu.SemaphoreType.DMA((n_expert,)),
+            pltpu.SemaphoreType.DMA((n_dp,)),
+            pltpu.SemaphoreType.DMA((n_dp,)),
+            pltpu.SemaphoreType.DMA((n_expert,)),
+            pltpu.SemaphoreType.DMA((n_expert,)),
+        ],
+        compiler_params=pltpu.CompilerParams(collective_id=4, has_side_effects=True),
+    )(chunks)
+    return out.reshape(rows, cols)
 
 
 def local(n_dp, n_expert, tokens, router, weight_in, weight_out, cotangent):

time: 273 us -> 254 us (0.930)
  Pallas kernels: 97.2 us -> 81.6 us
  other arithmetic: 3.2 us -> 0.19 us
    pallas_call x8 -> x4, Pallas kernels: 97.2 us -> 47.3 us  [exchange(): pl.pallas_call(functools.partial(_exchange_kernel, axis, other, n, gather...]
    pallas_call x0 -> x1, Pallas kernels: none -> 34.3 us  [all_sum(): pl.pallas_call(functools.partial(_allsum_kernel, n_dp, n_expert), out_sha...]
    reduce_sum x2 -> x0, other arithmetic: 3.01 us -> none  [the longest x1 1.69 us: all_sum(): part = exchange(part, 'expert', n_expert, 4).sum(0)]
  transfers between devices with their start and end apart: 4 -> 4, of which waited for: 4 -> 4; matrix products, arithmetic and copies ran while one was open for 20% -> 22% of each run, Pallas kernels for 9% -> 9%
where the time goes in v4:
time: 254 us; the launch traced here: 253 us
  waiting for transfers between devices  85.4 us (34%)
  Pallas kernels  81.6 us (32%)
  local copies, waits for them, and re-layouts  40.4 us (16%)
  matrix products  30.8 us (12%)
  between operations  14 us (6%)
    pallas_call x4, Pallas kernels, exchange(): pl.pallas_call(functools.partial(_exchange_kernel, axis, other, n, gather...  47.3 us
    reduce_scatter x2, waiting for transfers between devices, from_owners(): lax.psum_scatter(partial_value, 'dp', scatter_dimension=0, tiled=True)  45.1 us
    all_gather x2, waiting for transfers between devices, to_owners(): return lax.all_gather(arrived, 'dp', axis=0, tiled=True)  40.3 us
    pallas_call x1, Pallas kernels, all_sum(): pl.pallas_call(functools.partial(_allsum_kernel, n_dp, n_expert), out_sha...  34.3 us
    reshape x2, local copies, waits for them, and re-layouts, local(): blocks = slot_rows.reshape(-1, experts_dev, width)  8.38 us
    dot_general x1, matrix products, local(): jnp.einsum('rkd,kfd->rkf', grad_blocks, weight_out, preferred_element_typ...  5.73 us
    dot_general x1, matrix products, local(): jnp.einsum('rkd,kdf->rkf', blocks, weight_in, preferred_element_type=jnp....  5.45 us
  transfers between devices with their start and end apart: 4, of which 4 were waited for; matrix products, arithmetic and copies ran while one was open for 22% of the time, Pallas kernels for 9%

profile of v4, /device:TPU:1, one launch (start us, length us, event | category | flops | bytes accessed | tf_op | source)
XLA Modules:
  0.0 252.8 jit_solution(4824801395908640596)
XLA Ops:
  7.2 0.0 copy-start
  7.2 0.0 copy-start.5
  7.2 0.0 all-gather.3.cloned.1.call-start
  7.2 1.7 fusion.52
  8.9 0.2 fusion.39
  9.1 1.3 convolution_convert_fusion.4
  10.4 0.8 reshape.143.x_ref
  11.2 13.6 %shard_map.92 = bf16[32,4,1024]{2,1,0:T(4,128)(2,1)} custom-call(bf16[32,4,1024]{2,1,0:T(4,128)(2,1)} %reshape.143.x_ref), custom_call_target="tpu_custom_call" | custom-call | tf_op jit(solution)/shard_map/pallas_call | solution.py:74
  24.9 1.7 reshape.144
  26.6 0.0 all-gather.3.cloned.1.call-update
  26.6 0.0 all-gather.5.cloned.1.call-start
  26.7 0.0 copy-done.5
  26.7 0.4 convolution_convert_fusion.3
  27.0 0.8 reshape.150.x_ref
  27.9 11.4 %shard_map.94 = bf16[32,4,1024]{2,1,0:T(4,128)(2,1)} custom-call(bf16[32,4,1024]{2,1,0:T(4,128)(2,1)} %reshape.150.x_ref), custom_call_target="tpu_custom_call" | custom-call | tf_op jit(solution)/shard_map/pallas_call | solution.py:74
  39.3 1.7 reshape.151
  41.0 0.0 all-gather.5.cloned.1.call-update
  41.0 0.0 reduce-scatter.3.cloned.1.call-start
  41.1 23.9 %all-gather.3.cloned.1.call-done = bf16[8,128,1024]{2,1,0:T(8,128)(2,1)} async-done(((bf16[1,128,1024]{2,1,0:T(8,128)(2,1)}), bf16[8,128,1024]{2,1,0:T(8,128)(2,1)}) %all-gather.3.cloned.1.call-update) | async-done | bytes 2097168 | tf_op jit(solution)/shard_map/all_gather | solution.py:221
  65.0 4.1 %reshape.145 = bf16[256,4,1024]{2,1,0:T(4,128)(2,1)} reshape(bf16[8,128,1024]{2,1,0:T(8,128)(2,1)} %all-gather.3.cloned.1.call-done) | data formatting | bytes 4194304 | tf_op jit(solution)/shard_map/reshape | solution.py:229
  69.1 4.3 %copy.32 = bf16[256,4,1024]{0,2,1:T(8,128)(2,1)} copy(bf16[256,4,1024]{2,1,0:T(4,128)(2,1)} %reshape.145) | data formatting | bytes 4194304 | tf_op jit(solution)/shard_map/reshape | solution.py:229
  73.4 0.0 copy-done
  73.4 5.4 %fusion.11 = (bf16[256,4,256]{2,0,1:T(8,128)(2,1)S(1)}, f32[4,256,256]{2,1,0:T(8,128)}) fusion(bf16[256,4,1024]{0,2,1:T(8,128)(2,1)} %copy.32, bf16[4,1024,256]{2,1,0:T(8,128)(2,1)S(1)} %copy-done), kind=kOutput, calls=%fused_computation.27 | convolution fusion | flops 553910272 | bytes 5767168 | tf_op jit(solution)/shard_map/rkd,kdf->rkf/dot_general | solution.py:230
  78.8 0.0 copy-done.7
  78.8 0.7 convert_bitcast_fusion.1
  79.6 2.9 %copy.27 = bf16[256,4,1024]{2,1,0:T(4,128)(2,1)} copy(bf16[256,4,1024]{2,0,1:T(8,128)(2,1)S(1)} %convert_bitcast_fusion.1) | data formatting | bytes 4194304 | tf_op jit(solution)/shard_map/convert_element_type | solution.py:239
  82.5 4.0 %reshape.146 = bf16[8,128,1024]{2,1,0:T(8,128)(2,1)} reshape(bf16[256,4,1024]{2,1,0:T(4,128)(2,1)} %copy.27) | data formatting | bytes 4194304 | tf_op jit(solution)/shard_map/reshape | solution.py:239
  86.5 0.0 reduce-scatter.3.cloned.1.call-update
  86.5 0.2 reduce-scatter.5.cloned.1.call-start
  86.7 16.3 %all-gather.5.cloned.1.call-done = bf16[8,128,1024]{2,1,0:T(8,128)(2,1)} async-done(((bf16[1,128,1024]{2,1,0:T(8,128)(2,1)}), bf16[8,128,1024]{2,1,0:T(8,128)(2,1)}) %all-gather.5.cloned.1.call-update) | async-done | bytes 2097168 | tf_op jit(solution)/shard_map/all_gather | solution.py:221
  103.0 4.1 %reshape.152 = bf16[256,4,1024]{2,1,0:T(4,128)(2,1)} reshape(bf16[8,128,1024]{2,1,0:T(8,128)(2,1)} %all-gather.5.cloned.1.call-done) | data formatting | bytes 4194304 | tf_op jit(solution)/shard_map/reshape | solution.py:243
  107.1 5.7 %fusion.17 = bf16[256,4,256]{2,0,1:T(8,128)(2,1)S(1)} fusion(bf16[4,256,1024]{2,1,0:T(8,128)(2,1)} %param.8, bf16[256,4,1024]{2,1,0:T(4,128)(2,1)} %reshape.152, f32[4,256,256]{2,1,0:T(8,128)} %get-tuple-element.13), kind=kOutput, calls=%fused_computation.33 | convolution fusion | flops 555745280 | bytes 5767168 | tf_op jit(solution)/shard_map/rkd,kfd->rkf/dot_general | solution.py:244
  112.9 0.0 copy-start.4
  112.9 0.7 convert_bitcast_fusion
  113.6 0.0 copy-done.4
  113.7 2.9 %copy.29 = bf16[256,4,1024]{2,1,0:T(4,128)(2,1)} copy(bf16[256,4,1024]{2,0,1:T(8,128)(2,1)S(1)} %convert_bitcast_fusion) | data formatting | bytes 4194304 | tf_op jit(solution)/shard_map/convert_element_type | solution.py:261
  116.6 4.0 %reshape.153 = bf16[8,128,1024]{2,1,0:T(8,128)(2,1)} reshape(bf16[256,4,1024]{2,1,0:T(4,128)(2,1)} %copy.29) | data formatting | bytes 4194304 | tf_op jit(solution)/shard_map/reshape | solution.py:261
  120.6 0.0 reduce-scatter.5.cloned.1.call-update
  120.6 1.0 copy-done.2
  121.6 1.0 copy.25
  122.6 3.9 %convolution_convert_fusion.1 = bf16[4,1024,256]{2,1,0:T(8,128)(2,1)} fusion(bf16[256,4,1024]{0,2,1:T(8,128)(2,1)} %copy.32, bf16[256,4,256]{2,0,1:T(8,128)(2,1)} %copy-done.4), kind=kOutput, calls=%fused_computation.3 | convolution fusion | flops 537919488 | bytes 4718592 | tf_op jit(solution)/shard_map/rkd,rkf->kdf/dot_general | solution.py:252
  126.5 2.9 %convolution_convert_fusion = bf16[4,256,1024]{2,1,0:T(8,128)(2,1)} fusion(bf16[256,4,256]{2,0,1:T(8,128)(2,1)S(1)} %get-tuple-element.12, bf16[256,4,1024]{2,1,0:T(4,128)(2,1)S(1)} %copy-done.1), kind=kOutput, calls=%fused_computation.2 | convolution fusion | flops 537919488 | bytes 4718592 | tf_op jit(solution)/shard_map/rkf,rkd->kfd/dot_general | solution.py:249
  129.4 16.2 %reduce-scatter.3.cloned.1.call-done = bf16[1,128,1024]{2,1,0:T(8,128)(2,1)} async-done(((bf16[8,128,1024]{2,1,0:T(8,128)(2,1)}), bf16[1,128,1024]{2,1,0:T(8,128)(2,1)}) %reduce-scatter.3.cloned.1.call-update) | async-done | bytes 262160 | tf_op jit(solution)/shard_map/reduce_scatter | solution.py:224
  145.6 1.8 reshape.147.x_ref
  147.4 10.8 %shard_map.93 = bf16[32,4,1024]{2,1,0:T(4,128)(2,1)} custom-call(bf16[32,4,1024]{2,1,0:T(4,128)(2,1)} %reshape.147.x_ref), custom_call_target="tpu_custom_call" | custom-call | tf_op jit(solution)/shard_map/pallas_call | solution.py:74
  158.2 1.0 reshape.148
  159.2 1.2 fusion.7
  160.4 0.0 copy-done.6
  160.4 0.9 convolution_bitcast_fusion.1
  161.3 28.9 %reduce-scatter.5.cloned.1.call-done = bf16[1,128,1024]{2,1,0:T(8,128)(2,1)} async-done(((bf16[8,128,1024]{2,1,0:T(8,128)(2,1)}), bf16[1,128,1024]{2,1,0:T(8,128)(2,1)}) %reduce-scatter.5.cloned.1.call-update) | async-done | bytes 262160 | tf_op jit(solution)/shard_map/reduce_scatter | solution.py:224
  190.3 1.8 reshape.154.x_ref
  192.0 11.5 %shard_map.95 = bf16[32,4,1024]{2,1,0:T(4,128)(2,1)} custom-call(bf16[32,4,1024]{2,1,0:T(4,128)(2,1)} %reshape.154.x_ref), custom_call_target="tpu_custom_call" | custom-call | tf_op jit(solution)/shard_map/pallas_call | solution.py:74
  203.5 1.0 reshape.155
  204.5 0.0 copy-start.11
  204.5 1.3 fusion.43
  205.8 0.3 multiply_reduce_fusion.1
  206.2 0.6 copy-done.12
  206.8 0.0 copy-done.13
  206.8 0.0 copy-done.11
  206.8 2.1 convolution_bitcast_fusion.x_ref
  208.9 34.3 %shard_map.96 = f32[32,32,128]{2,1,0:T(8,128)} custom-call(f32[32,32,128]{2,1,0:T(8,128)} %convolution_bitcast_fusion.x_ref), custom_call_target="tpu_custom_call" | custom-call | tf_op jit(solution)/shard_map/pallas_call | solution.py:180
  243.3 2.2 fusion.8
  245.5 0.0 copy-done.8
  245.5 0.8 copy.47
  (16 shorter events, 0.0 us)
Async XLA Ops:
  7.2 66.2 %copy-start = (bf16[4,1024,256]{2,1,0:T(8,128)(2,1)S(1)}, bf16[4,1024,256]{2,1,0:T(8,128)(2,1)}, u32[]{:S(2)}) copy-start(bf16[4,1024,256]{2,1,0:T(8,128)(2,1)} %param.7) | copy-start | bytes 6291460
  7.2 19.5 %copy-start.5 = (bf16[1,256,1024]{2,1,0:T(8,128)(2,1)S(1)}, bf16[1,256,1024]{2,1,0:T(8,128)(2,1)}, u32[]{:S(2)}) copy-start(bf16[1,256,1024]{2,1,0:T(8,128)(2,1)} %param.9) | copy-start | bytes 1572868
  7.2 57.8 %all-gather.3.cloned.1.call-start = ((), (), s32[]{:S(2)}) async-start(), calls=%async_computation.2 | async-start | bytes 2359296 | tf_op jit(solution)/shard_map/all_gather | solution.py:221
  26.6 76.4 %all-gather.5.cloned.1.call-start = ((), (), s32[]{:S(2)}) async-start(), calls=%async_computation.4 | async-start | bytes 2359296 | tf_op jit(solution)/shard_map/all_gather | solution.py:221
  41.0 104.6 %reduce-scatter.3.cloned.1.call-start = ((), (), s32[]{:S(2)}) async-start(), calls=%async_computation.3 | async-start | bytes 2359296 | tf_op jit(solution)/shard_map/reduce_scatter | solution.py:224
  73.4 5.5 %copy-start.7 = (bf16[4,256,1024]{2,1,0:T(8,128)(2,1)S(1)}, bf16[4,256,1024]{2,1,0:T(8,128)(2,1)}, u32[]{:S(2)}) copy-start(bf16[4,256,1024]{2,1,0:T(8,128)(2,1)} %param.8) | copy-start | bytes 6291460
  86.5 103.8 %reduce-scatter.5.cloned.1.call-start = ((), (), s32[]{:S(2)}) async-start(), calls=%async_computation.5 | async-start | bytes 2359296 | tf_op jit(solution)/shard_map/reduce_scatter | solution.py:224
  112.9 0.8 copy-start.4
  120.6 1.0 copy-start.2
  122.6 3.9 %copy-start.1 = (bf16[256,4,1024]{2,1,0:T(4,128)(2,1)S(1)}, bf16[256,4,1024]{2,1,0:T(4,128)(2,1)}, u32[]{:S(2)}) copy-start(bf16[256,4,1024]{2,1,0:T(4,128)(2,1)} %reshape.152) | copy-start | bytes 6291460
  129.4 31.0 %copy-start.6 = (bf16[1,256,1024]{2,1,0:T(8,128)(2,1)S(1)}, bf16[1,256,1024]{2,1,0:T(8,128)(2,1)}, u32[]{:S(2)}) copy-start(bf16[1,256,1024]{2,1,0:T(8,128)(2,1)} %param.9) | copy-start | bytes 1572868
  161.3 44.5 %copy-start.10 = (f32[256,128]{1,0:T(8,128)S(1)}, f32[256,128]{1,0:T(8,128)}, u32[]{:S(2)}) copy-start(f32[256,128]{1,0:T(8,128)} %convolution_bitcast_fusion.1) | copy-start | bytes 393220
  204.5 2.3 copy-start.11
  205.8 37.5 %copy-start.9 = (bf16[1024,128]{1,0:T(8,128)(2,1)S(1)}, bf16[1024,128]{1,0:T(8,128)(2,1)}, u32[]{:S(2)}) copy-start(bf16[1024,128]{1,0:T(8,128)(2,1)} %param.6) | copy-start | bytes 786436
  206.1 0.7 copy-start.12
  206.1 0.7 copy-start.13
  206.1 0.7 copy-start.14
  206.1 37.1 %copy-start.3 = (f32[256,1024]{1,0:T(8,128)S(1)}, f32[256,1024]{1,0:T(8,128)}, u32[]{:S(2)}) copy-start(f32[256,1024]{1,0:T(8,128)} %fusion.43) | copy-start | bytes 3145732
  243.2 2.2 copy-start.8
Sparse Core Ops, SparseCore 0:
  26.7 38.2 all-gather.2
  67.4 35.5 all-gather.4
  105.6 39.9 reduce-scatter.2
  148.0 42.1 reduce-scatter.4

commit v5 on v4

--- a/solution.py
+++ b/solution.py
@@ -87,6 +87,76 @@
 
 def gelu_exact(values):
     return jax.nn.gelu(values, approximate=False)
+
+
+def _relay_sum_kernel(n_chip, x_ref, o_ref, land1, pair, land2, s1, r1, s2, r2):
+    me = lax.axis_index("dp")
+    fixed = lax.axis_index("expert")
+    core = me % 2
+    chip = me // 2
+    partner = me + 1 - 2 * core
+    mesh_id = pl.DeviceIdType.MESH
+    barrier = pltpu.get_barrier_semaphore()
+    pl.semaphore_signal(barrier, inc=1, device_id=(partner, fixed), device_id_type=mesh_id)
+    for h in range(n_chip):
+        @pl.when(h != chip)
+        def _():
+            pl.semaphore_signal(barrier, inc=1, device_id=(2 * h + core, fixed), device_id_type=mesh_id)
+    pl.semaphore_wait(barrier, n_chip)
+
+    def to_partner(h):
+        return pltpu.make_async_remote_copy(
+            src_ref=x_ref.at[2 * h + 1 - core], dst_ref=land1.at[h], send_sem=s1.at[h], recv_sem=r1.at[h],
+            device_id=(partner, fixed), device_id_type=mesh_id)
+
+    for h in range(n_chip):
+        to_partner(h).start()
+    for h in range(n_chip):
+        to_partner(h).wait_recv()
+        pair[h] = (x_ref[2 * h + core].astype(jnp.float32) + land1[h].astype(jnp.float32)).astype(pair.dtype)
+        to_partner(h).wait_send()
+
+    def to_chip(h, slot):
+        return pltpu.make_async_remote_copy(
+            src_ref=pair.at[h], dst_ref=land2.at[slot], send_sem=s2.at[h], recv_sem=r2.at[slot],
+            device_id=(2 * h + core, fixed), device_id_type=mesh_id)
+
+    for h in range(n_chip):
+        @pl.when(h != chip)
+        def _():
+            to_chip(h, chip).start()
+    land2[chip] = pair[chip]
+    for h in range(n_chip):
+        @pl.when(h != chip)
+        def _():
+            to_chip(h, h).wait_recv()
+            to_chip(h, chip).wait_send()
+    total = land2[0].astype(jnp.float32)
+    for h in range(1, n_chip):
+        total = total + land2[h].astype(jnp.float32)
+    o_ref[...] = total.astype(o_ref.dtype)
+
+
+def relay_sum(x, collective_id):
+    n_dp = x.shape[0]
+    n_chip = n_dp // 2
+    block = x.shape[1:]
+    return pl.pallas_call(
+        functools.partial(_relay_sum_kernel, n_chip),
+        out_shape=jax.ShapeDtypeStruct(block, x.dtype),
+        in_specs=[pl.BlockSpec(memory_space=pltpu.VMEM)],
+        out_specs=pl.BlockSpec(memory_space=pltpu.VMEM),
+        scratch_shapes=[
+            pltpu.VMEM((n_chip,) + block, x.dtype),
+            pltpu.VMEM((n_chip,) + block, x.dtype),
+            pltpu.VMEM((n_chip,) + block, x.dtype),
+            pltpu.SemaphoreType.DMA((n_chip,)),
+            pltpu.SemaphoreType.DMA((n_chip,)),
+            pltpu.SemaphoreType.DMA((n_chip,)),
+            pltpu.SemaphoreType.DMA((n_chip,)),
+        ],
+        compiler_params=pltpu.CompilerParams(collective_id=collective_id, has_side_effects=True),
+    )(x)
 
 
 def _allsum_kernel(n_dp, n_ex, x_ref, o_ref, land1, land2, land3, red1, red2, s1, r1, s2, r2, s3, r3):
@@ -221,9 +291,9 @@
         return lax.all_gather(arrived, "dp", axis=0, tiled=True)
 
     def from_owners(partial_value, cid):
-        summed = lax.psum_scatter(partial_value, "dp", scatter_dimension=0, tiled=True)
+        summed = relay_sum(partial_value, cid + 8)
         chunks = summed.reshape(n_expert, experts_dev, width)
-        return exchange(chunks, "expert", n_expert, cid).reshape(summed.shape)
+        return exchange(chunks, "expert", n_expert, cid).reshape(1, *summed.shape)
 
     slot_rows = to_owners(slots, 0)
     blocks = slot_rows.reshape(-1, experts_dev, width)

time: 254 us -> 284 us (1.12)
  Pallas kernels: 81.6 us -> 149 us
  waiting for transfers between devices: 85.4 us -> 47.2 us
    pallas_call x0 -> x2, Pallas kernels: none -> 64.2 us  [relay_sum(): pl.pallas_call(functools.partial(_relay_sum_kernel, n_chip), out_shape=ja...]
    reduce_scatter x2 -> x0, waiting for transfers between devices: 45.1 us -> none  [from_owners(): lax.psum_scatter(partial_value, 'dp', scatter_dimension=0, tiled=True)]
    all_gather x2, waiting for transfers between devices: 40.3 us -> 47.2 us  [to_owners(): return lax.all_gather(arrived, 'dp', axis=0, tiled=True)]
    pallas_call x1, Pallas kernels: 34.3 us -> 38.5 us  [all_sum(): pl.pallas_call(functools.partial(_allsum_kernel, n_dp, n_expert), out_sha...]
  transfers between devices with their start and end apart: 4 -> 2, of which waited for: 4 -> 2; matrix products, arithmetic and copies ran while one was open for 22% -> 6% of each run, Pallas kernels for 9% -> 4%
where the time goes in v5:
time: 284 us; the launch traced here: 283 us
  Pallas kernels  149 us (52%)
  waiting for transfers between devices  47.2 us (17%)
  local copies, waits for them, and re-layouts  39.4 us (14%)
  matrix products  32.9 us (12%)
  between operations  14.3 us (5%)
    pallas_call x2, Pallas kernels, relay_sum(): pl.pallas_call(functools.partial(_relay_sum_kernel, n_chip), out_shape=ja...  64.2 us
    all_gather x2, waiting for transfers between devices, to_owners(): return lax.all_gather(arrived, 'dp', axis=0, tiled=True)  47.2 us
    pallas_call x4, Pallas kernels, exchange(): pl.pallas_call(functools.partial(_exchange_kernel, axis, other, n, gather...  46.5 us
    pallas_call x1, Pallas kernels, all_sum(): pl.pallas_call(functools.partial(_allsum_kernel, n_dp, n_expert), out_sha...  38.5 us
    reshape x2, local copies, waits for them, and re-layouts, local(): blocks = slot_rows.reshape(-1, experts_dev, width)  8.36 us
    dot_general x1, matrix products, local(): jnp.einsum('rkd,kfd->rkf', grad_blocks, weight_out, preferred_element_typ...  5.77 us
  transfers between devices with their start and end apart: 2, of which 2 were waited for; matrix products, arithmetic and copies ran while one was open for 6% of the time, Pallas kernels for 4%

profile of v5, /device:TPU:1, one launch (start us, length us, event | category | flops | bytes accessed | tf_op | source)
XLA Modules:
  0.0 283.1 jit_solution(8254270638802850632)
XLA Ops:
  7.2 0.0 copy-start
  7.2 0.0 copy-start.5
  7.2 0.0 all-gather.3.cloned.1.call-start
  7.2 1.7 fusion.52
  8.9 0.2 fusion.39
  9.1 1.3 convolution_convert_fusion.4
  10.4 0.8 reshape.143.x_ref
  11.2 13.7 %shard_map.92 = bf16[32,4,1024]{2,1,0:T(4,128)(2,1)} custom-call(bf16[32,4,1024]{2,1,0:T(4,128)(2,1)} %reshape.143.x_ref), custom_call_target="tpu_custom_call" | custom-call | tf_op jit(solution)/shard_map/pallas_call | solution.py:74
  24.9 1.7 reshape.144
  26.6 0.0 all-gather.3.cloned.1.call-update
  26.7 0.0 all-gather.5.cloned.1.call-start
  26.7 0.0 copy-done.5
  26.7 0.4 convolution_convert_fusion.3
  27.1 0.8 reshape.150.x_ref
  27.9 11.4 %shard_map.95 = bf16[32,4,1024]{2,1,0:T(4,128)(2,1)} custom-call(bf16[32,4,1024]{2,1,0:T(4,128)(2,1)} %reshape.150.x_ref), custom_call_target="tpu_custom_call" | custom-call | tf_op jit(solution)/shard_map/pallas_call | solution.py:74
  39.3 1.7 reshape.151
  41.1 0.0 all-gather.5.cloned.1.call-update
  41.1 0.0 copy-done.3
  41.1 1.0 copy.27
  42.1 23.0 %all-gather.3.cloned.1.call-done = bf16[8,128,1024]{2,1,0:T(8,128)(2,1)} async-done(((bf16[1,128,1024]{2,1,0:T(8,128)(2,1)}), bf16[8,128,1024]{2,1,0:T(8,128)(2,1)}) %all-gather.3.cloned.1.call-update) | async-done | bytes 2097168 | tf_op jit(solution)/shard_map/all_gather | solution.py:291
  65.1 4.1 %reshape.145 = bf16[256,4,1024]{2,1,0:T(4,128)(2,1)} reshape(bf16[8,128,1024]{2,1,0:T(8,128)(2,1)} %all-gather.3.cloned.1.call-done) | data formatting | bytes 4194304 | tf_op jit(solution)/shard_map/reshape | solution.py:299
  69.2 4.3 %copy.34 = bf16[256,4,1024]{0,2,1:T(8,128)(2,1)} copy(bf16[256,4,1024]{2,1,0:T(4,128)(2,1)} %reshape.145) | data formatting | bytes 4194304 | tf_op jit(solution)/shard_map/reshape | solution.py:299
  73.4 0.0 copy-done
  73.4 5.3 %fusion.11 = (bf16[256,4,256]{2,0,1:T(8,128)(2,1)S(1)}, f32[4,256,256]{2,1,0:T(8,128)}) fusion(bf16[256,4,1024]{0,2,1:T(8,128)(2,1)} %copy.34, bf16[4,1024,256]{2,1,0:T(8,128)(2,1)S(1)} %copy-done), kind=kOutput, calls=%fused_computation.27 | convolution fusion | flops 553910272 | bytes 5767168 | tf_op jit(solution)/shard_map/rkd,kdf->rkf/dot_general | solution.py:300
  78.7 24.2 %all-gather.5.cloned.1.call-done = bf16[8,128,1024]{2,1,0:T(8,128)(2,1)} async-done(((bf16[1,128,1024]{2,1,0:T(8,128)(2,1)}), bf16[8,128,1024]{2,1,0:T(8,128)(2,1)}) %all-gather.5.cloned.1.call-update) | async-done | bytes 2097168 | tf_op jit(solution)/shard_map/all_gather | solution.py:291
  102.9 4.1 %reshape.152 = bf16[256,4,1024]{2,1,0:T(4,128)(2,1)} reshape(bf16[8,128,1024]{2,1,0:T(8,128)(2,1)} %all-gather.5.cloned.1.call-done) | data formatting | bytes 4194304 | tf_op jit(solution)/shard_map/reshape | solution.py:313
  107.0 5.8 %fusion.17 = bf16[256,4,256]{2,0,1:T(8,128)(2,1)S(1)} fusion(bf16[4,256,1024]{2,1,0:T(8,128)(2,1)} %param.8, bf16[256,4,1024]{2,1,0:T(4,128)(2,1)} %reshape.152, f32[4,256,256]{2,1,0:T(8,128)} %get-tuple-element.13), kind=kOutput, calls=%fused_computation.33 | convolution fusion | flops 555745280 | bytes 5767168 | tf_op jit(solution)/shard_map/rkd,kfd->rkf/dot_general | solution.py:314
  112.8 0.0 copy-start.2
  112.8 2.1 convert_bitcast_fusion
  114.9 0.0 copy-done.2
  114.9 2.0 convolution_convert_fusion.1
  116.9 0.0 copy-done.6
  116.9 0.7 convert_bitcast_fusion.1
  117.6 2.9 %copy.29 = bf16[256,4,1024]{2,1,0:T(4,128)(2,1)} copy(bf16[256,4,1024]{2,0,1:T(8,128)(2,1)S(1)} %convert_bitcast_fusion.1) | data formatting | bytes 4194304 | tf_op jit(solution)/shard_map/convert_element_type | solution.py:309
  120.6 4.0 %reshape.146.x_ref = bf16[8,128,1024]{2,1,0:T(8,128)(2,1)} reshape(bf16[256,4,1024]{2,1,0:T(4,128)(2,1)} %copy.29) | data formatting | bytes 4194304 | tf_op jit(solution)/shard_map/reshape | solution.py:309
  124.5 27.8 %shard_map.93 = bf16[128,1024]{1,0:T(8,128)(2,1)} custom-call(bf16[8,128,1024]{2,1,0:T(8,128)(2,1)} %reshape.146.x_ref), custom_call_target="tpu_custom_call" | custom-call | tf_op jit(solution)/shard_map/pallas_call | solution.py:144
  152.3 1.8 reshape.147.x_ref
  154.1 10.9 %shard_map.94 = bf16[32,4,1024]{2,1,0:T(4,128)(2,1)} custom-call(bf16[32,4,1024]{2,1,0:T(4,128)(2,1)} %reshape.147.x_ref), custom_call_target="tpu_custom_call" | custom-call | tf_op jit(solution)/shard_map/pallas_call | solution.py:74
  165.0 1.0 reshape.148
  166.0 2.0 convolution_bitcast_fusion.1
  168.0 1.1 fusion.7
  169.1 4.6 %convolution_convert_fusion = bf16[4,256,1024]{2,1,0:T(8,128)(2,1)} fusion(bf16[256,4,256]{2,0,1:T(8,128)(2,1)S(1)} %get-tuple-element.12, bf16[256,4,1024]{2,1,0:T(4,128)(2,1)} %reshape.152), kind=kOutput, calls=%fused_computation.2 | convolution fusion | flops 537919488 | bytes 4718592 | tf_op jit(solution)/shard_map/rkf,rkd->kfd/dot_general | solution.py:319
  173.8 0.0 copy-done.1
  173.8 2.9 %copy.31 = bf16[256,4,1024]{2,1,0:T(4,128)(2,1)} copy(bf16[256,4,1024]{2,0,1:T(8,128)(2,1)S(1)} %copy-done.1) | data formatting | bytes 4194304 | tf_op jit(solution)/shard_map/convert_element_type | solution.py:331
  176.7 4.0 %reshape.153.x_ref = bf16[8,128,1024]{2,1,0:T(8,128)(2,1)} reshape(bf16[256,4,1024]{2,1,0:T(4,128)(2,1)} %copy.31) | data formatting | bytes 4194304 | tf_op jit(solution)/shard_map/reshape | solution.py:331
  180.7 36.4 %shard_map.96 = bf16[128,1024]{1,0:T(8,128)(2,1)} custom-call(bf16[8,128,1024]{2,1,0:T(8,128)(2,1)} %reshape.153.x_ref), custom_call_target="tpu_custom_call" | custom-call | tf_op jit(solution)/shard_map/pallas_call | solution.py:144
  217.1 0.0 copy-start.9
  217.1 1.8 reshape.154.x_ref
  218.9 10.5 %shard_map.97 = bf16[32,4,1024]{2,1,0:T(4,128)(2,1)} custom-call(bf16[32,4,1024]{2,1,0:T(4,128)(2,1)} %reshape.154.x_ref), custom_call_target="tpu_custom_call" | custom-call | tf_op jit(solution)/shard_map/pallas_call | solution.py:74
  229.3 1.0 reshape.155
  230.4 0.0 copy-start.10
  230.4 1.3 fusion.43
  231.6 0.0 copy-done.9
  231.6 0.3 multiply_reduce_fusion.1
  232.0 0.0 copy-start.12
  232.0 0.0 copy-start.13
  232.0 0.0 copy-start.4
  232.0 0.6 copy-done.11
  232.6 0.0 copy-done.12
  232.6 0.0 copy-done.13
  232.6 2.1 convolution_bitcast_fusion.x_ref
  234.8 38.5 %shard_map.98 = f32[32,32,128]{2,1,0:T(8,128)} custom-call(f32[32,32,128]{2,1,0:T(8,128)} %convolution_bitcast_fusion.x_ref), custom_call_target="tpu_custom_call" | custom-call | tf_op jit(solution)/shard_map/pallas_call | solution.py:250
  273.3 2.2 fusion.8
  275.5 0.8 copy.49
  (10 shorter events, 0.0 us)
Async XLA Ops:
  7.2 66.3 %copy-start = (bf16[4,1024,256]{2,1,0:T(8,128)(2,1)S(1)}, bf16[4,1024,256]{2,1,0:T(8,128)(2,1)}, u32[]{:S(2)}) copy-start(bf16[4,1024,256]{2,1,0:T(8,128)(2,1)} %param.7) | copy-start | bytes 6291460
  7.2 19.5 %copy-start.5 = (bf16[1,256,1024]{2,1,0:T(8,128)(2,1)S(1)}, bf16[1,256,1024]{2,1,0:T(8,128)(2,1)}, u32[]{:S(2)}) copy-start(bf16[1,256,1024]{2,1,0:T(8,128)(2,1)} %param.9) | copy-start | bytes 1572868
  7.2 57.9 %all-gather.3.cloned.1.call-start = ((), (), s32[]{:S(2)}) async-start(), calls=%async_computation | async-start | bytes 2359296 | tf_op jit(solution)/shard_map/all_gather | solution.py:291
  11.2 29.9 %copy-start.3 = (bf16[1,256,1024]{2,1,0:T(8,128)(2,1)S(1)}, bf16[1,256,1024]{2,1,0:T(8,128)(2,1)}, u32[]{:S(2)}) copy-start(bf16[1,256,1024]{2,1,0:T(8,128)(2,1)} %param.5) | copy-start | bytes 1572868
  26.7 76.3 %all-gather.5.cloned.1.call-start = ((), (), s32[]{:S(2)}) async-start(), calls=%async_computation.1 | async-start | bytes 2359296 | tf_op jit(solution)/shard_map/all_gather | solution.py:291
  112.8 2.1 copy-start.2
  114.9 2.0 copy-start.6
  169.1 4.6 %copy-start.1 = (bf16[256,4,1024]{2,0,1:T(8,128)(2,1)S(1)}, bf16[256,4,1024]{2,0,1:T(8,128)(2,1)}, u32[]{:S(2)}) copy-start(bf16[256,4,1024]{2,0,1:T(8,128)(2,1)} %convert_bitcast_fusion) | copy-start | bytes 6291460
  217.1 14.6 %copy-start.9 = (f32[256,128]{1,0:T(8,128)S(1)}, f32[256,128]{1,0:T(8,128)}, u32[]{:S(2)}) copy-start(f32[256,128]{1,0:T(8,128)} %convolution_bitcast_fusion.1) | copy-start | bytes 393220
  230.4 2.3 copy-start.10
  231.6 41.6 %copy-start.8 = (bf16[1024,128]{1,0:T(8,128)(2,1)S(1)}, bf16[1024,128]{1,0:T(8,128)(2,1)}, u32[]{:S(2)}) copy-start(bf16[1024,128]{1,0:T(8,128)(2,1)} %param.6) | copy-start | bytes 786436
  231.9 0.7 copy-start.11
  232.0 0.7 copy-start.12
  232.0 0.6 copy-start.13
  232.0 41.3 %copy-start.4 = (f32[256,1024]{1,0:T(8,128)S(1)}, f32[256,1024]{1,0:T(8,128)}, u32[]{:S(2)}) copy-start(f32[256,1024]{1,0:T(8,128)} %fusion.43) | copy-start | bytes 3145732
  273.3 2.2 copy-start.7
Sparse Core Ops, SparseCore 0:
  26.8 38.2 all-gather.2
  67.5 35.3 all-gather.4

commit v6 on v5

--- a/solution.py
+++ b/solution.py
@@ -154,6 +154,74 @@
             pltpu.SemaphoreType.DMA((n_chip,)),
             pltpu.SemaphoreType.DMA((n_chip,)),
             pltpu.SemaphoreType.DMA((n_chip,)),
+        ],
+        compiler_params=pltpu.CompilerParams(collective_id=collective_id, has_side_effects=True),
+    )(x)
+
+
+def _relay_gather_kernel(n_chip, x_ref, o_ref, land, s_off, s_fwd, recv):
+    me = lax.axis_index("dp")
+    fixed = lax.axis_index("expert")
+    core = me % 2
+    chip = me // 2
+    partner = me + 1 - 2 * core
+    mesh_id = pl.DeviceIdType.MESH
+    barrier = pltpu.get_barrier_semaphore()
+    pl.semaphore_signal(barrier, inc=1, device_id=(partner, fixed), device_id_type=mesh_id)
+    for h in range(n_chip):
+        @pl.when(h != chip)
+        def _():
+            pl.semaphore_signal(barrier, inc=1, device_id=(2 * h + core, fixed), device_id_type=mesh_id)
+    pl.semaphore_wait(barrier, n_chip)
+
+    def off_chip(h, slot):
+        return pltpu.make_async_remote_copy(
+            src_ref=x_ref, dst_ref=land.at[slot], send_sem=s_off.at[h], recv_sem=recv.at[slot],
+            device_id=(2 * h + core, fixed), device_id_type=mesh_id)
+
+    def on_chip(h, slot):
+        src = x_ref if h is None else land.at[slot]
+        return pltpu.make_async_remote_copy(
+            src_ref=src, dst_ref=land.at[slot], send_sem=s_fwd.at[slot], recv_sem=recv.at[slot],
+            device_id=(partner, fixed), device_id_type=mesh_id)
+
+    for h in range(n_chip):
+        @pl.when(h != chip)
+        def _():
+            off_chip(h, me).start()
+    on_chip(None, me).start()
+    o_ref[me] = x_ref[...]
+    for h in range(n_chip):
+        @pl.when(h != chip)
+        def _():
+            slot = 2 * h + core
+            off_chip(h, slot).wait_recv()
+            on_chip(h, slot).start()
+            o_ref[slot] = land[slot]
+    for h in range(n_chip):
+        slot = 2 * h + 1 - core
+        on_chip(h, slot).wait_recv()
+        o_ref[slot] = land[slot]
+    for h in range(n_chip):
+        @pl.when(h != chip)
+        def _():
+            off_chip(h, me).wait_send()
+            on_chip(h, 2 * h + core).wait_send()
+    on_chip(None, me).wait_send()
+
+
+def relay_gather(x, n_dp, collective_id):
+    n_chip = n_dp // 2
+    return pl.pallas_call(
+        functools.partial(_relay_gather_kernel, n_chip),
+        out_shape=jax.ShapeDtypeStruct((n_dp,) + x.shape, x.dtype),
+        in_specs=[pl.BlockSpec(memory_space=pltpu.VMEM)],
+        out_specs=pl.BlockSpec(memory_space=pltpu.VMEM),
+        scratch_shapes=[
+            pltpu.VMEM((n_dp,) + x.shape, x.dtype),
+            pltpu.SemaphoreType.DMA((n_chip,)),
+            pltpu.SemaphoreType.DMA((n_dp,)),
+            pltpu.SemaphoreType.DMA((n_dp,)),
         ],
         compiler_params=pltpu.CompilerParams(collective_id=collective_id, has_side_effects=True),
     )(x)
@@ -288,7 +356,7 @@
     def to_owners(local_rows, cid):
         chunks = local_rows.reshape(n_expert, experts_dev, width)
         arrived = exchange(chunks, "expert", n_expert, cid).reshape(local_rows.shape)
-        return lax.all_gather(arrived, "dp", axis=0, tiled=True)
+        return relay_gather(arrived[0], n_dp, cid + 12)
 
     def from_owners(partial_value, cid):
         summed = relay_sum(partial_value, cid + 8)

time: 284 us -> 294 us (1.035)
  Pallas kernels: 149 us -> 218 us
  waiting for transfers between devices: 47.2 us -> 0 us
  between operations: 14.3 us -> 0.82 us
    pallas_call x0 -> x2, Pallas kernels: none -> 55.6 us  [relay_gather(): pl.pallas_call(functools.partial(_relay_gather_kernel, n_chip), out_shape...]
    all_gather x2 -> x0, waiting for transfers between devices: 47.2 us -> none  [to_owners(): return lax.all_gather(arrived, 'dp', axis=0, tiled=True)]
    pallas_call x2, Pallas kernels: 64.2 us -> 77.7 us  [relay_sum(): pl.pallas_call(functools.partial(_relay_sum_kernel, n_chip), out_shape=ja...]
    another operation x2 -> x4, local copies, waits for them, and re-layouts: 2.03 us -> 6.15 us  [the longest x2 3.43 us: to_owners(): return relay_gather(arrived[0], n_dp, cid + 12)]
    reshape x2 -> x0, local copies, waits for them, and re-layouts: 3.43 us -> none  [to_owners(): exchange(chunks, 'expert', n_expert, cid).reshape(local_rows.shape)]
  transfers between devices with their start and end apart: 2 -> 0, of which waited for: 2 -> 0; matrix products, arithmetic and copies ran while one was open for 6% -> 0% of each run, Pallas kernels for 4% -> 0%
where the time goes in v6:
time: 294 us; the launch traced here: 293 us
  Pallas kernels  218 us (74%)
  local copies, waits for them, and re-layouts  40.1 us (14%)
  matrix products  33.5 us (11%)
    pallas_call x2, Pallas kernels, relay_sum(): pl.pallas_call(functools.partial(_relay_sum_kernel, n_chip), out_shape=ja...  77.7 us
    pallas_call x2, Pallas kernels, relay_gather(): pl.pallas_call(functools.partial(_relay_gather_kernel, n_chip), out_shape...  55.6 us
    pallas_call x4, Pallas kernels, exchange(): pl.pallas_call(functools.partial(_exchange_kernel, axis, other, n, gather...  48.4 us
    pallas_call x1, Pallas kernels, all_sum(): pl.pallas_call(functools.partial(_allsum_kernel, n_dp, n_expert), out_sha...  36.5 us
    reshape x2, local copies, waits for them, and re-layouts, local(): blocks = slot_rows.reshape(-1, experts_dev, width)  8.37 us

profile of v6, /device:TPU:1, one launch (start us, length us, event | category | flops | bytes accessed | tf_op | source)
XLA Modules:
  0.0 292.8 jit_solution(377261158560544053)
XLA Ops:
  0.6 0.0 copy-start
  0.6 1.6 fusion.52
  2.3 0.2 fusion.39
  2.5 1.3 convolution_convert_fusion.4
  3.8 0.8 reshape.137.x_ref
  4.6 13.6 %shard_map.92 = bf16[32,4,1024]{2,1,0:T(4,128)(2,1)} custom-call(bf16[32,4,1024]{2,1,0:T(4,128)(2,1)} %reshape.137.x_ref), custom_call_target="tpu_custom_call" | custom-call | tf_op jit(solution)/shard_map/pallas_call | solution.py:74
  18.2 1.7 squeeze_reshape.6.x_ref
  19.9 29.6 %shard_map.93 = bf16[8,128,1024]{2,1,0:T(8,128)(2,1)} custom-call(bf16[128,1024]{1,0:T(8,128)(2,1)} %squeeze_reshape.6.x_ref), custom_call_target="tpu_custom_call" | custom-call | tf_op jit(solution)/shard_map/pallas_call | solution.py:215
  49.6 4.1 %reshape.138 = bf16[256,4,1024]{2,1,0:T(4,128)(2,1)} reshape(bf16[8,128,1024]{2,1,0:T(8,128)(2,1)} %shard_map.93) | data formatting | bytes 4194304 | tf_op jit(solution)/shard_map/reshape | solution.py:367
  53.7 4.3 %copy.27 = bf16[256,4,1024]{0,2,1:T(8,128)(2,1)} copy(bf16[256,4,1024]{2,1,0:T(4,128)(2,1)} %reshape.138) | data formatting | bytes 4194304 | tf_op jit(solution)/shard_map/reshape | solution.py:367
  57.9 0.0 copy-done
  57.9 0.0 copy-start.6
  57.9 5.4 %fusion.11 = (bf16[256,4,256]{2,0,1:T(8,128)(2,1)S(1)}, f32[4,256,256]{2,1,0:T(8,128)}) fusion(bf16[256,4,1024]{0,2,1:T(8,128)(2,1)} %copy.27, bf16[4,1024,256]{2,1,0:T(8,128)(2,1)S(1)} %copy-done), kind=kOutput, calls=%fused_computation.27 | convolution fusion | flops 553910272 | bytes 5767168 | tf_op jit(solution)/shard_map/rkd,kdf->rkf/dot_general | solution.py:368
  63.3 0.0 copy-done.6
  63.3 0.4 convolution_convert_fusion.3
  63.7 0.8 reshape.143.x_ref
  64.5 14.2 %shard_map.96 = bf16[32,4,1024]{2,1,0:T(4,128)(2,1)} custom-call(bf16[32,4,1024]{2,1,0:T(4,128)(2,1)} %reshape.143.x_ref), custom_call_target="tpu_custom_call" | custom-call | tf_op jit(solution)/shard_map/pallas_call | solution.py:74
  78.7 1.7 squeeze_reshape.7.x_ref
  80.4 26.0 %shard_map.97 = bf16[8,128,1024]{2,1,0:T(8,128)(2,1)} custom-call(bf16[128,1024]{1,0:T(8,128)(2,1)} %squeeze_reshape.7.x_ref), custom_call_target="tpu_custom_call" | custom-call | tf_op jit(solution)/shard_map/pallas_call | solution.py:215
  106.4 4.1 %reshape.144 = bf16[256,4,1024]{2,1,0:T(4,128)(2,1)} reshape(bf16[8,128,1024]{2,1,0:T(8,128)(2,1)} %shard_map.97) | data formatting | bytes 4194304 | tf_op jit(solution)/shard_map/reshape | solution.py:381
  110.5 5.7 %fusion.17 = bf16[256,4,256]{2,0,1:T(8,128)(2,1)S(1)} fusion(bf16[4,256,1024]{2,1,0:T(8,128)(2,1)} %param.8, bf16[256,4,1024]{2,1,0:T(4,128)(2,1)} %reshape.144, f32[4,256,256]{2,1,0:T(8,128)} %get-tuple-element.13), kind=kOutput, calls=%fused_computation.33 | convolution fusion | flops 555745280 | bytes 5767168 | tf_op jit(solution)/shard_map/rkd,kfd->rkf/dot_general | solution.py:382
  116.2 0.0 copy-start.4
  116.2 0.7 convert_bitcast_fusion
  117.0 0.0 copy-done.4
  117.0 2.9 %copy.24 = bf16[256,4,1024]{2,1,0:T(4,128)(2,1)} copy(bf16[256,4,1024]{2,0,1:T(8,128)(2,1)S(1)} %convert_bitcast_fusion) | data formatting | bytes 4194304 | tf_op jit(solution)/shard_map/convert_element_type | solution.py:399
  120.0 4.0 %reshape.145.x_ref = bf16[8,128,1024]{2,1,0:T(8,128)(2,1)} reshape(bf16[256,4,1024]{2,1,0:T(4,128)(2,1)} %copy.24) | data formatting | bytes 4194304 | tf_op jit(solution)/shard_map/reshape | solution.py:399
  123.9 44.7 %shard_map.98 = bf16[128,1024]{1,0:T(8,128)(2,1)} custom-call(bf16[8,128,1024]{2,1,0:T(8,128)(2,1)} %reshape.145.x_ref), custom_call_target="tpu_custom_call" | custom-call | tf_op jit(solution)/shard_map/pallas_call | solution.py:144
  168.6 1.8 reshape.146.x_ref
  170.4 10.3 %shard_map.99 = bf16[32,4,1024]{2,1,0:T(4,128)(2,1)} custom-call(bf16[32,4,1024]{2,1,0:T(4,128)(2,1)} %reshape.146.x_ref), custom_call_target="tpu_custom_call" | custom-call | tf_op jit(solution)/shard_map/pallas_call | solution.py:74
  180.7 1.7 reshape.147
  182.4 2.3 convert_bitcast_fusion.1
  184.7 2.9 %copy.22 = bf16[256,4,1024]{2,1,0:T(4,128)(2,1)} copy(bf16[256,4,1024]{2,0,1:T(8,128)(2,1)S(1)} %convert_bitcast_fusion.1) | data formatting | bytes 4194304 | tf_op jit(solution)/shard_map/convert_element_type | solution.py:377
  187.7 4.0 %reshape.139.x_ref = bf16[8,128,1024]{2,1,0:T(8,128)(2,1)} reshape(bf16[256,4,1024]{2,1,0:T(4,128)(2,1)} %copy.22) | data formatting | bytes 4194304 | tf_op jit(solution)/shard_map/reshape | solution.py:377
  191.6 0.0 copy-start.3
  191.6 33.0 %shard_map.94 = bf16[128,1024]{1,0:T(8,128)(2,1)} custom-call(bf16[8,128,1024]{2,1,0:T(8,128)(2,1)} %reshape.139.x_ref), custom_call_target="tpu_custom_call" | custom-call | tf_op jit(solution)/shard_map/pallas_call | solution.py:144
  224.7 1.8 reshape.140.x_ref
  226.4 10.3 %shard_map.95 = bf16[32,4,1024]{2,1,0:T(4,128)(2,1)} custom-call(bf16[32,4,1024]{2,1,0:T(4,128)(2,1)} %reshape.140.x_ref), custom_call_target="tpu_custom_call" | custom-call | tf_op jit(solution)/shard_map/pallas_call | solution.py:74
  236.7 1.0 reshape.141
  237.7 1.3 convolution_bitcast_fusion.1
  239.1 0.0 copy-start.8
  239.1 0.6 copy-done.8
  239.7 0.0 copy-done.3
  239.7 2.5 multiply_reduce_fusion.1
  242.2 1.0 copy.20
  243.2 2.4 convolution_bitcast_fusion.x_ref
  245.6 36.5 %shard_map.100 = f32[32,32,128]{2,1,0:T(8,128)} custom-call(f32[32,32,128]{2,1,0:T(8,128)} %convolution_bitcast_fusion.x_ref), custom_call_target="tpu_custom_call" | custom-call | tf_op jit(solution)/shard_map/pallas_call | solution.py:318
  282.1 0.0 copy-start.1
  282.1 0.0 copy-start.5
  282.2 1.4 fusion.43
  283.5 2.3 fusion.8
  285.8 0.0 copy-done.1
  285.8 0.0 copy-done.5
  285.8 0.0 copy-start.2
  285.8 2.0 convolution_convert_fusion.1
  287.9 1.1 fusion.7
  289.0 0.0 copy-done.2
  289.0 0.0 copy-start.7
  289.0 2.9 %convolution_convert_fusion = bf16[4,256,1024]{2,1,0:T(8,128)(2,1)} fusion(bf16[256,4,256]{2,0,1:T(8,128)(2,1)S(1)} %get-tuple-element.12, bf16[256,4,1024]{2,1,0:T(4,128)(2,1)S(1)} %copy-done.2), kind=kOutput, calls=%fused_computation.2 | convolution fusion | flops 537919488 | bytes 4718592 | tf_op jit(solution)/shard_map/rkf,rkd->kfd/dot_general | solution.py:387
  292.0 0.0 copy-done.7
  292.0 0.8 copy.42
Async XLA Ops:
  0.6 57.3 %copy-start = (bf16[4,1024,256]{2,1,0:T(8,128)(2,1)S(1)}, bf16[4,1024,256]{2,1,0:T(8,128)(2,1)}, u32[]{:S(2)}) copy-start(bf16[4,1024,256]{2,1,0:T(8,128)(2,1)} %param.7) | copy-start | bytes 6291460
  57.9 5.4 %copy-start.6 = (bf16[1,256,1024]{2,1,0:T(8,128)(2,1)S(1)}, bf16[1,256,1024]{2,1,0:T(8,128)(2,1)}, u32[]{:S(2)}) copy-start(bf16[1,256,1024]{2,1,0:T(8,128)(2,1)} %param.9) | copy-start | bytes 1572868
  116.2 0.8 copy-start.4
  191.6 48.1 %copy-start.3 = (bf16[1,256,1024]{2,1,0:T(8,128)(2,1)S(1)}, bf16[1,256,1024]{2,1,0:T(8,128)(2,1)}, u32[]{:S(2)}) copy-start(bf16[1,256,1024]{2,1,0:T(8,128)(2,1)} %param.5) | copy-start | bytes 1572868
  239.1 0.7 copy-start.8
  282.1 3.7 %copy-start.1 = (bf16[256,4,1024]{0,2,1:T(8,128)(2,1)S(1)}, bf16[256,4,1024]{0,2,1:T(8,128)(2,1)}, u32[]{:S(2)}) copy-start(bf16[256,4,1024]{0,2,1:T(8,128)(2,1)} %copy.27) | copy-start | bytes 6291460
  282.1 3.7 %copy-start.5 = (bf16[256,4,256]{2,0,1:T(8,128)(2,1)S(1)}, bf16[256,4,256]{2,0,1:T(8,128)(2,1)}, u32[]{:S(2)}) copy-start(bf16[256,4,256]{2,0,1:T(8,128)(2,1)} %copy-done.4) | copy-start | bytes 1572868
  285.8 3.2 %copy-start.2 = (bf16[256,4,1024]{2,1,0:T(4,128)(2,1)S(1)}, bf16[256,4,1024]{2,1,0:T(4,128)(2,1)}, u32[]{:S(2)}) copy-start(bf16[256,4,1024]{2,1,0:T(4,128)(2,1)} %reshape.144) | copy-start | bytes 6291460
  289.0 2.9 %copy-start.7 = (f32[32,32,128]{2,1,0:T(8,128)S(1)}, f32[32,32,128]{2,1,0:T(8,128)}, u32[]{:S(2)}) copy-start(f32[32,32,128]{2,1,0:T(8,128)} %shard_map.100) | copy-start | bytes 1572868

commit v7 on v4

--- a/solution.py
+++ b/solution.py
@@ -87,6 +87,74 @@
 
 def gelu_exact(values):
     return jax.nn.gelu(values, approximate=False)
+
+
+def _relay_gather_kernel(n_chip, x_ref, o_ref, land, s_off, s_fwd, recv):
+    me = lax.axis_index("dp")
+    fixed = lax.axis_index("expert")
+    core = me % 2
+    chip = me // 2
+    partner = me + 1 - 2 * core
+    mesh_id = pl.DeviceIdType.MESH
+    barrier = pltpu.get_barrier_semaphore()
+    pl.semaphore_signal(barrier, inc=1, device_id=(partner, fixed), device_id_type=mesh_id)
+    for h in range(n_chip):
+        @pl.when(h != chip)
+        def _():
+            pl.semaphore_signal(barrier, inc=1, device_id=(2 * h + core, fixed), device_id_type=mesh_id)
+    pl.semaphore_wait(barrier, n_chip)
+
+    def off_chip(h, slot):
+        return pltpu.make_async_remote_copy(
+            src_ref=x_ref, dst_ref=land.at[slot], send_sem=s_off.at[h], recv_sem=recv.at[slot],
+            device_id=(2 * h + core, fixed), device_id_type=mesh_id)
+
+    def on_chip(h, slot):
+        src = x_ref if h is None else land.at[slot]
+        return pltpu.make_async_remote_copy(
+            src_ref=src, dst_ref=land.at[slot], send_sem=s_fwd.at[slot], recv_sem=recv.at[slot],
+            device_id=(partner, fixed), device_id_type=mesh_id)
+
+    for h in range(n_chip):
+        @pl.when(h != chip)
+        def _():
+            off_chip(h, me).start()
+    on_chip(None, me).start()
+    o_ref[me] = x_ref[...]
+    for h in range(n_chip):
+        @pl.when(h != chip)
+        def _():
+            slot = 2 * h + core
+            off_chip(h, slot).wait_recv()
+            on_chip(h, slot).start()
+            o_ref[slot] = land[slot]
+    for h in range(n_chip):
+        slot = 2 * h + 1 - core
+        on_chip(h, slot).wait_recv()
+        o_ref[slot] = land[slot]
+    for h in range(n_chip):
+        @pl.when(h != chip)
+        def _():
+            off_chip(h, me).wait_send()
+            on_chip(h, 2 * h + core).wait_send()
+    on_chip(None, me).wait_send()
+
+
+def relay_gather(x, n_dp, collective_id):
+    n_chip = n_dp // 2
+    return pl.pallas_call(
+        functools.partial(_relay_gather_kernel, n_chip),
+        out_shape=jax.ShapeDtypeStruct((n_dp,) + x.shape, x.dtype),
+        in_specs=[pl.BlockSpec(memory_space=pltpu.VMEM)],
+        out_specs=pl.BlockSpec(memory_space=pltpu.VMEM),
+        scratch_shapes=[
+            pltpu.VMEM((n_dp,) + x.shape, x.dtype),
+            pltpu.SemaphoreType.DMA((n_chip,)),
+            pltpu.SemaphoreType.DMA((n_dp,)),
+            pltpu.SemaphoreType.DMA((n_dp,)),
+        ],
+        compiler_params=pltpu.CompilerParams(collective_id=collective_id, has_side_effects=True),
+    )(x)
 
 
 def _allsum_kernel(n_dp, n_ex, x_ref, o_ref, land1, land2, land3, red1, red2, s1, r1, s2, r2, s3, r3):
@@ -218,6 +286,8 @@
     def to_owners(local_rows, cid):
         chunks = local_rows.reshape(n_expert, experts_dev, width)
         arrived = exchange(chunks, "expert", n_expert, cid).reshape(local_rows.shape)
+        if cid == 1:
+            return relay_gather(arrived[0], n_dp, cid + 12)
         return lax.all_gather(arrived, "dp", axis=0, tiled=True)
 
     def from_owners(partial_value, cid):
@@ -226,6 +296,8 @@
         return exchange(chunks, "expert", n_expert, cid).reshape(summed.shape)
 
     slot_rows = to_owners(slots, 0)
+    grad_rows = to_owners(grad_slots, 1)
+    slot_rows, grad_rows = lax.optimization_barrier((slot_rows, grad_rows))
     blocks = slot_rows.reshape(-1, experts_dev, width)
     pre_act = jnp.einsum("rkd,kdf->rkf", blocks, weight_in, preferred_element_type=jnp.float32)
     hidden = gelu_exact(pre_act).astype(jnp.bfloat16)
@@ -239,7 +311,6 @@
         partial_value.astype(jnp.bfloat16).reshape(slot_rows.shape),
     )
     expert_outs = from_owners(partial_value, 2)
-    grad_rows = to_owners(grad_slots, 1)
     grad_blocks = grad_rows.reshape(blocks.shape)
     grad_hidden = jnp.einsum(
         "rkd,kfd->rkf", grad_blocks, weight_out, preferred_element_type=jnp.float32

time: 254 us -> 259 us (1.020)
  Pallas kernels: 81.6 us -> 127 us
  waiting for transfers between devices: 85.4 us -> 45.4 us
    pallas_call x0 -> x1, Pallas kernels: none -> 45.5 us  [relay_gather(): pl.pallas_call(functools.partial(_relay_gather_kernel, n_chip), out_shape...]
    all_gather x2 -> x1, waiting for transfers between devices: 40.3 us -> 0.02 us  [to_owners(): return lax.all_gather(arrived, 'dp', axis=0, tiled=True)]
  transfers between devices with their start and end apart: 4 -> 3, of which waited for: 4 -> 2; matrix products, arithmetic and copies ran while one was open for 22% -> 13% of each run, Pallas kernels for 9% -> 26%
where the time goes in v7:
time: 259 us; the launch traced here: 258 us
  Pallas kernels  127 us (49%)
  waiting for transfers between devices  45.4 us (18%)
  local copies, waits for them, and re-layouts  40.4 us (16%)
  matrix products  30.9 us (12%)
  between operations  14 us (5%)
    pallas_call x4, Pallas kernels, exchange(): pl.pallas_call(functools.partial(_exchange_kernel, axis, other, n, gather...  46.8 us
    pallas_call x1, Pallas kernels, relay_gather(): pl.pallas_call(functools.partial(_relay_gather_kernel, n_chip), out_shape...  45.5 us
    reduce_scatter x2, waiting for transfers between devices, from_owners(): lax.psum_scatter(partial_value, 'dp', scatter_dimension=0, tiled=True)  45.3 us
    pallas_call x1, Pallas kernels, all_sum(): pl.pallas_call(functools.partial(_allsum_kernel, n_dp, n_expert), out_sha...  34.5 us
    reshape x2, local copies, waits for them, and re-layouts, local(): blocks = slot_rows.reshape(-1, experts_dev, width)  8.39 us
    dot_general x1, matrix products, local(): jnp.einsum('rkd,kfd->rkf', grad_blocks, weight_out, preferred_element_typ...  5.73 us
    dot_general x1, matrix products, local(): jnp.einsum('rkd,kdf->rkf', blocks, weight_in, preferred_element_type=jnp....  5.45 us
  transfers between devices with their start and end apart: 3, of which 2 were waited for; matrix products, arithmetic and copies ran while one was open for 13% of the time, Pallas kernels for 26%

profile of v7, /device:TPU:1, one launch (start us, length us, event | category | flops | bytes accessed | tf_op | source)
XLA Modules:
  0.0 257.9 jit_solution(4045662087618052343)
XLA Ops:
  7.2 0.0 copy-start
  7.2 0.0 copy-start.5
  7.2 0.0 all-gather.2.cloned.1.call-start
  7.2 1.7 fusion.52
  8.9 0.2 fusion.39
  9.1 1.3 convolution_convert_fusion.4
  10.4 0.8 reshape.140.x_ref
  11.2 13.6 %shard_map.92 = bf16[32,4,1024]{2,1,0:T(4,128)(2,1)} custom-call(bf16[32,4,1024]{2,1,0:T(4,128)(2,1)} %reshape.140.x_ref), custom_call_target="tpu_custom_call" | custom-call | tf_op jit(solution)/shard_map/pallas_call | solution.py:74
  24.9 1.7 reshape.141
  26.6 0.0 all-gather.2.cloned.1.call-update
  26.6 0.0 reduce-scatter.3.cloned.1.call-start
  26.6 0.0 copy-done.5
  26.7 0.4 convolution_convert_fusion.3
  27.0 0.8 reshape.143.x_ref
  27.8 11.4 %shard_map.93 = bf16[32,4,1024]{2,1,0:T(4,128)(2,1)} custom-call(bf16[32,4,1024]{2,1,0:T(4,128)(2,1)} %reshape.143.x_ref), custom_call_target="tpu_custom_call" | custom-call | tf_op jit(solution)/shard_map/pallas_call | solution.py:74
  39.3 1.7 squeeze_reshape.3.x_ref
  41.0 45.5 %shard_map.94 = bf16[8,128,1024]{2,1,0:T(8,128)(2,1)} custom-call(bf16[128,1024]{1,0:T(8,128)(2,1)} %squeeze_reshape.3.x_ref), custom_call_target="tpu_custom_call" | custom-call | tf_op jit(solution)/shard_map/pallas_call | solution.py:145
  86.5 0.0 all-gather.2.cloned.1.call-done
  86.6 4.1 %reshape.144 = bf16[256,4,1024]{2,1,0:T(4,128)(2,1)} reshape(bf16[8,128,1024]{2,1,0:T(8,128)(2,1)} %all-gather.2.cloned.1.call-done) | data formatting | bytes 4194304 | tf_op jit(solution)/shard_map/reshape | solution.py:301
  90.7 4.3 %copy.34 = bf16[256,4,1024]{0,2,1:T(8,128)(2,1)} copy(bf16[256,4,1024]{2,1,0:T(4,128)(2,1)} %reshape.144) | data formatting | bytes 4194304 | tf_op jit(solution)/shard_map/reshape | solution.py:301
  94.9 0.0 copy-done
  95.0 5.4 %fusion.11 = (bf16[256,4,256]{2,0,1:T(8,128)(2,1)S(1)}, f32[4,256,256]{2,1,0:T(8,128)}) fusion(bf16[256,4,1024]{0,2,1:T(8,128)(2,1)} %copy.34, bf16[4,1024,256]{2,1,0:T(8,128)(2,1)S(1)} %copy-done), kind=kOutput, calls=%fused_computation.27 | convolution fusion | flops 553910272 | bytes 5767168 | tf_op jit(solution)/shard_map/rkd,kdf->rkf/dot_general | solution.py:302
  100.4 0.0 copy-done.7
  100.4 0.7 convert_bitcast_fusion.1
  101.1 2.9 %copy.29 = bf16[256,4,1024]{2,1,0:T(4,128)(2,1)} copy(bf16[256,4,1024]{2,0,1:T(8,128)(2,1)S(1)} %convert_bitcast_fusion.1) | data formatting | bytes 4194304 | tf_op jit(solution)/shard_map/convert_element_type | solution.py:311
  104.1 4.0 %reshape.145 = bf16[8,128,1024]{2,1,0:T(8,128)(2,1)} reshape(bf16[256,4,1024]{2,1,0:T(4,128)(2,1)} %copy.29) | data formatting | bytes 4194304 | tf_op jit(solution)/shard_map/reshape | solution.py:311
  108.1 0.0 reduce-scatter.3.cloned.1.call-update
  108.1 0.2 reduce-scatter.5.cloned.1.call-start
  108.3 4.1 %reshape.148 = bf16[256,4,1024]{2,1,0:T(4,128)(2,1)} reshape(bf16[8,128,1024]{2,1,0:T(8,128)(2,1)} %shard_map.94) | data formatting | bytes 4194304 | tf_op jit(solution)/shard_map/reshape | solution.py:314
  112.4 5.7 %fusion.17 = bf16[256,4,256]{2,0,1:T(8,128)(2,1)S(1)} fusion(bf16[4,256,1024]{2,1,0:T(8,128)(2,1)} %param.8, bf16[256,4,1024]{2,1,0:T(4,128)(2,1)} %reshape.148, f32[4,256,256]{2,1,0:T(8,128)} %get-tuple-element.17), kind=kOutput, calls=%fused_computation.33 | convolution fusion | flops 555745280 | bytes 5767168 | tf_op jit(solution)/shard_map/rkd,kfd->rkf/dot_general | solution.py:315
  118.2 0.0 copy-start.4
  118.2 0.7 convert_bitcast_fusion
  118.9 0.0 copy-done.4
  118.9 2.9 %copy.31 = bf16[256,4,1024]{2,1,0:T(4,128)(2,1)} copy(bf16[256,4,1024]{2,0,1:T(8,128)(2,1)S(1)} %convert_bitcast_fusion) | data formatting | bytes 4194304 | tf_op jit(solution)/shard_map/convert_element_type | solution.py:332
  121.9 3.9 %reshape.149 = bf16[8,128,1024]{2,1,0:T(8,128)(2,1)} reshape(bf16[256,4,1024]{2,1,0:T(4,128)(2,1)} %copy.31) | data formatting | bytes 4194304 | tf_op jit(solution)/shard_map/reshape | solution.py:332
  125.8 0.0 reduce-scatter.5.cloned.1.call-update
  125.9 1.0 copy-done.2
  126.9 1.0 copy.27
  127.9 3.9 %convolution_convert_fusion.1 = bf16[4,1024,256]{2,1,0:T(8,128)(2,1)} fusion(bf16[256,4,1024]{0,2,1:T(8,128)(2,1)} %copy.34, bf16[256,4,256]{2,0,1:T(8,128)(2,1)} %copy-done.4), kind=kOutput, calls=%fused_computation.3 | convolution fusion | flops 537919488 | bytes 4718592 | tf_op jit(solution)/shard_map/rkd,rkf->kdf/dot_general | solution.py:323
  131.8 0.0 copy-done.1
  131.8 2.9 %convolution_convert_fusion = bf16[4,256,1024]{2,1,0:T(8,128)(2,1)} fusion(bf16[256,4,256]{2,0,1:T(8,128)(2,1)S(1)} %get-tuple-element.16, bf16[256,4,1024]{2,1,0:T(4,128)(2,1)S(1)} %copy-done.1), kind=kOutput, calls=%fused_computation.2 | convolution fusion | flops 537919488 | bytes 4718592 | tf_op jit(solution)/shard_map/rkf,rkd->kfd/dot_general | solution.py:320
  134.7 16.0 %reduce-scatter.3.cloned.1.call-done = bf16[1,128,1024]{2,1,0:T(8,128)(2,1)} async-done(((bf16[8,128,1024]{2,1,0:T(8,128)(2,1)}), bf16[1,128,1024]{2,1,0:T(8,128)(2,1)}) %reduce-scatter.3.cloned.1.call-update) | async-done | bytes 262160 | tf_op jit(solution)/shard_map/reduce_scatter | solution.py:294
  150.7 1.8 reshape.146.x_ref
  152.5 11.1 %shard_map.95 = bf16[32,4,1024]{2,1,0:T(4,128)(2,1)} custom-call(bf16[32,4,1024]{2,1,0:T(4,128)(2,1)} %reshape.146.x_ref), custom_call_target="tpu_custom_call" | custom-call | tf_op jit(solution)/shard_map/pallas_call | solution.py:74
  163.6 1.0 reshape.147
  164.7 1.2 fusion.7
  165.8 0.0 copy-done.6
  165.8 1.0 convolution_bitcast_fusion.1
  166.8 29.3 %reduce-scatter.5.cloned.1.call-done = bf16[1,128,1024]{2,1,0:T(8,128)(2,1)} async-done(((bf16[8,128,1024]{2,1,0:T(8,128)(2,1)}), bf16[1,128,1024]{2,1,0:T(8,128)(2,1)}) %reduce-scatter.5.cloned.1.call-update) | async-done | bytes 262160 | tf_op jit(solution)/shard_map/reduce_scatter | solution.py:294
  196.1 1.8 reshape.150.x_ref
  197.8 10.6 %shard_map.96 = bf16[32,4,1024]{2,1,0:T(4,128)(2,1)} custom-call(bf16[32,4,1024]{2,1,0:T(4,128)(2,1)} %reshape.150.x_ref), custom_call_target="tpu_custom_call" | custom-call | tf_op jit(solution)/shard_map/pallas_call | solution.py:74
  208.5 1.0 reshape.151
  209.5 0.0 copy-start.11
  209.5 1.3 fusion.43
  210.8 0.3 multiply_reduce_fusion.1
  211.1 0.0 copy-start.13
  211.1 0.0 copy-start.14
  211.1 0.0 copy-start.3
  211.1 0.6 copy-done.12
  211.7 0.0 copy-done.14
  211.8 2.1 convolution_bitcast_fusion.x_ref
  213.9 34.5 %shard_map.97 = f32[32,32,128]{2,1,0:T(8,128)} custom-call(f32[32,32,128]{2,1,0:T(8,128)} %convolution_bitcast_fusion.x_ref), custom_call_target="tpu_custom_call" | custom-call | tf_op jit(solution)/shard_map/pallas_call | solution.py:248
  248.4 2.2 fusion.8
  250.6 0.8 copy.49
  (14 shorter events, 0.0 us)
Async XLA Ops:
  7.2 87.8 %copy-start = (bf16[4,1024,256]{2,1,0:T(8,128)(2,1)S(1)}, bf16[4,1024,256]{2,1,0:T(8,128)(2,1)}, u32[]{:S(2)}) copy-start(bf16[4,1024,256]{2,1,0:T(8,128)(2,1)} %param.7) | copy-start | bytes 6291460
  7.2 19.5 %copy-start.5 = (bf16[1,256,1024]{2,1,0:T(8,128)(2,1)S(1)}, bf16[1,256,1024]{2,1,0:T(8,128)(2,1)}, u32[]{:S(2)}) copy-start(bf16[1,256,1024]{2,1,0:T(8,128)(2,1)} %param.9) | copy-start | bytes 1572868
  7.2 79.4 %all-gather.2.cloned.1.call-start = ((), (), s32[]{:S(2)}) async-start(), calls=%async_computation.2 | async-start | bytes 2359296 | tf_op jit(solution)/shard_map/all_gather | solution.py:291
  26.6 124.1 %reduce-scatter.3.cloned.1.call-start = ((), (), s32[]{:S(2)}) async-start(), calls=%async_computation.3 | async-start | bytes 2359296 | tf_op jit(solution)/shard_map/reduce_scatter | solution.py:294
  95.0 5.5 %copy-start.7 = (bf16[4,256,1024]{2,1,0:T(8,128)(2,1)S(1)}, bf16[4,256,1024]{2,1,0:T(8,128)(2,1)}, u32[]{:S(2)}) copy-start(bf16[4,256,1024]{2,1,0:T(8,128)(2,1)} %param.8) | copy-start | bytes 6291460
  108.1 88.0 %reduce-scatter.5.cloned.1.call-start = ((), (), s32[]{:S(2)}) async-start(), calls=%async_computation.4 | async-start | bytes 2359296 | tf_op jit(solution)/shard_map/reduce_scatter | solution.py:294
  118.2 0.8 copy-start.4
  125.8 1.0 copy-start.2
  127.9 3.9 %copy-start.1 = (bf16[256,4,1024]{2,1,0:T(4,128)(2,1)S(1)}, bf16[256,4,1024]{2,1,0:T(4,128)(2,1)}, u32[]{:S(2)}) copy-start(bf16[256,4,1024]{2,1,0:T(4,128)(2,1)} %reshape.148) | copy-start | bytes 6291460
  134.7 31.1 %copy-start.6 = (bf16[1,256,1024]{2,1,0:T(8,128)(2,1)S(1)}, bf16[1,256,1024]{2,1,0:T(8,128)(2,1)}, u32[]{:S(2)}) copy-start(bf16[1,256,1024]{2,1,0:T(8,128)(2,1)} %param.9) | copy-start | bytes 1572868
  166.8 44.0 %copy-start.10 = (f32[256,128]{1,0:T(8,128)S(1)}, f32[256,128]{1,0:T(8,128)}, u32[]{:S(2)}) copy-start(f32[256,128]{1,0:T(8,128)} %convolution_bitcast_fusion.1) | copy-start | bytes 393220
  209.5 2.3 copy-start.11
  210.8 37.6 %copy-start.9 = (bf16[1024,128]{1,0:T(8,128)(2,1)S(1)}, bf16[1024,128]{1,0:T(8,128)(2,1)}, u32[]{:S(2)}) copy-start(bf16[1024,128]{1,0:T(8,128)(2,1)} %param.6) | copy-start | bytes 786436
  211.1 0.7 copy-start.12
  211.1 0.7 copy-start.13
  211.1 0.6 copy-start.14
  211.1 37.3 %copy-start.3 = (f32[256,1024]{1,0:T(8,128)S(1)}, f32[256,1024]{1,0:T(8,128)}, u32[]{:S(2)}) copy-start(f32[256,1024]{1,0:T(8,128)} %fusion.43) | copy-start | bytes 3145732
  248.4 2.2 copy-start.8
Sparse Core Ops, SparseCore 0:
  26.7 58.7 all-gather.1
  108.2 42.4 reduce-scatter.2
  153.3 42.7 reduce-scatter.4

commit v8 on v4

--- a/solution.py
+++ b/solution.py
@@ -80,6 +80,64 @@
             pltpu.VMEM(out_shape.shape, x.dtype),
             pltpu.SemaphoreType.DMA((n,)),
             pltpu.SemaphoreType.DMA((n,)),
+        ],
+        compiler_params=pltpu.CompilerParams(collective_id=collective_id, has_side_effects=True),
+    )(x)
+
+
+def _row_exchange_kernel(n, rows, x_ref, o_ref, land, send_sem, recv_sem, own_sem):
+    me = lax.axis_index("expert")
+    fixed = lax.axis_index("dp")
+    mesh_id = pl.DeviceIdType.MESH
+    barrier = pltpu.get_barrier_semaphore()
+
+    @pl.loop(0, n)
+    def _(j):
+        @pl.when(j != me)
+        def _():
+            pl.semaphore_signal(barrier, inc=1, device_id=(fixed, j), device_id_type=mesh_id)
+
+    pl.semaphore_wait(barrier, n - 1)
+
+    def block(ref, j):
+        return ref.at[pl.ds(j * rows, rows)]
+
+    def copy_to(j, slot):
+        return pltpu.make_async_remote_copy(
+            src_ref=block(x_ref, j), dst_ref=block(land, slot), send_sem=send_sem.at[j],
+            recv_sem=recv_sem.at[slot], device_id=(fixed, j), device_id_type=mesh_id)
+
+    @pl.loop(0, n)
+    def _(j):
+        @pl.when(j != me)
+        def _():
+            copy_to(j, me).start()
+
+    own = pltpu.make_async_copy(block(x_ref, me), block(land, me), own_sem)
+    own.start()
+
+    @pl.loop(0, n)
+    def _(j):
+        @pl.when(j != me)
+        def _():
+            copy_to(j, j).wait_recv()
+            copy_to(j, me).wait_send()
+
+    own.wait()
+    o_ref[...] = land[...]
+
+
+def row_exchange(x, n, collective_id):
+    return pl.pallas_call(
+        functools.partial(_row_exchange_kernel, n, x.shape[0] // n),
+        out_shape=jax.ShapeDtypeStruct(x.shape, x.dtype),
+        in_specs=[pl.BlockSpec(memory_space=pltpu.VMEM)],
+        out_specs=pl.BlockSpec(memory_space=pltpu.VMEM),
+        scratch_shapes=[
+            pltpu.VMEM(x.shape, x.dtype),
+            pltpu.SemaphoreType.DMA((n,)),
+            pltpu.SemaphoreType.DMA((n,)),
+            pltpu.SemaphoreType.DMA(()),
         ],
         compiler_params=pltpu.CompilerParams(collective_id=collective_id, has_side_effects=True),
     )(x)
@@ -216,14 +274,12 @@
     ).astype(jnp.bfloat16)
 
     def to_owners(local_rows, cid):
-        chunks = local_rows.reshape(n_expert, experts_dev, width)
-        arrived = exchange(chunks, "expert", n_expert, cid).reshape(local_rows.shape)
+        arrived = row_exchange(local_rows[0], n_expert, cid)[None]
         return lax.all_gather(arrived, "dp", axis=0, tiled=True)
 
     def from_owners(partial_value, cid):
         summed = lax.psum_scatter(partial_value, "dp", scatter_dimension=0, tiled=True)
-        chunks = summed.reshape(n_expert, experts_dev, width)
-        return exchange(chunks, "expert", n_expert, cid).reshape(summed.shape)
+        return row_exchange(summed[0], n_expert, cid)[None]
 
     slot_rows = to_owners(slots, 0)
     blocks = slot_rows.reshape(-1, experts_dev, width)

time: 254 us -> 250 us (0.984)
  local copies, waits for them, and re-layouts: 40.4 us -> 29.7 us
  matrix products: 30.8 us -> 35.9 us
    reshape x6 -> x0, local copies, waits for them, and re-layouts: 8.56 us -> none  [the longest x2 3.51 us: from_owners(): chunks = summed.reshape(n_expert, experts_dev, width)]
  transfers between devices with their start and end apart: 4 -> 4, of which waited for: 4 -> 4; matrix products, arithmetic and copies ran while one was open for 22% -> 21% of each run, Pallas kernels for 9% -> 9%
where the time goes in v8:
time: 250 us
  waiting for transfers between devices  87.8 us (35%)
  Pallas kernels  81.6 us (33%)
  matrix products  35.9 us (14%)
  local copies, waits for them, and re-layouts  29.7 us (12%)
  between operations  13.9 us (6%)
    pallas_call x4, Pallas kernels, row_exchange(): pl.pallas_call(functools.partial(_row_exchange_kernel, n, x.shape[0] // n...  47.3 us
    reduce_scatter x2, waiting for transfers between devices, from_owners(): lax.psum_scatter(partial_value, 'dp', scatter_dimension=0, tiled=True)  46.5 us
    all_gather x2, waiting for transfers between devices, to_owners(): return lax.all_gather(arrived, 'dp', axis=0, tiled=True)  41.3 us
    pallas_call x1, Pallas kernels, all_sum(): pl.pallas_call(functools.partial(_allsum_kernel, n_dp, n_expert), out_sha...  34.3 us
    reshape x2, local copies, waits for them, and re-layouts, local(): blocks = slot_rows.reshape(-1, experts_dev, width)  8.36 us
    dot_general x1, matrix products, local(): jnp.einsum('rkd,kfd->rkf', grad_blocks, weight_out, preferred_element_typ...  5.73 us
    dot_general x1, matrix products, local(): jnp.einsum('rkd,kdf->rkf', blocks, weight_in, preferred_element_type=jnp....  5.45 us
  transfers between devices with their start and end apart: 4, of which 4 were waited for; matrix products, arithmetic and copies ran while one was open for 21% of the time, Pallas kernels for 9%

profile of v8, /device:TPU:1, one launch (start us, length us, event | category | flops | bytes accessed | tf_op | source)
XLA Modules:
  0.0 249.5 jit_solution(3618187576643594085)
XLA Ops:
  7.2 0.0 copy-start
  7.2 0.0 copy-start.5
  7.2 0.0 all-gather.5.cloned.1.call-start
  7.2 1.7 fusion.52
  8.9 0.2 fusion.39
  9.1 2.0 convolution_convert_fusion.4.x_ref
  11.1 13.6 %shard_map.92 = bf16[128,1024]{1,0:T(8,128)(2,1)} custom-call(bf16[128,1024]{1,0:T(8,128)(2,1)} %convolution_convert_fusion.4.x_ref), custom_call_target="tpu_custom_call" | custom-call | tf_op jit(solution)/shard_map/pallas_call | solution.py:131
  24.8 0.0 all-gather.5.cloned.1.call-update
  24.8 0.0 all-gather.7.cloned.1.call-start
  24.8 0.0 copy-done.5
  24.8 1.1 convolution_convert_fusion.3.x_ref
  25.9 11.4 %shard_map.94 = bf16[128,1024]{1,0:T(8,128)(2,1)} custom-call(bf16[128,1024]{1,0:T(8,128)(2,1)} %convolution_convert_fusion.3.x_ref), custom_call_target="tpu_custom_call" | custom-call | tf_op jit(solution)/shard_map/pallas_call | solution.py:131
  37.3 0.0 all-gather.7.cloned.1.call-update
  37.4 0.0 reduce-scatter.3.cloned.1.call-start
  37.4 27.0 %all-gather.5.cloned.1.call-done = bf16[1024,1024]{1,0:T(8,128)(2,1)} async-done(((bf16[128,1024]{1,0:T(8,128)(2,1)}), bf16[1024,1024]{1,0:T(8,128)(2,1)}) %all-gather.5.cloned.1.call-update) | async-done | bytes 2097168 | tf_op jit(solution)/shard_map/all_gather | solution.py:278
  64.4 4.1 %reshape.119 = bf16[256,4,1024]{2,1,0:T(4,128)(2,1)} reshape(bf16[1024,1024]{1,0:T(8,128)(2,1)} %all-gather.5.cloned.1.call-done) | data formatting | bytes 4194304 | tf_op jit(solution)/shard_map/reshape | solution.py:285
  68.5 4.3 %copy.27 = bf16[256,4,1024]{0,2,1:T(8,128)(2,1)} copy(bf16[256,4,1024]{2,1,0:T(4,128)(2,1)} %reshape.119) | data formatting | bytes 4194304 | tf_op jit(solution)/shard_map/reshape | solution.py:285
  72.8 0.0 copy-done
  72.8 0.0 copy-start.6
  72.8 5.4 %fusion.11 = (bf16[256,4,256]{2,0,1:T(8,128)(2,1)S(1)}, f32[4,256,256]{2,1,0:T(8,128)}) fusion(bf16[256,4,1024]{0,2,1:T(8,128)(2,1)} %copy.27, bf16[4,1024,256]{2,1,0:T(8,128)(2,1)S(1)} %copy-done), kind=kOutput, calls=%fused_computation.27 | convolution fusion | flops 553910272 | bytes 5767168 | tf_op jit(solution)/shard_map/rkd,kdf->rkf/dot_general | solution.py:286
  78.2 0.0 copy-done.6
  78.2 0.7 convert_bitcast_fusion.1
  79.0 2.9 %copy.22 = bf16[256,4,1024]{2,1,0:T(4,128)(2,1)} copy(bf16[256,4,1024]{2,0,1:T(8,128)(2,1)S(1)} %convert_bitcast_fusion.1) | data formatting | bytes 4194304 | tf_op jit(solution)/shard_map/convert_element_type | solution.py:295
  81.9 4.0 %reshape.120 = bf16[8,128,1024]{2,1,0:T(8,128)(2,1)} reshape(bf16[256,4,1024]{2,1,0:T(4,128)(2,1)} %copy.22) | data formatting | bytes 4194304 | tf_op jit(solution)/shard_map/reshape | solution.py:295
  85.9 0.0 reduce-scatter.3.cloned.1.call-update
  85.9 0.2 reduce-scatter.5.cloned.1.call-start
  86.1 14.3 %all-gather.7.cloned.1.call-done = bf16[1024,1024]{1,0:T(8,128)(2,1)} async-done(((bf16[128,1024]{1,0:T(8,128)(2,1)}), bf16[1024,1024]{1,0:T(8,128)(2,1)}) %all-gather.7.cloned.1.call-update) | async-done | bytes 2097168 | tf_op jit(solution)/shard_map/all_gather | solution.py:278
  100.4 4.1 %reshape.122 = bf16[256,4,1024]{2,1,0:T(4,128)(2,1)} reshape(bf16[1024,1024]{1,0:T(8,128)(2,1)} %all-gather.7.cloned.1.call-done) | data formatting | bytes 4194304 | tf_op jit(solution)/shard_map/reshape | solution.py:299
  104.5 5.7 %fusion.17 = bf16[256,4,256]{2,0,1:T(8,128)(2,1)S(1)} fusion(bf16[4,256,1024]{2,1,0:T(8,128)(2,1)} %param.8, bf16[256,4,1024]{2,1,0:T(4,128)(2,1)} %reshape.122, f32[4,256,256]{2,1,0:T(8,128)} %get-tuple-element.13), kind=kOutput, calls=%fused_computation.33 | convolution fusion | flops 555745280 | bytes 5767168 | tf_op jit(solution)/shard_map/rkd,kfd->rkf/dot_general | solution.py:300
  110.2 0.0 copy-start.4
  110.2 0.7 convert_bitcast_fusion
  111.0 0.0 copy-done.4
  111.0 2.9 %copy.24 = bf16[256,4,1024]{2,1,0:T(4,128)(2,1)} copy(bf16[256,4,1024]{2,0,1:T(8,128)(2,1)S(1)} %convert_bitcast_fusion) | data formatting | bytes 4194304 | tf_op jit(solution)/shard_map/convert_element_type | solution.py:317
  114.0 3.9 %reshape.123 = bf16[8,128,1024]{2,1,0:T(8,128)(2,1)} reshape(bf16[256,4,1024]{2,1,0:T(4,128)(2,1)} %copy.24) | data formatting | bytes 4194304 | tf_op jit(solution)/shard_map/reshape | solution.py:317
  117.9 0.0 reduce-scatter.5.cloned.1.call-update
  117.9 1.0 copy-done.2
  119.0 1.0 copy.20
  120.0 3.9 %convolution_convert_fusion.1 = bf16[4,1024,256]{2,1,0:T(8,128)(2,1)} fusion(bf16[256,4,1024]{0,2,1:T(8,128)(2,1)} %copy.27, bf16[256,4,256]{2,0,1:T(8,128)(2,1)} %copy-done.4), kind=kOutput, calls=%fused_computation.3 | convolution fusion | flops 537919488 | bytes 4718592 | tf_op jit(solution)/shard_map/rkd,rkf->kdf/dot_general | solution.py:308
  123.9 0.0 copy-done.1
  123.9 2.9 %convolution_convert_fusion = bf16[4,256,1024]{2,1,0:T(8,128)(2,1)} fusion(bf16[256,4,256]{2,0,1:T(8,128)(2,1)S(1)} %get-tuple-element.12, bf16[256,4,1024]{2,1,0:T(4,128)(2,1)S(1)} %copy-done.1), kind=kOutput, calls=%fused_computation.2 | convolution fusion | flops 537919488 | bytes 4718592 | tf_op jit(solution)/shard_map/rkf,rkd->kfd/dot_general | solution.py:305
  126.8 16.1 %reduce-scatter.3.cloned.1.call-done = bf16[1,128,1024]{2,1,0:T(8,128)(2,1)} async-done(((bf16[8,128,1024]{2,1,0:T(8,128)(2,1)}), bf16[1,128,1024]{2,1,0:T(8,128)(2,1)}) %reduce-scatter.3.cloned.1.call-update) | async-done | bytes 262160 | tf_op jit(solution)/shard_map/reduce_scatter | solution.py:281
  142.9 11.0 %shard_map.93 = bf16[128,1024]{1,0:T(8,128)(2,1)} custom-call(bf16[128,1024]{1,0:T(8,128)(2,1)} %bitcast.142), custom_call_target="tpu_custom_call" | custom-call | tf_op jit(solution)/shard_map/pallas_call | solution.py:131
  153.9 2.1 fusion.7
  156.0 1.4 convolution_bitcast_fusion.1
  157.5 0.0 copy-start.9
  157.5 30.4 %reduce-scatter.5.cloned.1.call-done = bf16[1,128,1024]{2,1,0:T(8,128)(2,1)} async-done(((bf16[8,128,1024]{2,1,0:T(8,128)(2,1)}), bf16[1,128,1024]{2,1,0:T(8,128)(2,1)}) %reduce-scatter.5.cloned.1.call-update) | async-done | bytes 262160 | tf_op jit(solution)/shard_map/reduce_scatter | solution.py:281
  187.8 11.2 %shard_map.95 = bf16[128,1024]{1,0:T(8,128)(2,1)} custom-call(bf16[128,1024]{1,0:T(8,128)(2,1)} %bitcast.143), custom_call_target="tpu_custom_call" | custom-call | tf_op jit(solution)/shard_map/pallas_call | solution.py:131
  199.1 2.2 fusion.43
  201.3 0.0 copy-done.9
  201.3 1.3 multiply_reduce_fusion.1
  202.6 0.0 copy-start.11
  202.6 0.0 copy-start.12
  202.6 0.0 copy-start.3
  202.6 0.6 copy-done.10
  203.3 0.0 copy-done.11
  203.3 0.0 copy-done.12
  203.3 2.4 convolution_bitcast_fusion.x_ref
  205.6 34.3 %shard_map.96 = f32[32,32,128]{2,1,0:T(8,128)} custom-call(f32[32,32,128]{2,1,0:T(8,128)} %convolution_bitcast_fusion.x_ref), custom_call_target="tpu_custom_call" | custom-call | tf_op jit(solution)/shard_map/pallas_call | solution.py:238
  239.9 0.0 copy-start.7
  240.0 0.0 copy-done.8
  240.0 0.0 copy-done.3
  240.0 2.2 fusion.8
  242.2 0.0 copy-done.7
  242.2 0.8 copy.42
  (4 shorter events, 0.0 us)
Async XLA Ops:
  7.2 65.6 %copy-start = (bf16[4,1024,256]{2,1,0:T(8,128)(2,1)S(1)}, bf16[4,1024,256]{2,1,0:T(8,128)(2,1)}, u32[]{:S(2)}) copy-start(bf16[4,1024,256]{2,1,0:T(8,128)(2,1)} %param.7) | copy-start | bytes 6291460
  7.2 17.7 %copy-start.5 = (bf16[1,256,1024]{2,1,0:T(8,128)(2,1)S(1)}, bf16[1,256,1024]{2,1,0:T(8,128)(2,1)}, u32[]{:S(2)}) copy-start(bf16[1,256,1024]{2,1,0:T(8,128)(2,1)} %param.9) | copy-start | bytes 1572868
  7.2 57.2 %all-gather.5.cloned.1.call-start = ((), (), s32[]{:S(2)}) async-start(), calls=%async_computation.4 | async-start | bytes 2359296 | tf_op jit(solution)/shard_map/all_gather | solution.py:278
  24.8 75.6 %all-gather.7.cloned.1.call-start = ((), (), s32[]{:S(2)}) async-start(), calls=%async_computation.5 | async-start | bytes 2359296 | tf_op jit(solution)/shard_map/all_gather | solution.py:278
  37.4 105.5 %reduce-scatter.3.cloned.1.call-start = ((), (), s32[]{:S(2)}) async-start(), calls=%async_computation.2 | async-start | bytes 2359296 | tf_op jit(solution)/shard_map/reduce_scatter | solution.py:281
  72.8 5.5 %copy-start.6 = (bf16[4,256,1024]{2,1,0:T(8,128)(2,1)S(1)}, bf16[4,256,1024]{2,1,0:T(8,128)(2,1)}, u32[]{:S(2)}) copy-start(bf16[4,256,1024]{2,1,0:T(8,128)(2,1)} %param.8) | copy-start | bytes 6291460
  85.9 102.0 %reduce-scatter.5.cloned.1.call-start = ((), (), s32[]{:S(2)}) async-start(), calls=%async_computation.3 | async-start | bytes 2359296 | tf_op jit(solution)/shard_map/reduce_scatter | solution.py:281
  110.2 0.8 copy-start.4
  117.9 1.0 copy-start.2
  120.0 3.9 %copy-start.1 = (bf16[256,4,1024]{2,1,0:T(4,128)(2,1)S(1)}, bf16[256,4,1024]{2,1,0:T(4,128)(2,1)}, u32[]{:S(2)}) copy-start(bf16[256,4,1024]{2,1,0:T(4,128)(2,1)} %reshape.122) | copy-start | bytes 6291460
  157.5 43.8 %copy-start.9 = (f32[256,128]{1,0:T(8,128)}, f32[256,128]{1,0:T(8,128)S(1)}, u32[]{:S(2)}) copy-start(f32[256,128]{1,0:T(8,128)S(1)} %convolution_bitcast_fusion.1) | copy-start | bytes 393220
  201.3 38.7 %copy-start.8 = (bf16[1024,128]{1,0:T(8,128)(2,1)S(1)}, bf16[1024,128]{1,0:T(8,128)(2,1)}, u32[]{:S(2)}) copy-start(bf16[1024,128]{1,0:T(8,128)(2,1)} %param.6) | copy-start | bytes 786436
  202.6 0.7 copy-start.10
  202.6 0.7 copy-start.11
  202.6 0.6 copy-start.12
  202.6 37.3 %copy-start.3 = (f32[256,1024]{1,0:T(8,128)S(1)}, f32[256,1024]{1,0:T(8,128)}, u32[]{:S(2)}) copy-start(f32[256,1024]{1,0:T(8,128)} %fusion.43) | copy-start | bytes 3145732
  239.9 2.2 copy-start.7
Sparse Core Ops, SparseCore 0:
  24.9 39.4 all-gather.4
  66.3 34.0 all-gather.6
  103.0 39.8 reduce-scatter.2
  145.3 42.5 reduce-scatter.4

commit v9 on v8

--- a/solution.py
+++ b/solution.py
@@ -192,7 +192,7 @@
             ex_copy(x_ref.at[j], land1, s1, r1, j, j).wait_recv()
             ex_copy(x_ref.at[j], land1, s1, r1, j, me_e).wait_send()
 
-    red1[...] = jnp.sum(land1[...], axis=0)
+    red1[...] = jnp.sum(land1[...].astype(jnp.float32), axis=0).astype(red1.dtype)
 
     @pl.loop(0, n_dp)
     def _(k):
@@ -209,10 +209,10 @@
             dp_copy(red1, land2, s2, r2, k, k).wait_recv()
             dp_copy(red1, land2, s2, r2, k, me_d).wait_send()
 
-    total = land2[0]
+    total = land2[0].astype(jnp.float32)
     for k in range(1, n_dp):
-        total = total + land2[k]
-    red2[...] = total
+        total = total + land2[k].astype(jnp.float32)
+    red2[...] = total.astype(red2.dtype)
 
     @pl.loop(0, n_ex)
     def _(j):
@@ -220,32 +220,32 @@
         def _():
             ex_copy(red2, land3, s3, r3, j, me_e).start()
 
-    o_ref[me_e] = red2[...]
+    o_ref[me_e] = red2[...].astype(o_ref.dtype)
 
     @pl.loop(0, n_ex)
     def _(j):
         @pl.when(j != me_e)
         def _():
             ex_copy(red2, land3, s3, r3, j, j).wait_recv()
-            o_ref[j] = land3[j]
+            o_ref[j] = land3[j].astype(o_ref.dtype)
             ex_copy(red2, land3, s3, r3, j, me_e).wait_send()
 
 
 def all_sum(value, n_dp, n_expert):
     rows, cols = value.shape
     block = (rows // n_expert, cols)
-    chunks = value.reshape(n_expert, *block)
+    chunks = value.astype(jnp.bfloat16).reshape(n_expert, *block)
     out = pl.pallas_call(
         functools.partial(_allsum_kernel, n_dp, n_expert),
         out_shape=jax.ShapeDtypeStruct(chunks.shape, value.dtype),
         in_specs=[pl.BlockSpec(memory_space=pltpu.VMEM)],
         out_specs=pl.BlockSpec(memory_space=pltpu.VMEM),
         scratch_shapes=[
-            pltpu.VMEM(chunks.shape, value.dtype),
-            pltpu.VMEM((n_dp,) + block, value.dtype),
-            pltpu.VMEM(chunks.shape, value.dtype),
-            pltpu.VMEM(block, value.dtype),
-            pltpu.VMEM(block, value.dtype),
+            pltpu.VMEM(chunks.shape, chunks.dtype),
+            pltpu.VMEM((n_dp,) + block, chunks.dtype),
+            pltpu.VMEM(chunks.shape, chunks.dtype),
+            pltpu.VMEM(block, chunks.dtype),
+            pltpu.VMEM(block, chunks.dtype),
             pltpu.SemaphoreType.DMA((n_expert,)),
             pltpu.SemaphoreType.DMA((n_expert,)),
             pltpu.SemaphoreType.DMA((n_dp,)),

time: 250 us -> 241 us (0.964)
  Pallas kernels: 81.6 us -> 75.9 us
  matrix products: 35.9 us -> 31.6 us
    pallas_call x1, Pallas kernels: 34.3 us -> 28.2 us  [all_sum(): pl.pallas_call(functools.partial(_allsum_kernel, n_dp, n_expert), out_sha...]
where the time goes in v9:
time: 241 us; the launch traced here: 240 us
  waiting for transfers between devices  89.1 us (37%)
  Pallas kernels  75.9 us (31%)
  matrix products  31.6 us (13%)
  local copies, waits for them, and re-layouts  29 us (12%)
  between operations  13.9 us (6%)
    pallas_call x4, Pallas kernels, row_exchange(): pl.pallas_call(functools.partial(_row_exchange_kernel, n, x.shape[0] // n...  47.7 us
    reduce_scatter x2, waiting for transfers between devices, from_owners(): lax.psum_scatter(partial_value, 'dp', scatter_dimension=0, tiled=True)  47.3 us
    all_gather x2, waiting for transfers between devices, to_owners(): return lax.all_gather(arrived, 'dp', axis=0, tiled=True)  41.7 us
    pallas_call x1, Pallas kernels, all_sum(): pl.pallas_call(functools.partial(_allsum_kernel, n_dp, n_expert), out_sha...  28.2 us
    reshape x2, local copies, waits for them, and re-layouts, local(): blocks = slot_rows.reshape(-1, experts_dev, width)  8.36 us
    dot_general x1, matrix products, local(): jnp.einsum('rkd,kfd->rkf', grad_blocks, weight_out, preferred_element_typ...  5.73 us
    dot_general x1, matrix products, local(): jnp.einsum('rkd,kdf->rkf', blocks, weight_in, preferred_element_type=jnp....  5.48 us
  transfers between devices with their start and end apart: 4, of which 4 were waited for; matrix products, arithmetic and copies ran while one was open for 21% of the time, Pallas kernels for 9%

profile of v9, /device:TPU:1, one launch (start us, length us, event | category | flops | bytes accessed | tf_op | source)
XLA Modules:
  0.0 240.2 jit_solution(9098569260684615109)
XLA Ops:
  7.2 0.0 copy-start
  7.2 0.0 copy-start.3
  7.2 0.0 all-gather.5.cloned.1.call-start
  7.2 1.7 fusion.53
  8.9 0.2 fusion.41
  9.1 2.0 convolution_convert_fusion.5.x_ref
  11.1 13.6 %shard_map.92 = bf16[128,1024]{1,0:T(8,128)(2,1)} custom-call(bf16[128,1024]{1,0:T(8,128)(2,1)} %convolution_convert_fusion.5.x_ref), custom_call_target="tpu_custom_call" | custom-call | tf_op jit(solution)/shard_map/pallas_call | solution.py:131
  24.8 0.0 all-gather.5.cloned.1.call-update
  24.8 0.0 all-gather.7.cloned.1.call-start
  24.8 0.0 copy-done.3
  24.9 1.1 convolution_convert_fusion.4.x_ref
  25.9 11.4 %shard_map.94 = bf16[128,1024]{1,0:T(8,128)(2,1)} custom-call(bf16[128,1024]{1,0:T(8,128)(2,1)} %convolution_convert_fusion.4.x_ref), custom_call_target="tpu_custom_call" | custom-call | tf_op jit(solution)/shard_map/pallas_call | solution.py:131
  37.3 0.0 all-gather.7.cloned.1.call-update
  37.4 0.0 reduce-scatter.3.cloned.1.call-start
  37.4 25.7 %all-gather.5.cloned.1.call-done = bf16[1024,1024]{1,0:T(8,128)(2,1)} async-done(((bf16[128,1024]{1,0:T(8,128)(2,1)}), bf16[1024,1024]{1,0:T(8,128)(2,1)}) %all-gather.5.cloned.1.call-update) | async-done | bytes 2097168 | tf_op jit(solution)/shard_map/all_gather | solution.py:278
  63.1 4.1 %reshape.120 = bf16[256,4,1024]{2,1,0:T(4,128)(2,1)} reshape(bf16[1024,1024]{1,0:T(8,128)(2,1)} %all-gather.5.cloned.1.call-done) | data formatting | bytes 4194304 | tf_op jit(solution)/shard_map/reshape | solution.py:285
  67.2 4.3 %copy.17 = bf16[256,4,1024]{0,2,1:T(8,128)(2,1)} copy(bf16[256,4,1024]{2,1,0:T(4,128)(2,1)} %reshape.120) | data formatting | bytes 4194304 | tf_op jit(solution)/shard_map/reshape | solution.py:285
  71.5 0.0 copy-done
  71.5 0.0 copy-start.4
  71.5 5.5 %fusion.12 = (bf16[256,4,256]{2,0,1:T(8,128)(2,1)S(1)}, f32[4,256,256]{2,1,0:T(8,128)}) fusion(bf16[256,4,1024]{0,2,1:T(8,128)(2,1)} %copy.17, bf16[4,1024,256]{2,1,0:T(8,128)(2,1)S(1)} %copy-done), kind=kOutput, calls=%fused_computation.28 | convolution fusion | flops 553910272 | bytes 5767168 | tf_op jit(solution)/shard_map/rkd,kdf->rkf/dot_general | solution.py:286
  77.0 0.0 copy-done.4
  77.0 0.7 convert_bitcast_fusion.1
  77.7 2.9 %copy.11 = bf16[256,4,1024]{2,1,0:T(4,128)(2,1)} copy(bf16[256,4,1024]{2,0,1:T(8,128)(2,1)S(1)} %convert_bitcast_fusion.1) | data formatting | bytes 4194304 | tf_op jit(solution)/shard_map/convert_element_type | solution.py:295
  80.6 4.0 %reshape.121 = bf16[8,128,1024]{2,1,0:T(8,128)(2,1)} reshape(bf16[256,4,1024]{2,1,0:T(4,128)(2,1)} %copy.11) | data formatting | bytes 4194304 | tf_op jit(solution)/shard_map/reshape | solution.py:295
  84.6 0.0 reduce-scatter.3.cloned.1.call-update
  84.6 0.2 reduce-scatter.5.cloned.1.call-start
  84.9 16.0 %all-gather.7.cloned.1.call-done = bf16[1024,1024]{1,0:T(8,128)(2,1)} async-done(((bf16[128,1024]{1,0:T(8,128)(2,1)}), bf16[1024,1024]{1,0:T(8,128)(2,1)}) %all-gather.7.cloned.1.call-update) | async-done | bytes 2097168 | tf_op jit(solution)/shard_map/all_gather | solution.py:278
  100.9 4.1 %reshape.123 = bf16[256,4,1024]{2,1,0:T(4,128)(2,1)} reshape(bf16[1024,1024]{1,0:T(8,128)(2,1)} %all-gather.7.cloned.1.call-done) | data formatting | bytes 4194304 | tf_op jit(solution)/shard_map/reshape | solution.py:299
  105.0 5.7 %fusion.18 = bf16[256,4,256]{2,0,1:T(8,128)(2,1)S(1)} fusion(bf16[4,256,1024]{2,1,0:T(8,128)(2,1)} %param.8, bf16[256,4,1024]{2,1,0:T(4,128)(2,1)} %reshape.123, f32[4,256,256]{2,1,0:T(8,128)} %get-tuple-element.13), kind=kOutput, calls=%fused_computation.34 | convolution fusion | flops 555745280 | bytes 5767168 | tf_op jit(solution)/shard_map/rkd,kfd->rkf/dot_general | solution.py:300
  110.7 0.7 convert_bitcast_fusion
  111.5 2.9 %copy.13 = bf16[256,4,1024]{2,1,0:T(4,128)(2,1)} copy(bf16[256,4,1024]{2,0,1:T(8,128)(2,1)S(1)} %convert_bitcast_fusion) | data formatting | bytes 4194304 | tf_op jit(solution)/shard_map/convert_element_type | solution.py:317
  114.4 4.0 %reshape.124 = bf16[8,128,1024]{2,1,0:T(8,128)(2,1)} reshape(bf16[256,4,1024]{2,1,0:T(4,128)(2,1)} %copy.13) | data formatting | bytes 4194304 | tf_op jit(solution)/shard_map/reshape | solution.py:317
  118.4 0.0 reduce-scatter.5.cloned.1.call-update
  118.4 0.0 copy-start.1
  118.4 4.7 %convolution_convert_fusion = bf16[4,256,1024]{2,1,0:T(8,128)(2,1)} fusion(bf16[256,4,256]{2,0,1:T(8,128)(2,1)S(1)} %get-tuple-element.12, bf16[256,4,1024]{2,1,0:T(4,128)(2,1)} %reshape.123), kind=kOutput, calls=%fused_computation.2 | convolution fusion | flops 537919488 | bytes 4718592 | tf_op jit(solution)/shard_map/rkf,rkd->kfd/dot_general | solution.py:305
  123.1 0.0 copy-done.1
  123.1 2.0 convolution_convert_fusion.1
  125.1 17.8 %reduce-scatter.3.cloned.1.call-done = bf16[1,128,1024]{2,1,0:T(8,128)(2,1)} async-done(((bf16[8,128,1024]{2,1,0:T(8,128)(2,1)}), bf16[1,128,1024]{2,1,0:T(8,128)(2,1)}) %reduce-scatter.3.cloned.1.call-update) | async-done | bytes 262160 | tf_op jit(solution)/shard_map/reduce_scatter | solution.py:281
  142.9 0.0 copy-start.2
  142.9 11.4 %shard_map.93 = bf16[128,1024]{1,0:T(8,128)(2,1)} custom-call(bf16[128,1024]{1,0:T(8,128)(2,1)} %bitcast.136), custom_call_target="tpu_custom_call" | custom-call | tf_op jit(solution)/shard_map/pallas_call | solution.py:131
  154.3 2.1 fusion.7
  156.4 1.5 convolution_bitcast_fusion
  157.8 29.5 %reduce-scatter.5.cloned.1.call-done = bf16[1,128,1024]{2,1,0:T(8,128)(2,1)} async-done(((bf16[8,128,1024]{2,1,0:T(8,128)(2,1)}), bf16[1,128,1024]{2,1,0:T(8,128)(2,1)}) %reduce-scatter.5.cloned.1.call-update) | async-done | bytes 262160 | tf_op jit(solution)/shard_map/reduce_scatter | solution.py:281
  187.4 11.3 %shard_map.95 = bf16[128,1024]{1,0:T(8,128)(2,1)} custom-call(bf16[128,1024]{1,0:T(8,128)(2,1)} %bitcast.137), custom_call_target="tpu_custom_call" | custom-call | tf_op jit(solution)/shard_map/pallas_call | solution.py:131
  198.7 0.0 copy-start.5
  198.7 1.3 fusion.44
  200.0 0.0 copy-done.2
  200.0 1.3 multiply_reduce_fusion.1
  201.3 0.2 add_convert_fusion
  201.4 0.2 fusion.9
  201.7 0.0 copy-done.5
  201.7 1.1 fusion.8
  202.8 0.8 copy.16
  203.6 28.2 %shard_map.96 = f32[32,32,128]{2,1,0:T(8,128)} custom-call(bf16[32,32,128]{2,1,0:T(8,128)(2,1)} %bitcast.135), custom_call_target="tpu_custom_call" | custom-call | tf_op jit(solution)/shard_map/pallas_call | solution.py:238
  231.8 1.9 copy.32
Async XLA Ops:
  7.2 64.3 %copy-start = (bf16[4,1024,256]{2,1,0:T(8,128)(2,1)S(1)}, bf16[4,1024,256]{2,1,0:T(8,128)(2,1)}, u32[]{:S(2)}) copy-start(bf16[4,1024,256]{2,1,0:T(8,128)(2,1)} %param.7) | copy-start | bytes 6291460
  7.2 17.7 %copy-start.3 = (bf16[1,256,1024]{2,1,0:T(8,128)(2,1)S(1)}, bf16[1,256,1024]{2,1,0:T(8,128)(2,1)}, u32[]{:S(2)}) copy-start(bf16[1,256,1024]{2,1,0:T(8,128)(2,1)} %param.9) | copy-start | bytes 1572868
  7.2 55.9 %all-gather.5.cloned.1.call-start = ((), (), s32[]{:S(2)}) async-start(), calls=%async_computation.4 | async-start | bytes 2359296 | tf_op jit(solution)/shard_map/all_gather | solution.py:278
  24.8 76.1 %all-gather.7.cloned.1.call-start = ((), (), s32[]{:S(2)}) async-start(), calls=%async_computation.5 | async-start | bytes 2359296 | tf_op jit(solution)/shard_map/all_gather | solution.py:278
  37.4 105.5 %reduce-scatter.3.cloned.1.call-start = ((), (), s32[]{:S(2)}) async-start(), calls=%async_computation.2 | async-start | bytes 2359296 | tf_op jit(solution)/shard_map/reduce_scatter | solution.py:281
  71.5 5.5 %copy-start.4 = (bf16[4,256,1024]{2,1,0:T(8,128)(2,1)S(1)}, bf16[4,256,1024]{2,1,0:T(8,128)(2,1)}, u32[]{:S(2)}) copy-start(bf16[4,256,1024]{2,1,0:T(8,128)(2,1)} %param.8) | copy-start | bytes 6291460
  84.6 102.7 %reduce-scatter.5.cloned.1.call-start = ((), (), s32[]{:S(2)}) async-start(), calls=%async_computation.3 | async-start | bytes 2359296 | tf_op jit(solution)/shard_map/reduce_scatter | solution.py:281
  118.4 4.7 %copy-start.1 = (bf16[256,4,1024]{0,2,1:T(8,128)(2,1)S(1)}, bf16[256,4,1024]{0,2,1:T(8,128)(2,1)}, u32[]{:S(2)}) copy-start(bf16[256,4,1024]{0,2,1:T(8,128)(2,1)} %copy.17) | copy-start | bytes 6291460
  142.9 57.1 %copy-start.2 = (bf16[1,256,1024]{2,1,0:T(8,128)(2,1)S(1)}, bf16[1,256,1024]{2,1,0:T(8,128)(2,1)}, u32[]{:S(2)}) copy-start(bf16[1,256,1024]{2,1,0:T(8,128)(2,1)} %param.5) | copy-start | bytes 1572868
  198.7 3.0 %copy-start.5 = (bf16[1024,128]{1,0:T(8,128)(2,1)S(1)}, bf16[1024,128]{1,0:T(8,128)(2,1)}, u32[]{:S(2)}) copy-start(bf16[1024,128]{1,0:T(8,128)(2,1)} %param.6) | copy-start | bytes 786436
Sparse Core Ops, SparseCore 0:
  24.9 38.1 all-gather.4
  65.0 35.8 all-gather.6
  103.4 39.4 reduce-scatter.2
  145.3 42.0 reduce-scatter.4

commit v10 on v9

--- a/solution.py
+++ b/solution.py
@@ -220,14 +220,14 @@
         def _():
             ex_copy(red2, land3, s3, r3, j, me_e).start()
 
-    o_ref[me_e] = red2[...].astype(o_ref.dtype)
+    o_ref[me_e] = red2[...]
 
     @pl.loop(0, n_ex)
     def _(j):
         @pl.when(j != me_e)
         def _():
             ex_copy(red2, land3, s3, r3, j, j).wait_recv()
-            o_ref[j] = land3[j].astype(o_ref.dtype)
+            o_ref[j] = land3[j]
             ex_copy(red2, land3, s3, r3, j, me_e).wait_send()
 
 
@@ -237,7 +237,7 @@
     chunks = value.astype(jnp.bfloat16).reshape(n_expert, *block)
     out = pl.pallas_call(
         functools.partial(_allsum_kernel, n_dp, n_expert),
-        out_shape=jax.ShapeDtypeStruct(chunks.shape, value.dtype),
+        out_shape=jax.ShapeDtypeStruct(chunks.shape, chunks.dtype),
         in_specs=[pl.BlockSpec(memory_space=pltpu.VMEM)],
         out_specs=pl.BlockSpec(memory_space=pltpu.VMEM),
         scratch_shapes=[
@@ -255,7 +255,7 @@
         ],
         compiler_params=pltpu.CompilerParams(collective_id=4, has_side_effects=True),
     )(chunks)
-    return out.reshape(rows, cols)
+    return out.reshape(rows, cols).astype(value.dtype)
 
 
 def local(n_dp, n_expert, tokens, router, weight_in, weight_out, cotangent):

time: 241 us -> 241 us (level)
  no operation moved by 1% of the time
where the time goes in v10:
time: 241 us; the launch traced here: 240 us
  waiting for transfers between devices  89.1 us (37%)
  Pallas kernels  75.8 us (31%)
  matrix products  31.6 us (13%)
  local copies, waits for them, and re-layouts  27.2 us (11%)
  between operations  13.9 us (6%)
    pallas_call x4, Pallas kernels, row_exchange(): pl.pallas_call(functools.partial(_row_exchange_kernel, n, x.shape[0] // n...  47.7 us
    reduce_scatter x2, waiting for transfers between devices, from_owners(): lax.psum_scatter(partial_value, 'dp', scatter_dimension=0, tiled=True)  47.3 us
    all_gather x2, waiting for transfers between devices, to_owners(): return lax.all_gather(arrived, 'dp', axis=0, tiled=True)  41.7 us
    pallas_call x1, Pallas kernels, all_sum(): pl.pallas_call(functools.partial(_allsum_kernel, n_dp, n_expert), out_sha...  28.1 us
    reshape x2, local copies, waits for them, and re-layouts, local(): blocks = slot_rows.reshape(-1, experts_dev, width)  8.36 us
    dot_general x1, matrix products, local(): jnp.einsum('rkd,kfd->rkf', grad_blocks, weight_out, preferred_element_typ...  5.73 us
    dot_general x1, matrix products, local(): jnp.einsum('rkd,kdf->rkf', blocks, weight_in, preferred_element_type=jnp....  5.48 us
  transfers between devices with their start and end apart: 4, of which 4 were waited for; matrix products, arithmetic and copies ran while one was open for 21% of the time, Pallas kernels for 9%

profile of v10, /device:TPU:1, one launch (start us, length us, event | category | flops | bytes accessed | tf_op | source)
XLA Modules:
  0.0 240.1 jit_solution(4959665594109100949)
XLA Ops:
  7.2 0.0 copy-start
  7.2 0.0 copy-start.3
  7.2 0.0 all-gather.5.cloned.1.call-start
  7.2 1.7 fusion.53
  8.9 0.2 fusion.41
  9.1 2.0 convolution_convert_fusion.5.x_ref
  11.1 13.6 %shard_map.92 = bf16[128,1024]{1,0:T(8,128)(2,1)} custom-call(bf16[128,1024]{1,0:T(8,128)(2,1)} %convolution_convert_fusion.5.x_ref), custom_call_target="tpu_custom_call" | custom-call | tf_op jit(solution)/shard_map/pallas_call | solution.py:131
  24.8 0.0 all-gather.5.cloned.1.call-update
  24.8 0.0 all-gather.7.cloned.1.call-start
  24.8 0.0 copy-done.3
  24.9 1.1 convolution_convert_fusion.4.x_ref
  25.9 11.4 %shard_map.94 = bf16[128,1024]{1,0:T(8,128)(2,1)} custom-call(bf16[128,1024]{1,0:T(8,128)(2,1)} %convolution_convert_fusion.4.x_ref), custom_call_target="tpu_custom_call" | custom-call | tf_op jit(solution)/shard_map/pallas_call | solution.py:131
  37.3 0.0 all-gather.7.cloned.1.call-update
  37.4 0.0 reduce-scatter.3.cloned.1.call-start
  37.4 25.7 %all-gather.5.cloned.1.call-done = bf16[1024,1024]{1,0:T(8,128)(2,1)} async-done(((bf16[128,1024]{1,0:T(8,128)(2,1)}), bf16[1024,1024]{1,0:T(8,128)(2,1)}) %all-gather.5.cloned.1.call-update) | async-done | bytes 2097168 | tf_op jit(solution)/shard_map/all_gather | solution.py:278
  63.1 4.1 %reshape.120 = bf16[256,4,1024]{2,1,0:T(4,128)(2,1)} reshape(bf16[1024,1024]{1,0:T(8,128)(2,1)} %all-gather.5.cloned.1.call-done) | data formatting | bytes 4194304 | tf_op jit(solution)/shard_map/reshape | solution.py:285
  67.2 4.3 %copy.17 = bf16[256,4,1024]{0,2,1:T(8,128)(2,1)} copy(bf16[256,4,1024]{2,1,0:T(4,128)(2,1)} %reshape.120) | data formatting | bytes 4194304 | tf_op jit(solution)/shard_map/reshape | solution.py:285
  71.5 0.0 copy-done
  71.5 0.0 copy-start.4
  71.5 5.5 %fusion.12 = (bf16[256,4,256]{2,0,1:T(8,128)(2,1)S(1)}, f32[4,256,256]{2,1,0:T(8,128)}) fusion(bf16[256,4,1024]{0,2,1:T(8,128)(2,1)} %copy.17, bf16[4,1024,256]{2,1,0:T(8,128)(2,1)S(1)} %copy-done), kind=kOutput, calls=%fused_computation.28 | convolution fusion | flops 553910272 | bytes 5767168 | tf_op jit(solution)/shard_map/rkd,kdf->rkf/dot_general | solution.py:286
  77.0 0.0 copy-done.4
  77.0 0.7 convert_bitcast_fusion.1
  77.7 2.9 %copy.11 = bf16[256,4,1024]{2,1,0:T(4,128)(2,1)} copy(bf16[256,4,1024]{2,0,1:T(8,128)(2,1)S(1)} %convert_bitcast_fusion.1) | data formatting | bytes 4194304 | tf_op jit(solution)/shard_map/convert_element_type | solution.py:295
  80.6 4.0 %reshape.121 = bf16[8,128,1024]{2,1,0:T(8,128)(2,1)} reshape(bf16[256,4,1024]{2,1,0:T(4,128)(2,1)} %copy.11) | data formatting | bytes 4194304 | tf_op jit(solution)/shard_map/reshape | solution.py:295
  84.6 0.0 reduce-scatter.3.cloned.1.call-update
  84.6 0.2 reduce-scatter.5.cloned.1.call-start
  84.9 16.0 %all-gather.7.cloned.1.call-done = bf16[1024,1024]{1,0:T(8,128)(2,1)} async-done(((bf16[128,1024]{1,0:T(8,128)(2,1)}), bf16[1024,1024]{1,0:T(8,128)(2,1)}) %all-gather.7.cloned.1.call-update) | async-done | bytes 2097168 | tf_op jit(solution)/shard_map/all_gather | solution.py:278
  100.9 4.1 %reshape.123 = bf16[256,4,1024]{2,1,0:T(4,128)(2,1)} reshape(bf16[1024,1024]{1,0:T(8,128)(2,1)} %all-gather.7.cloned.1.call-done) | data formatting | bytes 4194304 | tf_op jit(solution)/shard_map/reshape | solution.py:299
  105.0 5.7 %fusion.18 = bf16[256,4,256]{2,0,1:T(8,128)(2,1)S(1)} fusion(bf16[4,256,1024]{2,1,0:T(8,128)(2,1)} %param.8, bf16[256,4,1024]{2,1,0:T(4,128)(2,1)} %reshape.123, f32[4,256,256]{2,1,0:T(8,128)} %get-tuple-element.13), kind=kOutput, calls=%fused_computation.34 | convolution fusion | flops 555745280 | bytes 5767168 | tf_op jit(solution)/shard_map/rkd,kfd->rkf/dot_general | solution.py:300
  110.7 0.7 convert_bitcast_fusion
  111.5 2.9 %copy.13 = bf16[256,4,1024]{2,1,0:T(4,128)(2,1)} copy(bf16[256,4,1024]{2,0,1:T(8,128)(2,1)S(1)} %convert_bitcast_fusion) | data formatting | bytes 4194304 | tf_op jit(solution)/shard_map/convert_element_type | solution.py:317
  114.4 4.0 %reshape.124 = bf16[8,128,1024]{2,1,0:T(8,128)(2,1)} reshape(bf16[256,4,1024]{2,1,0:T(4,128)(2,1)} %copy.13) | data formatting | bytes 4194304 | tf_op jit(solution)/shard_map/reshape | solution.py:317
  118.4 0.0 reduce-scatter.5.cloned.1.call-update
  118.4 0.0 copy-start.1
  118.4 4.7 %convolution_convert_fusion = bf16[4,256,1024]{2,1,0:T(8,128)(2,1)} fusion(bf16[256,4,256]{2,0,1:T(8,128)(2,1)S(1)} %get-tuple-element.12, bf16[256,4,1024]{2,1,0:T(4,128)(2,1)} %reshape.123), kind=kOutput, calls=%fused_computation.2 | convolution fusion | flops 537919488 | bytes 4718592 | tf_op jit(solution)/shard_map/rkf,rkd->kfd/dot_general | solution.py:305
  123.1 0.0 copy-done.1
  123.1 2.0 convolution_convert_fusion.1
  125.1 17.8 %reduce-scatter.3.cloned.1.call-done = bf16[1,128,1024]{2,1,0:T(8,128)(2,1)} async-done(((bf16[8,128,1024]{2,1,0:T(8,128)(2,1)}), bf16[1,128,1024]{2,1,0:T(8,128)(2,1)}) %reduce-scatter.3.cloned.1.call-update) | async-done | bytes 262160 | tf_op jit(solution)/shard_map/reduce_scatter | solution.py:281
  142.9 0.0 copy-start.2
  142.9 11.4 %shard_map.93 = bf16[128,1024]{1,0:T(8,128)(2,1)} custom-call(bf16[128,1024]{1,0:T(8,128)(2,1)} %bitcast.137), custom_call_target="tpu_custom_call" | custom-call | tf_op jit(solution)/shard_map/pallas_call | solution.py:131
  154.3 2.1 fusion.7
  156.4 1.5 convolution_bitcast_fusion
  157.8 29.5 %reduce-scatter.5.cloned.1.call-done = bf16[1,128,1024]{2,1,0:T(8,128)(2,1)} async-done(((bf16[8,128,1024]{2,1,0:T(8,128)(2,1)}), bf16[1,128,1024]{2,1,0:T(8,128)(2,1)}) %reduce-scatter.5.cloned.1.call-update) | async-done | bytes 262160 | tf_op jit(solution)/shard_map/reduce_scatter | solution.py:281
  187.4 11.3 %shard_map.95 = bf16[128,1024]{1,0:T(8,128)(2,1)} custom-call(bf16[128,1024]{1,0:T(8,128)(2,1)} %bitcast.138), custom_call_target="tpu_custom_call" | custom-call | tf_op jit(solution)/shard_map/pallas_call | solution.py:131
  198.7 0.0 copy-start.5
  198.7 1.3 fusion.44
  200.0 0.0 copy-done.2
  200.0 1.3 multiply_reduce_fusion.1
  201.3 0.2 add_convert_fusion
  201.4 0.2 fusion.9
  201.7 0.0 copy-done.5
  201.7 1.1 fusion.8
  202.8 0.8 copy.16
  203.6 28.1 %shard_map.96 = bf16[32,32,128]{2,1,0:T(8,128)(2,1)} custom-call(bf16[32,32,128]{2,1,0:T(8,128)(2,1)} %bitcast.136), custom_call_target="tpu_custom_call" | custom-call | tf_op jit(solution)/shard_map/pallas_call | solution.py:238
  231.7 1.8 bitcast_convert_fusion
Async XLA Ops:
  7.2 64.3 %copy-start = (bf16[4,1024,256]{2,1,0:T(8,128)(2,1)S(1)}, bf16[4,1024,256]{2,1,0:T(8,128)(2,1)}, u32[]{:S(2)}) copy-start(bf16[4,1024,256]{2,1,0:T(8,128)(2,1)} %param.7) | copy-start | bytes 6291460
  7.2 17.7 %copy-start.3 = (bf16[1,256,1024]{2,1,0:T(8,128)(2,1)S(1)}, bf16[1,256,1024]{2,1,0:T(8,128)(2,1)}, u32[]{:S(2)}) copy-start(bf16[1,256,1024]{2,1,0:T(8,128)(2,1)} %param.9) | copy-start | bytes 1572868
  7.2 55.9 %all-gather.5.cloned.1.call-start = ((), (), s32[]{:S(2)}) async-start(), calls=%async_computation.4 | async-start | bytes 2359296 | tf_op jit(solution)/shard_map/all_gather | solution.py:278
  24.8 76.1 %all-gather.7.cloned.1.call-start = ((), (), s32[]{:S(2)}) async-start(), calls=%async_computation.5 | async-start | bytes 2359296 | tf_op jit(solution)/shard_map/all_gather | solution.py:278
  37.4 105.5 %reduce-scatter.3.cloned.1.call-start = ((), (), s32[]{:S(2)}) async-start(), calls=%async_computation.2 | async-start | bytes 2359296 | tf_op jit(solution)/shard_map/reduce_scatter | solution.py:281
  71.5 5.5 %copy-start.4 = (bf16[4,256,1024]{2,1,0:T(8,128)(2,1)S(1)}, bf16[4,256,1024]{2,1,0:T(8,128)(2,1)}, u32[]{:S(2)}) copy-start(bf16[4,256,1024]{2,1,0:T(8,128)(2,1)} %param.8) | copy-start | bytes 6291460
  84.6 102.7 %reduce-scatter.5.cloned.1.call-start = ((), (), s32[]{:S(2)}) async-start(), calls=%async_computation.3 | async-start | bytes 2359296 | tf_op jit(solution)/shard_map/reduce_scatter | solution.py:281
  118.4 4.7 %copy-start.1 = (bf16[256,4,1024]{0,2,1:T(8,128)(2,1)S(1)}, bf16[256,4,1024]{0,2,1:T(8,128)(2,1)}, u32[]{:S(2)}) copy-start(bf16[256,4,1024]{0,2,1:T(8,128)(2,1)} %copy.17) | copy-start | bytes 6291460
  142.9 57.1 %copy-start.2 = (bf16[1,256,1024]{2,1,0:T(8,128)(2,1)S(1)}, bf16[1,256,1024]{2,1,0:T(8,128)(2,1)}, u32[]{:S(2)}) copy-start(bf16[1,256,1024]{2,1,0:T(8,128)(2,1)} %param.5) | copy-start | bytes 1572868
  198.7 3.0 %copy-start.5 = (bf16[1024,128]{1,0:T(8,128)(2,1)S(1)}, bf16[1024,128]{1,0:T(8,128)(2,1)}, u32[]{:S(2)}) copy-start(bf16[1024,128]{1,0:T(8,128)(2,1)} %param.6) | copy-start | bytes 786436
Sparse Core Ops, SparseCore 0:
  24.9 38.1 all-gather.4
  65.0 35.8 all-gather.6
  103.4 39.4 reduce-scatter.2
  145.3 42.0 reduce-scatter.4

commit v11 on v10

--- a/solution.py
+++ b/solution.py
@@ -258,6 +258,161 @@
     return out.reshape(rows, cols).astype(value.dtype)
 
 
+def _tail_kernel(n_dp, n_ex, rows, summed_ref, tok_ref, tokt_ref, prob_ref, comb_ref,
+                 gsa_ref, logit_ref, o_ref,
+                 land0, xs, land1, land2, land3, red1, red2, s0, r0, own_sem, s1, r1, s2, r2, s3, r3):
+    me_d = lax.axis_index("dp")
+    me_e = lax.axis_index("expert")
+    mesh_id = pl.DeviceIdType.MESH
+    barrier = pltpu.get_barrier_semaphore()
+
+    @pl.loop(0, n_ex)
+    def _(j):
+        @pl.when(j != me_e)
+        def _():
+            pl.semaphore_signal(barrier, inc=1, device_id=(me_d, j), device_id_type=mesh_id)
+
+    @pl.loop(0, n_dp)
+    def _(k):
+        @pl.when(k != me_d)
+        def _():
+            pl.semaphore_signal(barrier, inc=1, device_id=(k, me_e), device_id_type=mesh_id)
+
+    pl.semaphore_wait(barrier, n_ex - 1 + n_dp - 1)
+
+    def row_copy(j, slot):
+        return pltpu.make_async_remote_copy(
+            src_ref=summed_ref.at[pl.ds(j * rows, rows)], dst_ref=land0.at[pl.ds(slot * rows, rows)],
+            send_sem=s0.at[j], recv_sem=r0.at[slot], device_id=(me_d, j), device_id_type=mesh_id)
+
+    @pl.loop(0, n_ex)
+    def _(j):
+        @pl.when(j != me_e)
+        def _():
+            row_copy(j, me_e).start()
+
+    own = pltpu.make_async_copy(
+        summed_ref.at[pl.ds(me_e * rows, rows)], land0.at[pl.ds(me_e * rows, rows)], own_sem)
+    own.start()
+
+    @pl.loop(0, n_ex)
+    def _(j):
+        @pl.when(j != me_e)
+        def _():
+            row_copy(j, j).wait_recv()
+            row_copy(j, me_e).wait_send()
+
+    own.wait()
+    gsa = land0[...]
+    gsa_ref[...] = gsa
+    prob = prob_ref[...]
+    grad_disp = lax.dot_general(tok_ref[...], gsa, (((1,), (1,)), ((), ())), preferred_element_type=jnp.float32)
+    part_disp = prob * (grad_disp - jnp.sum(prob * grad_disp, axis=0, keepdims=True))
+    logits = (part_disp + comb_ref[...]).astype(logit_ref.dtype)
+    logit_ref[...] = logits
+    term = jnp.dot(tokt_ref[...], logits, preferred_element_type=jnp.float32)
+    xs[...] = term.astype(xs.dtype).reshape(xs.shape)
+
+    def ex_copy(src, land, send, recv, j, slot):
+        return pltpu.make_async_remote_copy(
+            src_ref=src, dst_ref=land.at[slot], send_sem=send.at[j], recv_sem=recv.at[slot],
+            device_id=(me_d, j), device_id_type=mesh_id)
+
+    def dp_copy(src, land, send, recv, k, slot):
+        return pltpu.make_async_remote_copy(
+            src_ref=src, dst_ref=land.at[slot], send_sem=send.at[k], recv_sem=recv.at[slot],
+            device_id=(k, me_e), device_id_type=mesh_id)
+
+    @pl.loop(0, n_ex)
+    def _(j):
+        @pl.when(j != me_e)
+        def _():
+            ex_copy(xs.at[j], land1, s1, r1, j, me_e).start()
+
+    land1[me_e] = xs[me_e]
+
+    @pl.loop(0, n_ex)
+    def _(j):
+        @pl.when(j != me_e)
+        def _():
+            ex_copy(xs.at[j], land1, s1, r1, j, j).wait_recv()
+            ex_copy(xs.at[j], land1, s1, r1, j, me_e).wait_send()
+
+    red1[...] = jnp.sum(land1[...].astype(jnp.float32), axis=0).astype(red1.dtype)
+
+    @pl.loop(0, n_dp)
+    def _(k):
+        @pl.when(k != me_d)
+        def _():
+            dp_copy(red1, land2, s2, r2, k, me_d).start()
+
+    land2[me_d] = red1[...]
+
+    @pl.loop(0, n_dp)
+    def _(k):
+        @pl.when(k != me_d)
+        def _():
+            dp_copy(red1, land2, s2, r2, k, k).wait_recv()
+            dp_copy(red1, land2, s2, r2, k, me_d).wait_send()
+
+    total = land2[0].astype(jnp.float32)
+    for k in range(1, n_dp):
+        total = total + land2[k].astype(jnp.float32)
+    red2[...] = total.astype(red2.dtype)
+
+    @pl.loop(0, n_ex)
+    def _(j):
+        @pl.when(j != me_e)
+        def _():
+            ex_copy(red2, land3, s3, r3, j, me_e).start()
+
+    o_ref[me_e] = red2[...]
+
+    @pl.loop(0, n_ex)
+    def _(j):
+        @pl.when(j != me_e)
+        def _():
+            ex_copy(red2, land3, s3, r3, j, j).wait_recv()
+            o_ref[j] = land3[j]
+            ex_copy(red2, land3, s3, r3, j, me_e).wait_send()
+
+
+def tail(summed, tokens, tokens_t, prob, part_comb, n_dp, n_ex):
+    width, experts = tokens_t.shape[0], prob.shape[1]
+    block = (width // n_ex, experts)
+    chunks = (n_ex,) + block
+    bf = jnp.bfloat16
+    vmem = pl.BlockSpec(memory_space=pltpu.VMEM)
+    gsa, logits, out = pl.pallas_call(
+        functools.partial(_tail_kernel, n_dp, n_ex, summed.shape[0] // n_ex),
+        out_shape=(jax.ShapeDtypeStruct(summed.shape, summed.dtype),
+                   jax.ShapeDtypeStruct(prob.shape, bf),
+                   jax.ShapeDtypeStruct(chunks, bf)),
+        in_specs=[vmem] * 5,
+        out_specs=(vmem, vmem, vmem),
+        scratch_shapes=[
+            pltpu.VMEM(summed.shape, summed.dtype),
+            pltpu.VMEM(chunks, bf),
+            pltpu.VMEM(chunks, bf),
+            pltpu.VMEM((n_dp,) + block, bf),
+            pltpu.VMEM(chunks, bf),
+            pltpu.VMEM(block, bf),
+            pltpu.VMEM(block, bf),
+            pltpu.SemaphoreType.DMA((n_ex,)),
+            pltpu.SemaphoreType.DMA((n_ex,)),
+            pltpu.SemaphoreType.DMA(()),
+            pltpu.SemaphoreType.DMA((n_ex,)),
+            pltpu.SemaphoreType.DMA((n_ex,)),
+            pltpu.SemaphoreType.DMA((n_dp,)),
+            pltpu.SemaphoreType.DMA((n_dp,)),
+            pltpu.SemaphoreType.DMA((n_ex,)),
+            pltpu.SemaphoreType.DMA((n_ex,)),
+        ],
+        compiler_params=pltpu.CompilerParams(collective_id=5, has_side_effects=True),
+    )(summed, tokens, tokens_t, prob, part_comb)
+    return gsa, logits, out.reshape(width, experts).astype(jnp.float32)
+
+
 def local(n_dp, n_expert, tokens, router, weight_in, weight_out, cotangent):
     experts_dev = weight_in.shape[0]
     width = tokens.shape[2]
@@ -316,29 +471,25 @@
         grad_second,
         partial_back.astype(jnp.bfloat16).reshape(grad_rows.shape),
     )
-    grad_slot_all = from_owners(partial_back, 3)
+    summed_back = lax.psum_scatter(partial_back, "dp", scatter_dimension=0, tiled=True)[0]
     mixed = jnp.einsum(
         "ise,ied->isd", combine, expert_outs, preferred_element_type=jnp.float32
     ).astype(jnp.bfloat16)
     grad_comb = jnp.einsum(
         "isd,ied->ise", cotangent, expert_outs, preferred_element_type=jnp.float32
     )
-    grad_disp = jnp.einsum(
-        "isd,ied->ise", tokens, grad_slot_all, preferred_element_type=jnp.float32
-    )
-    part_disp = dispatch_prob * (
-        grad_disp - jnp.sum(dispatch_prob * grad_disp, axis=1, keepdims=True)
-    )
     part_comb = combine_prob * (
         grad_comb - jnp.sum(combine_prob * grad_comb, axis=2, keepdims=True)
     )
-    grad_logits = (part_disp + part_comb).astype(jnp.bfloat16)
+    gsa, logits, grad_router = tail(
+        summed_back, tokens[0], tokens[0].T, dispatch_prob[0], part_comb[0], n_dp, n_expert
+    )
+    grad_slot_all = gsa[None]
+    grad_logits = logits[None]
     grad_tokens = (
         jnp.einsum("ise,ied->isd", dispatch, grad_slot_all, preferred_element_type=jnp.float32)
         + jnp.einsum("ise,de->isd", grad_logits, router, preferred_element_type=jnp.float32)
     ).astype(jnp.bfloat16)
-    router_term = jnp.einsum("isd,ise->de", tokens, grad_logits, preferred_element_type=jnp.float32)
-    grad_router = all_sum(router_term, n_dp, n_expert)
     return (mixed, grad_tokens, grad_router, grad_first, grad_second)
 
 

time: 241 us -> 234 us (0.971)
  Pallas kernels: 75.8 us -> 70.9 us
  waiting for transfers between devices: 89.1 us -> 85.4 us
    reduce_scatter x2 -> x1, waiting for transfers between devices: 47.3 us -> 15.4 us  [from_owners(): lax.psum_scatter(partial_value, 'dp', scatter_dimension=0, tiled=True)]
    reduce_scatter x0 -> x1, waiting for transfers between devices: none -> 28.7 us  [local(): lax.psum_scatter(partial_back, 'dp', scatter_dimension=0, tiled=True)[0]]
    pallas_call x4 -> x3, Pallas kernels: 47.7 us -> 36 us  [row_exchange(): pl.pallas_call(functools.partial(_row_exchange_kernel, n, x.shape[0] // n...]
    pallas_call x1, Pallas kernels: 28.1 us -> 34.9 us  [tail(): pl.pallas_call(functools.partial(_tail_kernel, n_dp, n_ex, summed.shape[0...]
    unnamed x12 -> x25, local copies, waits for them, and re-layouts: 0.04 us -> 2.86 us
  transfers between devices with their start and end apart: 4 -> 4, of which waited for: 4 -> 4; matrix products, arithmetic and copies ran while one was open for 21% -> 22% of each run, Pallas kernels for 9% -> 10%
where the time goes in v11:
time: 234 us; the launch traced here: 233 us
  waiting for transfers between devices  85.4 us (36%)
  Pallas kernels  70.9 us (30%)
  matrix products  30 us (13%)
  local copies, waits for them, and re-layouts  29.2 us (12%)
  between operations  13.9 us (6%)
  other arithmetic  2.86 us (1%)
    all_gather x2, waiting for transfers between devices, to_owners(): return lax.all_gather(arrived, 'dp', axis=0, tiled=True)  41.2 us
    pallas_call x3, Pallas kernels, row_exchange(): pl.pallas_call(functools.partial(_row_exchange_kernel, n, x.shape[0] // n...  36 us
    pallas_call x1, Pallas kernels, tail(): pl.pallas_call(functools.partial(_tail_kernel, n_dp, n_ex, summed.shape[0...  34.9 us
    reduce_scatter x1, waiting for transfers between devices, local(): lax.psum_scatter(partial_back, 'dp', scatter_dimension=0, tiled=True)[0]  28.7 us
    reduce_scatter x1, waiting for transfers between devices, from_owners(): lax.psum_scatter(partial_value, 'dp', scatter_dimension=0, tiled=True)  15.4 us
    reshape x2, local copies, waits for them, and re-layouts, local(): blocks = slot_rows.reshape(-1, experts_dev, width)  8.36 us
    dot_general x1, matrix products, local(): jnp.einsum('rkd,kfd->rkf', grad_blocks, weight_out, preferred_element_typ...  5.73 us
    dot_general x1, matrix products, local(): jnp.einsum('rkd,kdf->rkf', blocks, weight_in, preferred_element_type=jnp....  5.47 us
  transfers between devices with their start and end apart: 4, of which 4 were waited for; matrix products, arithmetic and copies ran while one was open for 22% of the time, Pallas kernels for 10%

profile of v11, /device:TPU:1, one launch (start us, length us, event | category | flops | bytes accessed | tf_op | source)
XLA Modules:
  0.0 232.7 jit_solution(580301745843012670)
XLA Ops:
  7.2 0.0 copy-start
  7.2 0.0 copy-start.9
  7.2 0.0 all-gather.5.cloned.1.call-start
  7.2 1.7 fusion.48
  8.9 0.1 copy.11
  9.0 0.2 fusion.35
  9.3 0.0 copy-start.6
  9.3 2.0 convolution_convert_fusion.4.x_ref
  11.3 13.7 %shard_map.92 = bf16[128,1024]{1,0:T(8,128)(2,1)} custom-call(bf16[128,1024]{1,0:T(8,128)(2,1)} %convolution_convert_fusion.4.x_ref), custom_call_target="tpu_custom_call" | custom-call | tf_op jit(solution)/shard_map/pallas_call | solution.py:131
  25.0 0.0 all-gather.5.cloned.1.call-update
  25.0 0.0 all-gather.7.cloned.1.call-start
  25.1 0.0 copy-done.9
  25.1 1.1 convolution_convert_fusion.3.x_ref
  26.2 11.4 %shard_map.94 = bf16[128,1024]{1,0:T(8,128)(2,1)} custom-call(bf16[128,1024]{1,0:T(8,128)(2,1)} %convolution_convert_fusion.3.x_ref), custom_call_target="tpu_custom_call" | custom-call | tf_op jit(solution)/shard_map/pallas_call | solution.py:131
  37.6 0.0 all-gather.7.cloned.1.call-update
  37.6 0.0 reduce-scatter.3.cloned.1.call-start
  37.7 27.0 %all-gather.5.cloned.1.call-done = bf16[1024,1024]{1,0:T(8,128)(2,1)} async-done(((bf16[128,1024]{1,0:T(8,128)(2,1)}), bf16[1024,1024]{1,0:T(8,128)(2,1)}) %all-gather.5.cloned.1.call-update) | async-done | bytes 2097168 | tf_op jit(solution)/shard_map/all_gather | solution.py:433
  64.6 4.1 %reshape.102 = bf16[256,4,1024]{2,1,0:T(4,128)(2,1)} reshape(bf16[1024,1024]{1,0:T(8,128)(2,1)} %all-gather.5.cloned.1.call-done) | data formatting | bytes 4194304 | tf_op jit(solution)/shard_map/reshape | solution.py:440
  68.7 0.0 copy-done.6
  68.7 4.3 %copy.19 = bf16[256,4,1024]{0,2,1:T(8,128)(2,1)} copy(bf16[256,4,1024]{2,1,0:T(4,128)(2,1)} %reshape.102) | data formatting | bytes 4194304 | tf_op jit(solution)/shard_map/reshape | solution.py:440
  73.0 0.0 copy-done
  73.0 0.0 copy-start.5
  73.0 5.5 %fusion.11 = (bf16[256,4,256]{2,0,1:T(8,128)(2,1)S(1)}, f32[4,256,256]{2,1,0:T(8,128)}) fusion(bf16[256,4,1024]{0,2,1:T(8,128)(2,1)} %copy.19, bf16[4,1024,256]{2,1,0:T(8,128)(2,1)S(1)} %copy-done), kind=kOutput, calls=%fused_computation.25 | convolution fusion | flops 553910272 | bytes 5767168 | tf_op jit(solution)/shard_map/rkd,kdf->rkf/dot_general | solution.py:441
  78.5 0.0 copy-done.5
  78.5 0.7 convert_bitcast_fusion.1
  79.2 2.9 %copy.14 = bf16[256,4,1024]{2,1,0:T(4,128)(2,1)} copy(bf16[256,4,1024]{2,0,1:T(8,128)(2,1)S(1)} %convert_bitcast_fusion.1) | data formatting | bytes 4194304 | tf_op jit(solution)/shard_map/convert_element_type | solution.py:450
  82.2 4.0 %reshape.103 = bf16[8,128,1024]{2,1,0:T(8,128)(2,1)} reshape(bf16[256,4,1024]{2,1,0:T(4,128)(2,1)} %copy.14) | data formatting | bytes 4194304 | tf_op jit(solution)/shard_map/reshape | solution.py:450
  86.1 0.0 reduce-scatter.3.cloned.1.call-update
  86.1 0.2 reduce-scatter.5.cloned.1.call-start
  86.4 14.3 %all-gather.7.cloned.1.call-done = bf16[1024,1024]{1,0:T(8,128)(2,1)} async-done(((bf16[128,1024]{1,0:T(8,128)(2,1)}), bf16[1024,1024]{1,0:T(8,128)(2,1)}) %all-gather.7.cloned.1.call-update) | async-done | bytes 2097168 | tf_op jit(solution)/shard_map/all_gather | solution.py:433
  100.6 4.1 %reshape.105 = bf16[256,4,1024]{2,1,0:T(4,128)(2,1)} reshape(bf16[1024,1024]{1,0:T(8,128)(2,1)} %all-gather.7.cloned.1.call-done) | data formatting | bytes 4194304 | tf_op jit(solution)/shard_map/reshape | solution.py:454
  104.7 5.7 %fusion.17 = bf16[256,4,256]{2,0,1:T(8,128)(2,1)S(1)} fusion(bf16[4,256,1024]{2,1,0:T(8,128)(2,1)} %param.8, bf16[256,4,1024]{2,1,0:T(4,128)(2,1)} %reshape.105, f32[4,256,256]{2,1,0:T(8,128)} %get-tuple-element.17), kind=kOutput, calls=%fused_computation.31 | convolution fusion | flops 555745280 | bytes 5767168 | tf_op jit(solution)/shard_map/rkd,kfd->rkf/dot_general | solution.py:455
  110.5 0.0 copy-start.3
  110.5 0.8 copy-done.3
  111.3 0.7 convert_bitcast_fusion
  112.0 2.9 %copy.16 = bf16[256,4,1024]{2,1,0:T(4,128)(2,1)} copy(bf16[256,4,1024]{2,0,1:T(8,128)(2,1)S(1)} %convert_bitcast_fusion) | data formatting | bytes 4194304 | tf_op jit(solution)/shard_map/convert_element_type | solution.py:472
  115.0 4.0 %reshape.106 = bf16[8,128,1024]{2,1,0:T(8,128)(2,1)} reshape(bf16[256,4,1024]{2,1,0:T(4,128)(2,1)} %copy.16) | data formatting | bytes 4194304 | tf_op jit(solution)/shard_map/reshape | solution.py:472
  118.9 0.0 copy-start.1
  118.9 0.0 reduce-scatter.5.cloned.1.call-update
  119.0 1.0 copy-done.1
  120.0 1.0 copy.10
  121.0 0.0 copy-start.2
  121.0 0.0 copy-start.4
  121.0 4.6 %convolution_convert_fusion = bf16[4,256,1024]{2,1,0:T(8,128)(2,1)} fusion(bf16[256,4,256]{2,0,1:T(8,128)(2,1)S(1)} %get-tuple-element.16, bf16[256,4,1024]{2,1,0:T(4,128)(2,1)} %reshape.105), kind=kOutput, calls=%fused_computation.2 | convolution fusion | flops 537919488 | bytes 4718592 | tf_op jit(solution)/shard_map/rkf,rkd->kfd/dot_general | solution.py:460
  125.6 0.0 copy-done.2
  125.6 0.0 copy-done.4
  125.6 0.0 copy-start.10
  125.7 2.0 convolution_convert_fusion.1
  127.7 15.4 %reduce-scatter.3.cloned.1.call-done = bf16[1,128,1024]{2,1,0:T(8,128)(2,1)} async-done(((bf16[8,128,1024]{2,1,0:T(8,128)(2,1)}), bf16[1,128,1024]{2,1,0:T(8,128)(2,1)}) %reduce-scatter.3.cloned.1.call-update) | async-done | bytes 262160 | tf_op jit(solution)/shard_map/reduce_scatter | solution.py:436
  143.1 10.9 %shard_map.93 = bf16[128,1024]{1,0:T(8,128)(2,1)} custom-call(bf16[128,1024]{1,0:T(8,128)(2,1)} %bitcast.132), custom_call_target="tpu_custom_call" | custom-call | tf_op jit(solution)/shard_map/pallas_call | solution.py:131
  154.0 2.1 fusion.7
  156.1 0.0 copy-done.10
  156.1 1.4 multiply_reduce_fusion
  157.5 0.0 copy-start.8
  157.5 0.8 subtract_multiply_fusion.comb_ref
  158.3 28.7 %reduce-scatter.5.cloned.1.call-done = bf16[1,128,1024]{2,1,0:T(8,128)(2,1)} async-done(((bf16[8,128,1024]{2,1,0:T(8,128)(2,1)}), bf16[1,128,1024]{2,1,0:T(8,128)(2,1)}) %reduce-scatter.5.cloned.1.call-update) | async-done | bytes 262160 | tf_op jit(solution)/shard_map/reduce_scatter | solution.py:474
  187.0 34.9 %shard_map.95 = (bf16[128,1024]{1,0:T(8,128)(2,1)}, bf16[256,128]{1,0:T(8,128)(2,1)}, bf16[32,32,128]{2,1,0:T(8,128)(2,1)}) custom-call(bf16[128,1024]{1,0:T(8,128)(2,1)} %bitcast.133, bf16[256,1024]{1,0:T(8,128)(2,1)} %bitcast.130, bf16[1024,256]{1,0:T(8,128)(2,1)} %bitcast.131, f32[256,128]{1,0:T(8,128)} %copy-done.6, ...), custom_call_target="tpu_custom_call" | custom-call | tf_op jit(solution)/shard_map/pallas_call | solution.py:386
  221.9 0.0 copy-start.11
  222.0 1.8 bitcast_convert_fusion
  223.8 0.0 copy-done.7
  223.8 1.2 fusion.38
  225.0 0.0 copy-done.8
  225.0 0.0 copy-done.11
  225.0 1.1 fusion.8
  (2 shorter events, 0.0 us)
Async XLA Ops:
  7.2 65.8 %copy-start = (bf16[4,1024,256]{2,1,0:T(8,128)(2,1)S(1)}, bf16[4,1024,256]{2,1,0:T(8,128)(2,1)}, u32[]{:S(2)}) copy-start(bf16[4,1024,256]{2,1,0:T(8,128)(2,1)} %param.7) | copy-start | bytes 6291460
  7.2 17.9 %copy-start.9 = (bf16[1,256,1024]{2,1,0:T(8,128)(2,1)S(1)}, bf16[1,256,1024]{2,1,0:T(8,128)(2,1)}, u32[]{:S(2)}) copy-start(bf16[1,256,1024]{2,1,0:T(8,128)(2,1)} %param.9) | copy-start | bytes 1572868
  7.2 57.4 %all-gather.5.cloned.1.call-start = ((), (), s32[]{:S(2)}) async-start(), calls=%async_computation.4 | async-start | bytes 2359296 | tf_op jit(solution)/shard_map/all_gather | solution.py:433
  9.3 59.5 %copy-start.6 = (f32[256,128]{1,0:T(8,128)}, f32[256,128]{1,0:T(8,128)S(1)}, u32[]{:S(2)}) copy-start(f32[256,128]{1,0:T(8,128)S(1)} %fusion.36.prob_ref) | copy-start | bytes 393220
  25.0 75.6 %all-gather.7.cloned.1.call-start = ((), (), s32[]{:S(2)}) async-start(), calls=%async_computation.5 | async-start | bytes 2359296 | tf_op jit(solution)/shard_map/all_gather | solution.py:433
  37.6 105.5 %reduce-scatter.3.cloned.1.call-start = ((), (), s32[]{:S(2)}) async-start(), calls=%async_computation.2 | async-start | bytes 2359296 | tf_op jit(solution)/shard_map/reduce_scatter | solution.py:436
  73.0 5.5 %copy-start.5 = (bf16[4,256,1024]{2,1,0:T(8,128)(2,1)S(1)}, bf16[4,256,1024]{2,1,0:T(8,128)(2,1)}, u32[]{:S(2)}) copy-start(bf16[4,256,1024]{2,1,0:T(8,128)(2,1)} %param.8) | copy-start | bytes 6291460
  86.1 100.9 %reduce-scatter.5.cloned.1.call-start = ((), (), s32[]{:S(2)}) async-start(), calls=%async_computation.3 | async-start | bytes 2359296 | tf_op jit(solution)/shard_map/reduce_scatter | solution.py:474
  110.5 0.8 copy-start.3
  118.9 1.1 copy-start.1
  121.0 4.6 %copy-start.2 = (bf16[256,4,1024]{0,2,1:T(8,128)(2,1)S(1)}, bf16[256,4,1024]{0,2,1:T(8,128)(2,1)}, u32[]{:S(2)}) copy-start(bf16[256,4,1024]{0,2,1:T(8,128)(2,1)} %copy.19) | copy-start | bytes 6291460
  121.0 4.6 %copy-start.4 = (bf16[256,4,256]{2,0,1:T(8,128)(2,1)S(1)}, bf16[256,4,256]{2,0,1:T(8,128)(2,1)}, u32[]{:S(2)}) copy-start(bf16[256,4,256]{2,0,1:T(8,128)(2,1)} %copy-done.3) | copy-start | bytes 1572868
  125.6 30.5 %copy-start.10 = (bf16[1,256,1024]{2,1,0:T(8,128)(2,1)S(1)}, bf16[1,256,1024]{2,1,0:T(8,128)(2,1)}, u32[]{:S(2)}) copy-start(bf16[1,256,1024]{2,1,0:T(8,128)(2,1)} %param.9) | copy-start | bytes 1572868
  156.1 67.7 %copy-start.7 = (f32[256,128]{1,0:T(8,128)S(1)}, f32[256,128]{1,0:T(8,128)}, u32[]{:S(2)}) copy-start(f32[256,128]{1,0:T(8,128)} %copy-done.6) | copy-start | bytes 393220
  157.5 67.5 %copy-start.8 = (bf16[1024,128]{1,0:T(8,128)(2,1)S(1)}, bf16[1024,128]{1,0:T(8,128)(2,1)}, u32[]{:S(2)}) copy-start(bf16[1024,128]{1,0:T(8,128)(2,1)} %param.6) | copy-start | bytes 786436
  221.9 3.1 %copy-start.11 = (bf16[256,128]{1,0:T(8,128)(2,1)S(1)}, bf16[256,128]{1,0:T(8,128)(2,1)}, u32[]{:S(2)}) copy-start(bf16[256,128]{1,0:T(8,128)(2,1)} %get-tuple-element.9) | copy-start | bytes 196612
Sparse Core Ops, SparseCore 0:
  25.1 39.4 all-gather.4
  66.5 34.0 all-gather.6
  103.2 39.8 reduce-scatter.2
  145.5 41.4 reduce-scatter.4

commit v12 on v11

--- a/solution.py
+++ b/solution.py
@@ -258,8 +258,8 @@
     return out.reshape(rows, cols).astype(value.dtype)
 
 
-def _tail_kernel(n_dp, n_ex, rows, summed_ref, tok_ref, tokt_ref, prob_ref, comb_ref,
-                 gsa_ref, logit_ref, o_ref,
+def _tail_kernel(n_dp, n_ex, rows, summed_ref, tok_ref, tokt_ref, prob_ref, comb_ref, disp_ref, router_ref,
+                 gtok_ref, o_ref,
                  land0, xs, land1, land2, land3, red1, red2, s0, r0, own_sem, s1, r1, s2, r2, s3, r3):
     me_d = lax.axis_index("dp")
     me_e = lax.axis_index("expert")
@@ -304,12 +304,10 @@
 
     own.wait()
     gsa = land0[...]
-    gsa_ref[...] = gsa
     prob = prob_ref[...]
     grad_disp = lax.dot_general(tok_ref[...], gsa, (((1,), (1,)), ((), ())), preferred_element_type=jnp.float32)
     part_disp = prob * (grad_disp - jnp.sum(prob * grad_disp, axis=0, keepdims=True))
-    logits = (part_disp + comb_ref[...]).astype(logit_ref.dtype)
-    logit_ref[...] = logits
+    logits = (part_disp + comb_ref[...]).astype(jnp.bfloat16)
     term = jnp.dot(tokt_ref[...], logits, preferred_element_type=jnp.float32)
     xs[...] = term.astype(xs.dtype).reshape(xs.shape)
 
@@ -330,6 +328,9 @@
             ex_copy(xs.at[j], land1, s1, r1, j, me_e).start()
 
     land1[me_e] = xs[me_e]
+    back = jnp.dot(disp_ref[...], gsa, preferred_element_type=jnp.float32)
+    back = back + lax.dot_general(logits, router_ref[...], (((1,), (1,)), ((), ())), preferred_element_type=jnp.float32)
+    gtok_ref[...] = back.astype(gtok_ref.dtype)
 
     @pl.loop(0, n_ex)
     def _(j):
@@ -377,19 +378,18 @@
             ex_copy(red2, land3, s3, r3, j, me_e).wait_send()
 
 
-def tail(summed, tokens, tokens_t, prob, part_comb, n_dp, n_ex):
+def tail(summed, tokens, tokens_t, prob, part_comb, dispatch, router, n_dp, n_ex):
     width, experts = tokens_t.shape[0], prob.shape[1]
     block = (width // n_ex, experts)
     chunks = (n_ex,) + block
     bf = jnp.bfloat16
     vmem = pl.BlockSpec(memory_space=pltpu.VMEM)
-    gsa, logits, out = pl.pallas_call(
+    grad_tokens, out = pl.pallas_call(
         functools.partial(_tail_kernel, n_dp, n_ex, summed.shape[0] // n_ex),
-        out_shape=(jax.ShapeDtypeStruct(summed.shape, summed.dtype),
-                   jax.ShapeDtypeStruct(prob.shape, bf),
+        out_shape=(jax.ShapeDtypeStruct(tokens.shape, bf),
                    jax.ShapeDtypeStruct(chunks, bf)),
-        in_specs=[vmem] * 5,
-        out_specs=(vmem, vmem, vmem),
+        in_specs=[vmem] * 7,
+        out_specs=(vmem, vmem),
         scratch_shapes=[
             pltpu.VMEM(summed.shape, summed.dtype),
             pltpu.VMEM(chunks, bf),
@@ -409,8 +409,8 @@
             pltpu.SemaphoreType.DMA((n_ex,)),
         ],
         compiler_params=pltpu.CompilerParams(collective_id=5, has_side_effects=True),
-    )(summed, tokens, tokens_t, prob, part_comb)
-    return gsa, logits, out.reshape(width, experts).astype(jnp.float32)
+    )(summed, tokens, tokens_t, prob, part_comb, dispatch, router)
+    return grad_tokens, out.reshape(width, experts).astype(jnp.float32)
 
 
 def local(n_dp, n_expert, tokens, router, weight_in, weight_out, cotangent):
@@ -481,15 +481,11 @@
     part_comb = combine_prob * (
         grad_comb - jnp.sum(combine_prob * grad_comb, axis=2, keepdims=True)
     )
-    gsa, logits, grad_router = tail(
-        summed_back, tokens[0], tokens[0].T, dispatch_prob[0], part_comb[0], n_dp, n_expert
-    )
-    grad_slot_all = gsa[None]
-    grad_logits = logits[None]
-    grad_tokens = (
-        jnp.einsum("ise,ied->isd", dispatch, grad_slot_all, preferred_element_type=jnp.float32)
-        + jnp.einsum("ise,de->isd", grad_logits, router, preferred_element_type=jnp.float32)
-    ).astype(jnp.bfloat16)
+    grad_tokens, grad_router = tail(
+        summed_back, tokens[0], tokens[0].T, dispatch_prob[0], part_comb[0], dispatch[0], router,
+        n_dp, n_expert,
+    )
+    grad_tokens = grad_tokens[None]
     return (mixed, grad_tokens, grad_router, grad_first, grad_second)
 
 

time: 234 us -> 234 us (level)
  matrix products: 30 us -> 27.6 us
    unnamed x25 -> x20, local copies, waits for them, and re-layouts: 2.86 us -> 4.72 us
where the time goes in v12:
time: 234 us; the launch traced here: 233 us
  waiting for transfers between devices  85.2 us (36%)
  Pallas kernels  71.1 us (30%)
  local copies, waits for them, and re-layouts  31.1 us (13%)
  matrix products  27.6 us (12%)
  between operations  13.9 us (6%)
  other arithmetic  3.49 us (1%)
    all_gather x2, waiting for transfers between devices, to_owners(): return lax.all_gather(arrived, 'dp', axis=0, tiled=True)  41.2 us
    pallas_call x3, Pallas kernels, row_exchange(): pl.pallas_call(functools.partial(_row_exchange_kernel, n, x.shape[0] // n...  36.4 us
    pallas_call x1, Pallas kernels, tail(): pl.pallas_call(functools.partial(_tail_kernel, n_dp, n_ex, summed.shape[0...  34.7 us
    reduce_scatter x1, waiting for transfers between devices, local(): lax.psum_scatter(partial_back, 'dp', scatter_dimension=0, tiled=True)[0]  29 us
    reduce_scatter x1, waiting for transfers between devices, from_owners(): lax.psum_scatter(partial_value, 'dp', scatter_dimension=0, tiled=True)  14.9 us
    reshape x2, local copies, waits for them, and re-layouts, local(): blocks = slot_rows.reshape(-1, experts_dev, width)  8.36 us
    dot_general x1, matrix products, local(): jnp.einsum('rkd,kfd->rkf', grad_blocks, weight_out, preferred_element_typ...  5.73 us
    dot_general x1, matrix products, local(): jnp.einsum('rkd,kdf->rkf', blocks, weight_in, preferred_element_type=jnp....  5.48 us
  transfers between devices with their start and end apart: 4, of which 4 were waited for; matrix products, arithmetic and copies ran while one was open for 22% of the time, Pallas kernels for 10%

profile of v12, /device:TPU:1, one launch (start us, length us, event | category | flops | bytes accessed | tf_op | source)
XLA Modules:
  0.0 232.7 jit_solution(1520441555572313003)
XLA Ops:
  7.2 0.0 copy-start
  7.2 0.0 copy-start.7
  7.2 0.0 all-gather.5.cloned.1.call-start
  7.2 1.7 fusion.43
  8.9 0.1 copy.11
  9.0 0.2 fusion.33
  9.2 0.7 fusion.44
  9.9 0.0 copy-start.6
  9.9 2.0 convolution_convert_fusion.4.x_ref
  11.9 13.7 %shard_map.92 = bf16[128,1024]{1,0:T(8,128)(2,1)} custom-call(bf16[128,1024]{1,0:T(8,128)(2,1)} %convolution_convert_fusion.4.x_ref), custom_call_target="tpu_custom_call" | custom-call | tf_op jit(solution)/shard_map/pallas_call | solution.py:131
  25.6 0.0 all-gather.5.cloned.1.call-update
  25.6 0.0 all-gather.7.cloned.1.call-start
  25.7 0.0 copy-done.7
  25.7 1.1 convolution_convert_fusion.3.x_ref
  26.8 11.4 %shard_map.94 = bf16[128,1024]{1,0:T(8,128)(2,1)} custom-call(bf16[128,1024]{1,0:T(8,128)(2,1)} %convolution_convert_fusion.3.x_ref), custom_call_target="tpu_custom_call" | custom-call | tf_op jit(solution)/shard_map/pallas_call | solution.py:131
  38.2 0.0 all-gather.7.cloned.1.call-update
  38.2 0.0 reduce-scatter.3.cloned.1.call-start
  38.3 25.7 %all-gather.5.cloned.1.call-done = bf16[1024,1024]{1,0:T(8,128)(2,1)} async-done(((bf16[128,1024]{1,0:T(8,128)(2,1)}), bf16[1024,1024]{1,0:T(8,128)(2,1)}) %all-gather.5.cloned.1.call-update) | async-done | bytes 2097168 | tf_op jit(solution)/shard_map/all_gather | solution.py:433
  64.0 4.1 %reshape.93 = bf16[256,4,1024]{2,1,0:T(4,128)(2,1)} reshape(bf16[1024,1024]{1,0:T(8,128)(2,1)} %all-gather.5.cloned.1.call-done) | data formatting | bytes 4194304 | tf_op jit(solution)/shard_map/reshape | solution.py:440
  68.0 0.0 copy-done.6
  68.1 4.3 %copy.19 = bf16[256,4,1024]{0,2,1:T(8,128)(2,1)} copy(bf16[256,4,1024]{2,1,0:T(4,128)(2,1)} %reshape.93) | data formatting | bytes 4194304 | tf_op jit(solution)/shard_map/reshape | solution.py:440
  72.3 0.0 copy-done
  72.3 0.0 copy-start.5
  72.3 5.5 %fusion.9 = (bf16[256,4,256]{2,0,1:T(8,128)(2,1)S(1)}, f32[4,256,256]{2,1,0:T(8,128)}) fusion(bf16[256,4,1024]{0,2,1:T(8,128)(2,1)} %copy.19, bf16[4,1024,256]{2,1,0:T(8,128)(2,1)S(1)} %copy-done), kind=kOutput, calls=%fused_computation.22 | convolution fusion | flops 553910272 | bytes 5767168 | tf_op jit(solution)/shard_map/rkd,kdf->rkf/dot_general | solution.py:441
  77.8 0.0 copy-done.5
  77.8 0.7 convert_bitcast_fusion.1
  78.5 2.9 %copy.14 = bf16[256,4,1024]{2,1,0:T(4,128)(2,1)} copy(bf16[256,4,1024]{2,0,1:T(8,128)(2,1)S(1)} %convert_bitcast_fusion.1) | data formatting | bytes 4194304 | tf_op jit(solution)/shard_map/convert_element_type | solution.py:450
  81.5 4.0 %reshape.94 = bf16[8,128,1024]{2,1,0:T(8,128)(2,1)} reshape(bf16[256,4,1024]{2,1,0:T(4,128)(2,1)} %copy.14) | data formatting | bytes 4194304 | tf_op jit(solution)/shard_map/reshape | solution.py:450
  85.4 0.0 reduce-scatter.3.cloned.1.call-update
  85.5 0.2 reduce-scatter.5.cloned.1.call-start
  85.7 15.5 %all-gather.7.cloned.1.call-done = bf16[1024,1024]{1,0:T(8,128)(2,1)} async-done(((bf16[128,1024]{1,0:T(8,128)(2,1)}), bf16[1024,1024]{1,0:T(8,128)(2,1)}) %all-gather.7.cloned.1.call-update) | async-done | bytes 2097168 | tf_op jit(solution)/shard_map/all_gather | solution.py:433
  101.2 4.1 %reshape.96 = bf16[256,4,1024]{2,1,0:T(4,128)(2,1)} reshape(bf16[1024,1024]{1,0:T(8,128)(2,1)} %all-gather.7.cloned.1.call-done) | data formatting | bytes 4194304 | tf_op jit(solution)/shard_map/reshape | solution.py:454
  105.3 5.7 %fusion.15 = bf16[256,4,256]{2,0,1:T(8,128)(2,1)S(1)} fusion(bf16[4,256,1024]{2,1,0:T(8,128)(2,1)} %param.8, bf16[256,4,1024]{2,1,0:T(4,128)(2,1)} %reshape.96, f32[4,256,256]{2,1,0:T(8,128)} %get-tuple-element.17), kind=kOutput, calls=%fused_computation.28 | convolution fusion | flops 555745280 | bytes 5767168 | tf_op jit(solution)/shard_map/rkd,kfd->rkf/dot_general | solution.py:455
  111.0 0.0 copy-start.3
  111.1 0.8 copy-done.3
  111.8 0.7 convert_bitcast_fusion
  112.6 2.9 %copy.16 = bf16[256,4,1024]{2,1,0:T(4,128)(2,1)} copy(bf16[256,4,1024]{2,0,1:T(8,128)(2,1)S(1)} %convert_bitcast_fusion) | data formatting | bytes 4194304 | tf_op jit(solution)/shard_map/convert_element_type | solution.py:472
  115.5 4.0 %reshape.97 = bf16[8,128,1024]{2,1,0:T(8,128)(2,1)} reshape(bf16[256,4,1024]{2,1,0:T(4,128)(2,1)} %copy.16) | data formatting | bytes 4194304 | tf_op jit(solution)/shard_map/reshape | solution.py:472
  119.5 0.0 copy-start.2
  119.5 0.0 reduce-scatter.5.cloned.1.call-update
  119.5 1.0 copy-done.2
  120.5 1.0 copy.10
  121.5 0.0 copy-start.1
  121.6 0.0 copy-start.4
  121.6 4.6 %convolution_convert_fusion = bf16[4,256,1024]{2,1,0:T(8,128)(2,1)} fusion(bf16[256,4,256]{2,0,1:T(8,128)(2,1)S(1)} %get-tuple-element.16, bf16[256,4,1024]{2,1,0:T(4,128)(2,1)} %reshape.96), kind=kOutput, calls=%fused_computation.2 | convolution fusion | flops 537919488 | bytes 4718592 | tf_op jit(solution)/shard_map/rkf,rkd->kfd/dot_general | solution.py:460
  126.2 0.0 copy-done.1
  126.2 0.0 copy-done.4
  126.2 0.0 copy-start.8
  126.2 2.0 convolution_convert_fusion.1
  128.2 14.9 %reduce-scatter.3.cloned.1.call-done = bf16[1,128,1024]{2,1,0:T(8,128)(2,1)} async-done(((bf16[8,128,1024]{2,1,0:T(8,128)(2,1)}), bf16[1,128,1024]{2,1,0:T(8,128)(2,1)}) %reduce-scatter.3.cloned.1.call-update) | async-done | bytes 262160 | tf_op jit(solution)/shard_map/reduce_scatter | solution.py:436
  143.1 11.3 %shard_map.93 = bf16[128,1024]{1,0:T(8,128)(2,1)} custom-call(bf16[128,1024]{1,0:T(8,128)(2,1)} %bitcast.130), custom_call_target="tpu_custom_call" | custom-call | tf_op jit(solution)/shard_map/pallas_call | solution.py:131
  154.4 2.1 fusion.6
  156.5 0.0 copy-done.8
  156.5 1.4 multiply_reduce_fusion
  157.9 0.8 subtract_multiply_fusion.comb_ref
  158.7 29.0 %reduce-scatter.5.cloned.1.call-done = bf16[1,128,1024]{2,1,0:T(8,128)(2,1)} async-done(((bf16[8,128,1024]{2,1,0:T(8,128)(2,1)}), bf16[1,128,1024]{2,1,0:T(8,128)(2,1)}) %reduce-scatter.5.cloned.1.call-update) | async-done | bytes 262160 | tf_op jit(solution)/shard_map/reduce_scatter | solution.py:474
  187.7 34.7 %shard_map.95 = (bf16[256,1024]{1,0:T(8,128)(2,1)}, bf16[32,32,128]{2,1,0:T(8,128)(2,1)}) custom-call(bf16[128,1024]{1,0:T(8,128)(2,1)} %bitcast.131, bf16[256,1024]{1,0:T(8,128)(2,1)} %bitcast.127, bf16[1024,256]{1,0:T(8,128)(2,1)} %bitcast.128, f32[256,128]{1,0:T(8,128)} %get-tuple-element.14.prob_ref, f32[256,128]{1,0:T(8,128)} %subtract_multiply_fusion.comb_ref, ...), custom_call_target="tpu_custom_call" | custom-call | tf_op jit(solution)/shard_map/pallas_call | solution.py:387
  222.5 1.8 bitcast_convert_fusion
  224.3 1.9 copy.34
Async XLA Ops:
  7.2 65.2 %copy-start = (bf16[4,1024,256]{2,1,0:T(8,128)(2,1)S(1)}, bf16[4,1024,256]{2,1,0:T(8,128)(2,1)}, u32[]{:S(2)}) copy-start(bf16[4,1024,256]{2,1,0:T(8,128)(2,1)} %param.7) | copy-start | bytes 6291460
  7.2 18.5 %copy-start.7 = (bf16[1,256,1024]{2,1,0:T(8,128)(2,1)S(1)}, bf16[1,256,1024]{2,1,0:T(8,128)(2,1)}, u32[]{:S(2)}) copy-start(bf16[1,256,1024]{2,1,0:T(8,128)(2,1)} %param.9) | copy-start | bytes 1572868
  7.2 56.8 %all-gather.5.cloned.1.call-start = ((), (), s32[]{:S(2)}) async-start(), calls=%async_computation.4 | async-start | bytes 2359296 | tf_op jit(solution)/shard_map/all_gather | solution.py:433
  9.9 58.2 %copy-start.6 = (bf16[256,128]{1,0:T(8,128)(2,1)}, bf16[256,128]{1,0:T(8,128)(2,1)S(1)}, u32[]{:S(2)}) copy-start(bf16[256,128]{1,0:T(8,128)(2,1)S(1)} %get-tuple-element.13.disp_ref) | copy-start | bytes 196612
  25.6 75.6 %all-gather.7.cloned.1.call-start = ((), (), s32[]{:S(2)}) async-start(), calls=%async_computation.5 | async-start | bytes 2359296 | tf_op jit(solution)/shard_map/all_gather | solution.py:433
  38.2 104.9 %reduce-scatter.3.cloned.1.call-start = ((), (), s32[]{:S(2)}) async-start(), calls=%async_computation.2 | async-start | bytes 2359296 | tf_op jit(solution)/shard_map/reduce_scatter | solution.py:436
  72.3 5.5 %copy-start.5 = (bf16[4,256,1024]{2,1,0:T(8,128)(2,1)S(1)}, bf16[4,256,1024]{2,1,0:T(8,128)(2,1)}, u32[]{:S(2)}) copy-start(bf16[4,256,1024]{2,1,0:T(8,128)(2,1)} %param.8) | copy-start | bytes 6291460
  85.5 102.3 %reduce-scatter.5.cloned.1.call-start = ((), (), s32[]{:S(2)}) async-start(), calls=%async_computation.3 | async-start | bytes 2359296 | tf_op jit(solution)/shard_map/reduce_scatter | solution.py:474
  111.0 0.8 copy-start.3
  119.5 1.1 copy-start.2
  121.5 4.6 %copy-start.1 = (bf16[256,4,1024]{0,2,1:T(8,128)(2,1)S(1)}, bf16[256,4,1024]{0,2,1:T(8,128)(2,1)}, u32[]{:S(2)}) copy-start(bf16[256,4,1024]{0,2,1:T(8,128)(2,1)} %copy.19) | copy-start | bytes 6291460
  121.6 4.6 %copy-start.4 = (bf16[256,4,256]{2,0,1:T(8,128)(2,1)S(1)}, bf16[256,4,256]{2,0,1:T(8,128)(2,1)}, u32[]{:S(2)}) copy-start(bf16[256,4,256]{2,0,1:T(8,128)(2,1)} %copy-done.3) | copy-start | bytes 1572868
  126.2 30.3 %copy-start.8 = (bf16[1,256,1024]{2,1,0:T(8,128)(2,1)S(1)}, bf16[1,256,1024]{2,1,0:T(8,128)(2,1)}, u32[]{:S(2)}) copy-start(bf16[1,256,1024]{2,1,0:T(8,128)(2,1)} %param.9) | copy-start | bytes 1572868
Sparse Core Ops, SparseCore 0:
  25.7 38.1 all-gather.4
  65.8 35.3 all-gather.6
  103.8 39.3 reduce-scatter.2
  145.5 42.1 reduce-scatter.4

commit v13 on v11

--- a/solution.py
+++ b/solution.py
@@ -145,6 +145,76 @@
 
 def gelu_exact(values):
     return jax.nn.gelu(values, approximate=False)
+
+
+def _relay_sum_kernel(n_chip, x_ref, o_ref, land1, pair, land2, s1, r1, s2, r2):
+    me = lax.axis_index("dp")
+    fixed = lax.axis_index("expert")
+    core = me % 2
+    chip = me // 2
+    partner = me + 1 - 2 * core
+    mesh_id = pl.DeviceIdType.MESH
+    barrier = pltpu.get_barrier_semaphore()
+    pl.semaphore_signal(barrier, inc=1, device_id=(partner, fixed), device_id_type=mesh_id)
+    for h in range(n_chip):
+        @pl.when(h != chip)
+        def _():
+            pl.semaphore_signal(barrier, inc=1, device_id=(2 * h + core, fixed), device_id_type=mesh_id)
+    pl.semaphore_wait(barrier, n_chip)
+
+    def to_partner(h):
+        return pltpu.make_async_remote_copy(
+            src_ref=x_ref.at[2 * h + 1 - core], dst_ref=land1.at[h], send_sem=s1.at[h], recv_sem=r1.at[h],
+            device_id=(partner, fixed), device_id_type=mesh_id)
+
+    for h in range(n_chip):
+        to_partner(h).start()
+    for h in range(n_chip):
+        to_partner(h).wait_recv()
+        pair[h] = (x_ref[2 * h + core].astype(jnp.float32) + land1[h].astype(jnp.float32)).astype(pair.dtype)
+        to_partner(h).wait_send()
+
+    def to_chip(h, slot):
+        return pltpu.make_async_remote_copy(
+            src_ref=pair.at[h], dst_ref=land2.at[slot], send_sem=s2.at[h], recv_sem=r2.at[slot],
+            device_id=(2 * h + core, fixed), device_id_type=mesh_id)
+
+    for h in range(n_chip):
+        @pl.when(h != chip)
+        def _():
+            to_chip(h, chip).start()
+    land2[chip] = pair[chip]
+    for h in range(n_chip):
+        @pl.when(h != chip)
+        def _():
+            to_chip(h, h).wait_recv()
+            to_chip(h, chip).wait_send()
+    total = land2[0].astype(jnp.float32)
+    for h in range(1, n_chip):
+        total = total + land2[h].astype(jnp.float32)
+    o_ref[...] = total.astype(o_ref.dtype)
+
+
+def relay_sum(x, collective_id):
+    n_dp = x.shape[0]
+    n_chip = n_dp // 2
+    block = x.shape[1:]
+    return pl.pallas_call(
+        functools.partial(_relay_sum_kernel, n_chip),
+        out_shape=jax.ShapeDtypeStruct(block, x.dtype),
+        in_specs=[pl.BlockSpec(memory_space=pltpu.VMEM)],
+        out_specs=pl.BlockSpec(memory_space=pltpu.VMEM),
+        scratch_shapes=[
+            pltpu.VMEM((n_chip,) + block, x.dtype),
+            pltpu.VMEM((n_chip,) + block, x.dtype),
+            pltpu.VMEM((n_chip,) + block, x.dtype),
+            pltpu.SemaphoreType.DMA((n_chip,)),
+            pltpu.SemaphoreType.DMA((n_chip,)),
+            pltpu.SemaphoreType.DMA((n_chip,)),
+            pltpu.SemaphoreType.DMA((n_chip,)),
+        ],
+        compiler_params=pltpu.CompilerParams(collective_id=collective_id, has_side_effects=True),
+    )(x)
 
 
 def _allsum_kernel(n_dp, n_ex, x_ref, o_ref, land1, land2, land3, red1, red2, s1, r1, s2, r2, s3, r3):
@@ -433,8 +503,8 @@
         return lax.all_gather(arrived, "dp", axis=0, tiled=True)
 
     def from_owners(partial_value, cid):
-        summed = lax.psum_scatter(partial_value, "dp", scatter_dimension=0, tiled=True)
-        return row_exchange(summed[0], n_expert, cid)[None]
+        summed = relay_sum(partial_value, cid + 8)
+        return row_exchange(summed, n_expert, cid)[None]
 
     slot_rows = to_owners(slots, 0)
     blocks = slot_rows.reshape(-1, experts_dev, width)

time: 234 us -> 242 us (1.034)
  Pallas kernels: 70.9 us -> 115 us
  waiting for transfers between devices: 85.4 us -> 49.5 us
    pallas_call x0 -> x1, Pallas kernels: none -> 33 us  [relay_sum(): pl.pallas_call(functools.partial(_relay_sum_kernel, n_chip), out_shape=ja...]
    reduce_scatter x1, waiting for transfers between devices: 28.7 us -> 0.01 us  [local(): lax.psum_scatter(partial_back, 'dp', scatter_dimension=0, tiled=True)[0]]
    reduce_scatter x1 -> x0, waiting for transfers between devices: 15.4 us -> none  [from_owners(): lax.psum_scatter(partial_value, 'dp', scatter_dimension=0, tiled=True)]
    pallas_call x1, Pallas kernels: 34.9 us -> 43.3 us  [tail(): pl.pallas_call(functools.partial(_tail_kernel, n_dp, n_ex, summed.shape[0...]
    all_gather x2, waiting for transfers between devices: 41.2 us -> 49.4 us  [to_owners(): return lax.all_gather(arrived, 'dp', axis=0, tiled=True)]
    pallas_call x3, Pallas kernels: 36 us -> 39.2 us  [row_exchange(): pl.pallas_call(functools.partial(_row_exchange_kernel, n, x.shape[0] // n...]
  transfers between devices with their start and end apart: 4 -> 3, of which waited for: 4 -> 2; matrix products, arithmetic and copies ran while one was open for 22% -> 14% of each run, Pallas kernels for 10% -> 24%
where the time goes in v13:
time: 242 us; the launch traced here: 241 us
  Pallas kernels  115 us (48%)
  waiting for transfers between devices  49.5 us (20%)
  matrix products  29.8 us (12%)
  local copies, waits for them, and re-layouts  29.2 us (12%)
  between operations  13.9 us (6%)
  other arithmetic  2.88 us (1%)
    all_gather x2, waiting for transfers between devices, to_owners(): return lax.all_gather(arrived, 'dp', axis=0, tiled=True)  49.4 us
    pallas_call x1, Pallas kernels, tail(): pl.pallas_call(functools.partial(_tail_kernel, n_dp, n_ex, summed.shape[0...  43.3 us
    pallas_call x3, Pallas kernels, row_exchange(): pl.pallas_call(functools.partial(_row_exchange_kernel, n, x.shape[0] // n...  39.2 us
    pallas_call x1, Pallas kernels, relay_sum(): pl.pallas_call(functools.partial(_relay_sum_kernel, n_chip), out_shape=ja...  33 us
    reshape x2, local copies, waits for them, and re-layouts, local(): blocks = slot_rows.reshape(-1, experts_dev, width)  8.36 us
    dot_general x1, matrix products, local(): jnp.einsum('rkd,kfd->rkf', grad_blocks, weight_out, preferred_element_typ...  5.77 us
    dot_general x1, matrix products, local(): jnp.einsum('rkd,kdf->rkf', blocks, weight_in, preferred_element_type=jnp....  5.3 us
  transfers between devices with their start and end apart: 3, of which 2 were waited for; matrix products, arithmetic and copies ran while one was open for 14% of the time, Pallas kernels for 24%

profile of v13, /device:TPU:1, one launch (start us, length us, event | category | flops | bytes accessed | tf_op | source)
XLA Modules:
  0.0 240.9 jit_solution(13559191202074666979)
XLA Ops:
  7.2 0.0 copy-start
  7.2 0.0 copy-start.9
  7.2 0.0 all-gather.5.cloned.1.call-start
  7.2 1.7 fusion.48
  8.9 0.1 copy.11
  9.0 0.2 fusion.35
  9.3 0.0 copy-start.6
  9.3 2.0 convolution_convert_fusion.4.x_ref
  11.3 13.7 %shard_map.92 = bf16[128,1024]{1,0:T(8,128)(2,1)} custom-call(bf16[128,1024]{1,0:T(8,128)(2,1)} %convolution_convert_fusion.4.x_ref), custom_call_target="tpu_custom_call" | custom-call | tf_op jit(solution)/shard_map/pallas_call | solution.py:131
  25.0 0.0 all-gather.5.cloned.1.call-update
  25.0 0.0 all-gather.7.cloned.1.call-start
  25.1 0.0 copy-done.9
  25.1 1.1 convolution_convert_fusion.3.x_ref
  26.1 11.4 %shard_map.95 = bf16[128,1024]{1,0:T(8,128)(2,1)} custom-call(bf16[128,1024]{1,0:T(8,128)(2,1)} %convolution_convert_fusion.3.x_ref), custom_call_target="tpu_custom_call" | custom-call | tf_op jit(solution)/shard_map/pallas_call | solution.py:131
  37.6 0.0 all-gather.7.cloned.1.call-update
  37.6 0.0 reduce-scatter.2.cloned.1.call-start
  37.7 27.0 %all-gather.5.cloned.1.call-done = bf16[1024,1024]{1,0:T(8,128)(2,1)} async-done(((bf16[128,1024]{1,0:T(8,128)(2,1)}), bf16[1024,1024]{1,0:T(8,128)(2,1)}) %all-gather.5.cloned.1.call-update) | async-done | bytes 2097168 | tf_op jit(solution)/shard_map/all_gather | solution.py:503
  64.6 4.1 %reshape.102 = bf16[256,4,1024]{2,1,0:T(4,128)(2,1)} reshape(bf16[1024,1024]{1,0:T(8,128)(2,1)} %all-gather.5.cloned.1.call-done) | data formatting | bytes 4194304 | tf_op jit(solution)/shard_map/reshape | solution.py:510
  68.7 0.0 copy-done.6
  68.7 4.3 %copy.19 = bf16[256,4,1024]{0,2,1:T(8,128)(2,1)} copy(bf16[256,4,1024]{2,1,0:T(4,128)(2,1)} %reshape.102) | data formatting | bytes 4194304 | tf_op jit(solution)/shard_map/reshape | solution.py:510
  73.0 0.0 copy-done
  73.0 5.3 %fusion.11 = (bf16[256,4,256]{2,0,1:T(8,128)(2,1)S(1)}, f32[4,256,256]{2,1,0:T(8,128)}) fusion(bf16[256,4,1024]{0,2,1:T(8,128)(2,1)} %copy.19, bf16[4,1024,256]{2,1,0:T(8,128)(2,1)S(1)} %copy-done), kind=kOutput, calls=%fused_computation.25 | convolution fusion | flops 553910272 | bytes 5767168 | tf_op jit(solution)/shard_map/rkd,kdf->rkf/dot_general | solution.py:511
  78.3 22.5 %all-gather.7.cloned.1.call-done = bf16[1024,1024]{1,0:T(8,128)(2,1)} async-done(((bf16[128,1024]{1,0:T(8,128)(2,1)}), bf16[1024,1024]{1,0:T(8,128)(2,1)}) %all-gather.7.cloned.1.call-update) | async-done | bytes 2097168 | tf_op jit(solution)/shard_map/all_gather | solution.py:503
  100.8 4.1 %reshape.105 = bf16[256,4,1024]{2,1,0:T(4,128)(2,1)} reshape(bf16[1024,1024]{1,0:T(8,128)(2,1)} %all-gather.7.cloned.1.call-done) | data formatting | bytes 4194304 | tf_op jit(solution)/shard_map/reshape | solution.py:524
  104.9 5.8 %fusion.17 = bf16[256,4,256]{2,0,1:T(8,128)(2,1)S(1)} fusion(bf16[4,256,1024]{2,1,0:T(8,128)(2,1)} %param.8, bf16[256,4,1024]{2,1,0:T(4,128)(2,1)} %reshape.105, f32[4,256,256]{2,1,0:T(8,128)} %get-tuple-element.17), kind=kOutput, calls=%fused_computation.31 | convolution fusion | flops 555745280 | bytes 5767168 | tf_op jit(solution)/shard_map/rkd,kfd->rkf/dot_general | solution.py:525
  110.6 0.0 copy-start.4
  110.7 0.8 copy-done.4
  111.4 0.7 convert_bitcast_fusion
  112.2 2.9 %copy.16 = bf16[256,4,1024]{2,1,0:T(4,128)(2,1)} copy(bf16[256,4,1024]{2,0,1:T(8,128)(2,1)S(1)} %convert_bitcast_fusion) | data formatting | bytes 4194304 | tf_op jit(solution)/shard_map/convert_element_type | solution.py:542
  115.1 4.0 %reshape.106 = bf16[8,128,1024]{2,1,0:T(8,128)(2,1)} reshape(bf16[256,4,1024]{2,1,0:T(4,128)(2,1)} %copy.16) | data formatting | bytes 4194304 | tf_op jit(solution)/shard_map/reshape | solution.py:542
  119.1 0.0 copy-start.1
  119.1 0.0 reduce-scatter.2.cloned.1.call-update
  119.1 1.0 copy-done.1
  120.1 1.0 copy.10
  121.1 2.3 convert_bitcast_fusion.1
  123.4 2.9 %copy.14 = bf16[256,4,1024]{2,1,0:T(4,128)(2,1)} copy(bf16[256,4,1024]{2,0,1:T(8,128)(2,1)S(1)} %convert_bitcast_fusion.1) | data formatting | bytes 4194304 | tf_op jit(solution)/shard_map/convert_element_type | solution.py:520
  126.4 4.0 %reshape.103.x_ref = bf16[8,128,1024]{2,1,0:T(8,128)(2,1)} reshape(bf16[256,4,1024]{2,1,0:T(4,128)(2,1)} %copy.14) | data formatting | bytes 4194304 | tf_op jit(solution)/shard_map/reshape | solution.py:520
  130.4 0.0 copy-start.10
  130.4 33.0 %shard_map.93.x_ref = bf16[128,1024]{1,0:T(8,128)(2,1)} custom-call(bf16[8,128,1024]{2,1,0:T(8,128)(2,1)} %reshape.103.x_ref), custom_call_target="tpu_custom_call" | custom-call | tf_op jit(solution)/shard_map/pallas_call | solution.py:202
  163.4 14.1 %shard_map.94 = bf16[128,1024]{1,0:T(8,128)(2,1)} custom-call(bf16[128,1024]{1,0:T(8,128)(2,1)} %shard_map.93.x_ref), custom_call_target="tpu_custom_call" | custom-call | tf_op jit(solution)/shard_map/pallas_call | solution.py:131
  177.5 0.0 copy-start.3
  177.5 2.3 fusion.7
  179.8 0.0 copy-done.10
  179.8 1.3 multiply_reduce_fusion
  181.1 0.8 subtract_multiply_fusion.comb_ref
  182.0 0.0 copy-done.3
  182.0 0.0 copy-start.2
  182.0 0.0 copy-start.5
  182.0 2.9 %convolution_convert_fusion = bf16[4,256,1024]{2,1,0:T(8,128)(2,1)} fusion(bf16[256,4,256]{2,0,1:T(8,128)(2,1)S(1)} %get-tuple-element.16, bf16[256,4,1024]{2,1,0:T(4,128)(2,1)S(1)} %copy-done.3), kind=kOutput, calls=%fused_computation.2 | convolution fusion | flops 537919488 | bytes 4718592 | tf_op jit(solution)/shard_map/rkf,rkd->kfd/dot_general | solution.py:530
  184.9 0.0 copy-done.2
  184.9 0.0 copy-done.5
  184.9 2.0 convolution_convert_fusion.1
  186.9 0.0 copy-start.7
  186.9 0.0 copy-start.8
  186.9 0.0 reduce-scatter.2.cloned.1.call-done
  186.9 43.3 %shard_map.96 = (bf16[128,1024]{1,0:T(8,128)(2,1)}, bf16[256,128]{1,0:T(8,128)(2,1)}, bf16[32,32,128]{2,1,0:T(8,128)(2,1)}) custom-call(bf16[128,1024]{1,0:T(8,128)(2,1)} %bitcast.131, bf16[256,1024]{1,0:T(8,128)(2,1)} %bitcast.129, bf16[1024,256]{1,0:T(8,128)(2,1)} %bitcast.130, f32[256,128]{1,0:T(8,128)} %copy-done.6, ...), custom_call_target="tpu_custom_call" | custom-call | tf_op jit(solution)/shard_map/pallas_call | solution.py:456
  230.2 0.0 copy-start.11
  230.2 1.8 bitcast_convert_fusion
  232.0 0.0 copy-done.7
  232.0 1.2 fusion.38
  233.3 0.0 copy-done.8
  233.3 0.0 copy-done.11
  233.3 1.1 fusion.8
  (1 shorter events, 0.0 us)
Async XLA Ops:
  7.2 65.8 %copy-start = (bf16[4,1024,256]{2,1,0:T(8,128)(2,1)S(1)}, bf16[4,1024,256]{2,1,0:T(8,128)(2,1)}, u32[]{:S(2)}) copy-start(bf16[4,1024,256]{2,1,0:T(8,128)(2,1)} %param.7) | copy-start | bytes 6291460
  7.2 17.9 %copy-start.9 = (bf16[1,256,1024]{2,1,0:T(8,128)(2,1)S(1)}, bf16[1,256,1024]{2,1,0:T(8,128)(2,1)}, u32[]{:S(2)}) copy-start(bf16[1,256,1024]{2,1,0:T(8,128)(2,1)} %param.9) | copy-start | bytes 1572868
  7.2 57.4 %all-gather.5.cloned.1.call-start = ((), (), s32[]{:S(2)}) async-start(), calls=%async_computation.2 | async-start | bytes 2359296 | tf_op jit(solution)/shard_map/all_gather | solution.py:503
  9.3 59.5 %copy-start.6 = (f32[256,128]{1,0:T(8,128)}, f32[256,128]{1,0:T(8,128)S(1)}, u32[]{:S(2)}) copy-start(f32[256,128]{1,0:T(8,128)S(1)} %fusion.36.prob_ref) | copy-start | bytes 393220
  25.0 75.8 %all-gather.7.cloned.1.call-start = ((), (), s32[]{:S(2)}) async-start(), calls=%async_computation.3 | async-start | bytes 2359296 | tf_op jit(solution)/shard_map/all_gather | solution.py:503
  37.6 149.3 %reduce-scatter.2.cloned.1.call-start = ((), (), s32[]{:S(2)}) async-start(), calls=%async_computation.1 | async-start | bytes 2359296 | tf_op jit(solution)/shard_map/reduce_scatter | solution.py:544
  110.6 0.8 copy-start.4
  119.1 1.0 copy-start.1
  130.4 49.4 %copy-start.10 = (bf16[1,256,1024]{2,1,0:T(8,128)(2,1)S(1)}, bf16[1,256,1024]{2,1,0:T(8,128)(2,1)}, u32[]{:S(2)}) copy-start(bf16[1,256,1024]{2,1,0:T(8,128)(2,1)} %param.9) | copy-start | bytes 1572868
  177.5 4.5 %copy-start.3 = (bf16[256,4,1024]{2,1,0:T(4,128)(2,1)S(1)}, bf16[256,4,1024]{2,1,0:T(4,128)(2,1)}, u32[]{:S(2)}) copy-start(bf16[256,4,1024]{2,1,0:T(4,128)(2,1)} %reshape.105) | copy-start | bytes 6291460
  182.0 2.9 %copy-start.2 = (bf16[256,4,1024]{0,2,1:T(8,128)(2,1)S(1)}, bf16[256,4,1024]{0,2,1:T(8,128)(2,1)}, u32[]{:S(2)}) copy-start(bf16[256,4,1024]{0,2,1:T(8,128)(2,1)} %copy.19) | copy-start | bytes 6291460
  182.0 2.9 %copy-start.5 = (bf16[256,4,256]{2,0,1:T(8,128)(2,1)S(1)}, bf16[256,4,256]{2,0,1:T(8,128)(2,1)}, u32[]{:S(2)}) copy-start(bf16[256,4,256]{2,0,1:T(8,128)(2,1)} %copy-done.4) | copy-start | bytes 1572868
  186.9 45.1 %copy-start.7 = (f32[256,128]{1,0:T(8,128)S(1)}, f32[256,128]{1,0:T(8,128)}, u32[]{:S(2)}) copy-start(f32[256,128]{1,0:T(8,128)} %copy-done.6) | copy-start | bytes 393220
  186.9 46.3 %copy-start.8 = (bf16[1024,128]{1,0:T(8,128)(2,1)S(1)}, bf16[1024,128]{1,0:T(8,128)(2,1)}, u32[]{:S(2)}) copy-start(bf16[1024,128]{1,0:T(8,128)(2,1)} %param.6) | copy-start | bytes 786436
  230.2 3.1 %copy-start.11 = (bf16[256,128]{1,0:T(8,128)(2,1)S(1)}, bf16[256,128]{1,0:T(8,128)(2,1)}, u32[]{:S(2)}) copy-start(bf16[256,128]{1,0:T(8,128)(2,1)} %get-tuple-element.9) | copy-start | bytes 196612
Sparse Core Ops, SparseCore 0:
  25.1 39.4 all-gather.4
  66.5 34.2 all-gather.6
  119.2 61.4 reduce-scatter.1

commit v14 on v13

--- a/solution.py
+++ b/solution.py
@@ -503,8 +503,8 @@
         return lax.all_gather(arrived, "dp", axis=0, tiled=True)
 
     def from_owners(partial_value, cid):
-        summed = relay_sum(partial_value, cid + 8)
-        return row_exchange(summed, n_expert, cid)[None]
+        summed = lax.psum_scatter(partial_value, "dp", scatter_dimension=0, tiled=True)
+        return row_exchange(summed[0], n_expert, cid)[None]
 
     slot_rows = to_owners(slots, 0)
     blocks = slot_rows.reshape(-1, experts_dev, width)
@@ -541,7 +541,7 @@
         grad_second,
         partial_back.astype(jnp.bfloat16).reshape(grad_rows.shape),
     )
-    summed_back = lax.psum_scatter(partial_back, "dp", scatter_dimension=0, tiled=True)[0]
+    summed_back = relay_sum(partial_back, 11)
     mixed = jnp.einsum(
         "ise,ied->isd", combine, expert_outs, preferred_element_type=jnp.float32
     ).astype(jnp.bfloat16)

time: 242 us -> 230 us (0.950)
  waiting for transfers between devices: 49.5 us -> 41.5 us
    all_gather x2, waiting for transfers between devices: 49.4 us -> 39.6 us  [to_owners(): return lax.all_gather(arrived, 'dp', axis=0, tiled=True)]
    pallas_call x1, Pallas kernels: 43.3 us -> 38.7 us  [tail(): pl.pallas_call(functools.partial(_tail_kernel, n_dp, n_ex, summed.shape[0...]
  transfers between devices with their start and end apart: 3 -> 3, of which waited for: 2 -> 3; matrix products, arithmetic and copies ran while one was open for 14% -> 21% of each run, Pallas kernels for 24% -> 20%
where the time goes in v14:
time: 230 us
  Pallas kernels  113 us (49%)
  waiting for transfers between devices  41.5 us (18%)
  matrix products  30 us (13%)
  local copies, waits for them, and re-layouts  28.4 us (12%)
  between operations  13.9 us (6%)
  other arithmetic  2.85 us (1%)
    pallas_call x3, Pallas kernels, row_exchange(): pl.pallas_call(functools.partial(_row_exchange_kernel, n, x.shape[0] // n...  39.7 us
    all_gather x2, waiting for transfers between devices, to_owners(): return lax.all_gather(arrived, 'dp', axis=0, tiled=True)  39.6 us
    pallas_call x1, Pallas kernels, tail(): pl.pallas_call(functools.partial(_tail_kernel, n_dp, n_ex, summed.shape[0...  38.7 us
    pallas_call x1, Pallas kernels, relay_sum(): pl.pallas_call(functools.partial(_relay_sum_kernel, n_chip), out_shape=ja...  34.3 us
    reshape x2, local copies, waits for them, and re-layouts, local(): blocks = slot_rows.reshape(-1, experts_dev, width)  8.36 us
    dot_general x1, matrix products, local(): jnp.einsum('rkd,kfd->rkf', grad_blocks, weight_out, preferred_element_typ...  5.73 us
    dot_general x1, matrix products, local(): jnp.einsum('rkd,kdf->rkf', blocks, weight_in, preferred_element_type=jnp....  5.48 us
    dot_general x1, matrix products, local(): jnp.einsum('rkf,rkd->kfd', hidden, grad_blocks, preferred_element_type=jn...  4.65 us
  transfers between devices with their start and end apart: 3, of which 3 were waited for; matrix products, arithmetic and copies ran while one was open for 21% of the time, Pallas kernels for 20%

profile of v14, /device:TPU:1, one launch (start us, length us, event | category | flops | bytes accessed | tf_op | source)
XLA Modules:
  0.0 229.6 jit_solution(5327191380549165547)
XLA Ops:
  7.2 0.0 copy-start
  7.2 0.0 copy-start.7
  7.2 0.0 all-gather.5.cloned.1.call-start
  7.2 1.7 fusion.48
  8.9 0.1 copy.11
  9.0 0.2 fusion.35
  9.3 0.0 copy-start.4
  9.3 2.0 convolution_convert_fusion.4.x_ref
  11.3 13.7 %shard_map.92 = bf16[128,1024]{1,0:T(8,128)(2,1)} custom-call(bf16[128,1024]{1,0:T(8,128)(2,1)} %convolution_convert_fusion.4.x_ref), custom_call_target="tpu_custom_call" | custom-call | tf_op jit(solution)/shard_map/pallas_call | solution.py:131
  25.0 0.0 all-gather.5.cloned.1.call-update
  25.0 0.0 all-gather.7.cloned.1.call-start
  25.1 0.0 copy-done.7
  25.1 1.1 convolution_convert_fusion.3.x_ref
  26.2 11.4 %shard_map.94 = bf16[128,1024]{1,0:T(8,128)(2,1)} custom-call(bf16[128,1024]{1,0:T(8,128)(2,1)} %convolution_convert_fusion.3.x_ref), custom_call_target="tpu_custom_call" | custom-call | tf_op jit(solution)/shard_map/pallas_call | solution.py:131
  37.6 0.0 all-gather.7.cloned.1.call-update
  37.6 0.0 reduce-scatter.2.cloned.1.call-start
  37.7 25.7 %all-gather.5.cloned.1.call-done = bf16[1024,1024]{1,0:T(8,128)(2,1)} async-done(((bf16[128,1024]{1,0:T(8,128)(2,1)}), bf16[1024,1024]{1,0:T(8,128)(2,1)}) %all-gather.5.cloned.1.call-update) | async-done | bytes 2097168 | tf_op jit(solution)/shard_map/all_gather | solution.py:503
  63.4 4.1 %reshape.102 = bf16[256,4,1024]{2,1,0:T(4,128)(2,1)} reshape(bf16[1024,1024]{1,0:T(8,128)(2,1)} %all-gather.5.cloned.1.call-done) | data formatting | bytes 4194304 | tf_op jit(solution)/shard_map/reshape | solution.py:510
  67.4 0.0 copy-done.4
  67.5 4.3 %copy.19 = bf16[256,4,1024]{0,2,1:T(8,128)(2,1)} copy(bf16[256,4,1024]{2,1,0:T(4,128)(2,1)} %reshape.102) | data formatting | bytes 4194304 | tf_op jit(solution)/shard_map/reshape | solution.py:510
  71.7 0.0 copy-done
  71.7 0.0 copy-start.3
  71.7 5.5 %fusion.11 = (bf16[256,4,256]{2,0,1:T(8,128)(2,1)S(1)}, f32[4,256,256]{2,1,0:T(8,128)}) fusion(bf16[256,4,1024]{0,2,1:T(8,128)(2,1)} %copy.19, bf16[4,1024,256]{2,1,0:T(8,128)(2,1)S(1)} %copy-done), kind=kOutput, calls=%fused_computation.25 | convolution fusion | flops 553910272 | bytes 5767168 | tf_op jit(solution)/shard_map/rkd,kdf->rkf/dot_general | solution.py:511
  77.2 0.0 copy-done.3
  77.2 0.7 convert_bitcast_fusion.1
  77.9 2.9 %copy.14 = bf16[256,4,1024]{2,1,0:T(4,128)(2,1)} copy(bf16[256,4,1024]{2,0,1:T(8,128)(2,1)S(1)} %convert_bitcast_fusion.1) | data formatting | bytes 4194304 | tf_op jit(solution)/shard_map/convert_element_type | solution.py:520
  80.9 4.0 %reshape.103 = bf16[8,128,1024]{2,1,0:T(8,128)(2,1)} reshape(bf16[256,4,1024]{2,1,0:T(4,128)(2,1)} %copy.14) | data formatting | bytes 4194304 | tf_op jit(solution)/shard_map/reshape | solution.py:520
  84.8 0.0 copy-start.1
  84.8 0.0 reduce-scatter.2.cloned.1.call-update
  84.9 1.0 copy-done.1
  85.9 1.0 copy.10
  86.9 13.9 %all-gather.7.cloned.1.call-done = bf16[1024,1024]{1,0:T(8,128)(2,1)} async-done(((bf16[128,1024]{1,0:T(8,128)(2,1)}), bf16[1024,1024]{1,0:T(8,128)(2,1)}) %all-gather.7.cloned.1.call-update) | async-done | bytes 2097168 | tf_op jit(solution)/shard_map/all_gather | solution.py:503
  100.8 4.1 %reshape.105 = bf16[256,4,1024]{2,1,0:T(4,128)(2,1)} reshape(bf16[1024,1024]{1,0:T(8,128)(2,1)} %all-gather.7.cloned.1.call-done) | data formatting | bytes 4194304 | tf_op jit(solution)/shard_map/reshape | solution.py:524
  104.9 5.7 %fusion.17 = bf16[256,4,256]{2,0,1:T(8,128)(2,1)S(1)} fusion(bf16[4,256,1024]{2,1,0:T(8,128)(2,1)} %param.8, bf16[256,4,1024]{2,1,0:T(4,128)(2,1)} %reshape.105, f32[4,256,256]{2,1,0:T(8,128)} %get-tuple-element.17), kind=kOutput, calls=%fused_computation.31 | convolution fusion | flops 555745280 | bytes 5767168 | tf_op jit(solution)/shard_map/rkd,kfd->rkf/dot_general | solution.py:525
  110.7 0.7 convert_bitcast_fusion
  111.4 2.9 %copy.16 = bf16[256,4,1024]{2,1,0:T(4,128)(2,1)} copy(bf16[256,4,1024]{2,0,1:T(8,128)(2,1)S(1)} %convert_bitcast_fusion) | data formatting | bytes 4194304 | tf_op jit(solution)/shard_map/convert_element_type | solution.py:542
  114.4 4.0 %reshape.106.x_ref = bf16[8,128,1024]{2,1,0:T(8,128)(2,1)} reshape(bf16[256,4,1024]{2,1,0:T(4,128)(2,1)} %copy.16) | data formatting | bytes 4194304 | tf_op jit(solution)/shard_map/reshape | solution.py:542
  118.3 34.3 %shard_map.95.summed_ref = bf16[128,1024]{1,0:T(8,128)(2,1)} custom-call(bf16[8,128,1024]{2,1,0:T(8,128)(2,1)} %reshape.106.x_ref), custom_call_target="tpu_custom_call" | custom-call | tf_op jit(solution)/shard_map/pallas_call | solution.py:202
  152.6 0.0 copy-start.2
  152.6 4.6 %convolution_convert_fusion = bf16[4,256,1024]{2,1,0:T(8,128)(2,1)} fusion(bf16[256,4,256]{2,0,1:T(8,128)(2,1)S(1)} %get-tuple-element.16, bf16[256,4,1024]{2,1,0:T(4,128)(2,1)} %reshape.105), kind=kOutput, calls=%fused_computation.2 | convolution fusion | flops 537919488 | bytes 4718592 | tf_op jit(solution)/shard_map/rkf,rkd->kfd/dot_general | solution.py:530
  157.3 0.0 copy-done.2
  157.3 0.0 copy-start.8
  157.3 2.0 convolution_convert_fusion.1
  159.3 1.8 reduce-scatter.2.cloned.1.call-done
  161.2 14.7 %shard_map.93 = bf16[128,1024]{1,0:T(8,128)(2,1)} custom-call(bf16[128,1024]{1,0:T(8,128)(2,1)} %bitcast.131), custom_call_target="tpu_custom_call" | custom-call | tf_op jit(solution)/shard_map/pallas_call | solution.py:131
  175.8 0.0 copy-done.8
  175.8 1.3 multiply_reduce_fusion
  177.2 0.0 copy-start.5
  177.2 2.1 fusion.7
  179.3 0.0 copy-start.6
  179.3 0.8 subtract_multiply_fusion.comb_ref
  180.1 38.7 %shard_map.96 = (bf16[128,1024]{1,0:T(8,128)(2,1)}, bf16[256,128]{1,0:T(8,128)(2,1)}, bf16[32,32,128]{2,1,0:T(8,128)(2,1)}) custom-call(bf16[128,1024]{1,0:T(8,128)(2,1)} %shard_map.95.summed_ref, bf16[256,1024]{1,0:T(8,128)(2,1)} %bitcast.129, bf16[1024,256]{1,0:T(8,128)(2,1)} %bitcast.130, f32[256,128]{1,0:T(8,128)} %copy-done.4, ...), custom_call_target="tpu_custom_call" | custom-call | tf_op jit(solution)/shard_map/pallas_call | solution.py:456
  218.9 0.0 copy-start.9
  218.9 1.8 bitcast_convert_fusion
  220.7 0.0 copy-done.5
  220.7 1.2 fusion.38
  221.9 0.0 copy-done.6
  222.0 0.0 copy-done.9
  222.0 1.1 fusion.8
  (1 shorter events, 0.0 us)
Async XLA Ops:
  7.2 64.6 %copy-start = (bf16[4,1024,256]{2,1,0:T(8,128)(2,1)S(1)}, bf16[4,1024,256]{2,1,0:T(8,128)(2,1)}, u32[]{:S(2)}) copy-start(bf16[4,1024,256]{2,1,0:T(8,128)(2,1)} %param.7) | copy-start | bytes 6291460
  7.2 17.9 %copy-start.7 = (bf16[1,256,1024]{2,1,0:T(8,128)(2,1)S(1)}, bf16[1,256,1024]{2,1,0:T(8,128)(2,1)}, u32[]{:S(2)}) copy-start(bf16[1,256,1024]{2,1,0:T(8,128)(2,1)} %param.9) | copy-start | bytes 1572868
  7.2 56.2 %all-gather.5.cloned.1.call-start = ((), (), s32[]{:S(2)}) async-start(), calls=%async_computation.2 | async-start | bytes 2359296 | tf_op jit(solution)/shard_map/all_gather | solution.py:503
  9.3 58.2 %copy-start.4 = (f32[256,128]{1,0:T(8,128)}, f32[256,128]{1,0:T(8,128)S(1)}, u32[]{:S(2)}) copy-start(f32[256,128]{1,0:T(8,128)S(1)} %fusion.36.prob_ref) | copy-start | bytes 393220
  25.0 75.8 %all-gather.7.cloned.1.call-start = ((), (), s32[]{:S(2)}) async-start(), calls=%async_computation.3 | async-start | bytes 2359296 | tf_op jit(solution)/shard_map/all_gather | solution.py:503
  37.6 123.5 %reduce-scatter.2.cloned.1.call-start = ((), (), s32[]{:S(2)}) async-start(), calls=%async_computation.1 | async-start | bytes 2359296 | tf_op jit(solution)/shard_map/reduce_scatter | solution.py:506
  71.7 5.5 %copy-start.3 = (bf16[4,256,1024]{2,1,0:T(8,128)(2,1)S(1)}, bf16[4,256,1024]{2,1,0:T(8,128)(2,1)}, u32[]{:S(2)}) copy-start(bf16[4,256,1024]{2,1,0:T(8,128)(2,1)} %param.8) | copy-start | bytes 6291460
  84.8 1.0 copy-start.1
  152.6 4.7 %copy-start.2 = (bf16[256,4,1024]{0,2,1:T(8,128)(2,1)S(1)}, bf16[256,4,1024]{0,2,1:T(8,128)(2,1)}, u32[]{:S(2)}) copy-start(bf16[256,4,1024]{0,2,1:T(8,128)(2,1)} %copy.19) | copy-start | bytes 6291460
  157.3 18.5 %copy-start.8 = (bf16[1,256,1024]{2,1,0:T(8,128)(2,1)S(1)}, bf16[1,256,1024]{2,1,0:T(8,128)(2,1)}, u32[]{:S(2)}) copy-start(bf16[1,256,1024]{2,1,0:T(8,128)(2,1)} %param.9) | copy-start | bytes 1572868
  177.2 43.5 %copy-start.5 = (f32[256,128]{1,0:T(8,128)S(1)}, f32[256,128]{1,0:T(8,128)}, u32[]{:S(2)}) copy-start(f32[256,128]{1,0:T(8,128)} %copy-done.4) | copy-start | bytes 393220
  179.3 42.6 %copy-start.6 = (bf16[1024,128]{1,0:T(8,128)(2,1)S(1)}, bf16[1024,128]{1,0:T(8,128)(2,1)}, u32[]{:S(2)}) copy-start(bf16[1024,128]{1,0:T(8,128)(2,1)} %param.6) | copy-start | bytes 786436
  218.9 3.1 %copy-start.9 = (bf16[256,128]{1,0:T(8,128)(2,1)S(1)}, bf16[256,128]{1,0:T(8,128)(2,1)}, u32[]{:S(2)}) copy-start(bf16[256,128]{1,0:T(8,128)(2,1)} %get-tuple-element.9) | copy-start | bytes 196612
Sparse Core Ops, SparseCore 0:
  25.1 38.1 all-gather.4
  65.2 35.5 all-gather.6
  103.4 57.7 reduce-scatter.1
